TPU v7x, 256 devices: a whole 4x4x8 slice. The times are simulated.
256 devices in a mesh: lat: 8 (over x_hi, y), lon: 16 (over z, core), freq: 2 (over x_lo).
Axes of the slice: x: 4 (x_hi: 2, x_lo: 2; x = x_hi * 2 + x_lo), y: 4, z: 8, core: 2. Of those that a mesh axis runs over, the one named last changes fastest.
Arguments:
- spectrum: float32 [36, 36, 32, 2048], P('freq', None, 'lat', 'lon'), may hold values from 0.05 to 1
- group_speed: float32 [36], P('freq'), may hold values from 0.15 to 0.6
- sea_mask: int32 [32, 2048], P('lat', 'lon'), may hold values 0 or 1
- wind_growth: float32 [32, 2048], P('lat', 'lon'), may hold values from 0.2 to 2
- dissipation: float32 [32, 2048], P('lat', 'lon'), may hold values from 0.1 to 1
- wind_profile: float32 [1296], replicated, may hold values from 0.02 to 0.2
- nonlinear_coef: float32 [1296], replicated, may hold values from 0.05 to 0.5
- momentum: float32 [2, 1296], replicated, may hold values from -6 to 6
- quadruplet: int32 [2, 1296], replicated, may hold values from 0 to 1295, as said below
- ocean_cell: int32 [32, 2048], P('lat', 'lon'), may hold values from 0 to 65535, as said below
Outputs:
- spectrum_out: float32 [36, 36, 32, 2048], P('freq', None, 'lat', 'lon')
- ocean_stress: float32 [65536, 2], P(('lon', 'freq'))
Inputs may be any that keep to these rules, and one draw needn't show every extreme that they name: quadruplet[0, b] names a bin 1 or 2 frequencies higher (at most the highest) and 1 to 6 directions further, cyclically; quadruplet[1, b] one 1 or 2 frequencies lower (at least the lowest) and 1 to 6 directions back. ocean_cell[i, j] = j * 32 + i2 with i2 within 1 of i.
All inputs are finite; a program needn't handle non-finite values. No bound on the sum of `sea_mask` on one device may be relied on, other than what follows from the above.
Results may differ from a plain program's by a relative error of at most 0.000094.
Values sent between devices are 32-bit elements; how exact they have to be, the bound alone decides.
No kernel may reach another device: no remote copies, remote signals or barrier semaphores. Data moves between devices by JAX's collectives and lax.ppermute only.
A program may use at most 64 MiB of HBM per device.

v0:
```python
import jax
import jax.numpy as jnp
from jax import lax
from jax.sharding import PartitionSpec as P

time_step = 0.5


def padded(shard, sides, width, wrap):
    for axis, dim in sides:
        size, length = (lax.axis_size(axis), shard.shape[dim])
        up = [(i, (i + 1) % size) for i in range(size if wrap else size - 1)]
        down = [(j, i) for i, j in up]
        last = lax.slice_in_dim(shard, length - width, length, axis=dim)
        leading = lax.slice_in_dim(shard, 0, width, axis=dim)
        before = lax.ppermute(last, axis, up)
        after = lax.ppermute(leading, axis, down)
        shard = jnp.concatenate([before, shard, after], axis=dim)
    return shard


def split_up(shard, dim, length):
    before, after = (shard.shape[:dim], shard.shape[dim + 1 :])
    return jnp.moveaxis(shard.reshape(*before, length, -1, *after), dim, 0)


def sum_at_owner(shard, axis, dim):
    length = lax.axis_size(axis)
    parts = lax.all_to_all(split_up(shard, dim, length), axis, 0, 0, tiled=True)
    return jnp.sum(parts, axis=0)


def copy_for_each(shard, axis):
    copies = jnp.broadcast_to(shard, (lax.axis_size(axis), *shard.shape))
    return lax.all_to_all(copies, axis, split_axis=0, concat_axis=0, tiled=True)


def over_copies(shard, axis):
    everything = copy_for_each(shard, axis)
    return jnp.sum(everything, axis=0)


def source_update(
    flat_bins, partners, coef_rows, profile_rows, energy, wind_flat, dissip_flat, mask_flat
):
    third = jnp.take(flat_bins, partners[0], axis=0)
    fourth = jnp.take(flat_bins, partners[1], axis=0)
    transfer = coef_rows[:, None] * (
        flat_bins * flat_bins * (third + fourth) - 2.0 * flat_bins * third * fourth
    )
    scattered = jnp.zeros_like(transfer).at[partners[0]].add(transfer).at[partners[1]].add(transfer)
    tendency = (
        wind_flat[None, :] * profile_rows[:, None] * flat_bins
        + scattered
        - 2.0 * transfer
        - dissip_flat[None, :] * energy[None, :] * flat_bins
    )
    return mask_flat[None, :] * (flat_bins + time_step * tendency)


def local(
    spectrum,
    group_speed,
    sea_mask,
    wind_growth,
    dissipation,
    wind_profile,
    nonlinear_coef,
    momentum,
    quadruplet,
    ocean_cell,
):
    highest = lax.Precision.HIGHEST
    band_freqs, ndirs, lat_rows, lon_cols = spectrum.shape
    nbins = wind_profile.shape[0]
    mask_float = sea_mask.astype(jnp.float32)
    angles = 2.0 * jnp.pi * jnp.arange(ndirs).astype(jnp.float32) / ndirs
    speed_x = (group_speed[:, None] * jnp.cos(angles)[None, :])[:, :, None, None]
    speed_y = (group_speed[:, None] * jnp.sin(angles)[None, :])[:, :, None, None]
    lat_ext = padded(spectrum, (("lat", 2),), 1, False)
    lon_ext = padded(spectrum, (("lon", 3),), 1, True)
    moved = (
        spectrum
        - jnp.maximum(speed_x, 0.0) * (spectrum - lon_ext[..., :-2])
        - jnp.minimum(speed_x, 0.0) * (lon_ext[..., 2:] - spectrum)
        - jnp.maximum(speed_y, 0.0) * (spectrum - lat_ext[:, :, :-2, :])
        - jnp.minimum(speed_y, 0.0) * (lat_ext[:, :, 2:, :] - spectrum)
    )
    moved = moved * mask_float[None, None]
    band_index = lax.axis_index("freq")
    band_bins = band_freqs * ndirs
    weights = momentum * wind_profile[None, :]
    band_weights = lax.dynamic_slice_in_dim(weights, band_index * band_bins, band_bins, 1)
    stress = (
        jnp.dot(band_weights, moved.reshape(band_bins, -1), precision=highest)
        * wind_growth.reshape(-1)[None, :]
    )
    cell_flat = ocean_cell.reshape(-1)
    all_rows = lax.axis_size("lat") * lat_rows
    share_cells = all_rows * lon_cols // lax.axis_size("freq")
    stress_cols = stress.T
    first_cell = lax.axis_index("lon") * (lon_cols * all_rows)

    def one_block(offset):
        cell_ids = first_cell + offset + jnp.arange(share_cells, dtype=jnp.int32)
        block_match = (cell_ids[:, None] == cell_flat[None, :]).astype(jnp.float32)
        return jnp.dot(block_match, stress_cols, precision=highest)

    offsets = (
        jnp.arange(share_cells * lax.axis_size("freq") // share_cells, dtype=jnp.int32)
        * share_cells
    )
    band_part = sum_at_owner(
        lax.map(one_block, offsets).reshape(share_cells * lax.axis_size("freq"), 2), "freq", 0
    )
    ocean_stress = over_copies(band_part, "lat")
    margin = min(4, band_freqs)
    extended = padded(moved, (("freq", 0),), margin, False)
    ext_freqs = band_freqs + 2 * margin
    ext_bins = ext_freqs * ndirs
    first_freq = band_index * band_freqs - margin
    local_bins = jnp.arange(ext_bins, dtype=jnp.int32)
    global_bins = jnp.clip(first_freq * ndirs + local_bins, 0, nbins - 1)
    partners = jnp.clip(
        jnp.take(quadruplet, global_bins, axis=1) - first_freq * ndirs, 0, ext_bins - 1
    )
    coef_rows = jnp.take(nonlinear_coef, global_bins)
    profile_rows = jnp.take(wind_profile, global_bins)
    band_sum = jnp.sum(moved.reshape(band_bins, -1), axis=0)
    energy = over_copies(band_sum, "freq") / nbins
    result = source_update(
        extended.reshape(ext_bins, -1),
        partners,
        coef_rows,
        profile_rows,
        energy,
        wind_growth.reshape(-1),
        dissipation.reshape(-1),
        mask_float.reshape(-1),
    )
    spectrum_out = result[margin * ndirs : (margin + band_freqs) * ndirs].reshape(moved.shape)
    return (spectrum_out, ocean_stress)


def solution(mesh):
    return jax.shard_map(
        local,
        mesh=mesh,
        in_specs=(
            P("freq", None, "lat", "lon"),
            P("freq"),
            P("lat", "lon"),
            P("lat", "lon"),
            P("lat", "lon"),
            P(),
            P(),
            P(),
            P(),
            P("lat", "lon"),
        ),
        out_specs=(P("freq", None, "lat", "lon"), P(("lon", "freq"), None)),
        check_vma=False,
    )
```

profile of v0, /device:TPU:8, one launch (start us, length us, event | category | flops | bytes accessed | tf_op | source)
XLA Modules:
  0.0 131.9 jit_solution(9330994302664790768)
XLA Ops:
  0.6 0.0 copy-start
  0.7 2.4 %fusion.41 = (f32[18,36,1,128]{3,2,1,0:T(1,128)S(1)}, f32[18,36,1,128]{3,2,1,0:T(1,128)S(1)}) fusion(f32[18,36,4,128]{3,2,1,0:T(4,128)} %param.16), kind=kLoop, calls=%fused_computation.79 | loop fusion | bytes 1327104 | tf_op jit(solution)/shard_map/slice | solution.py:14
  3.1 4.1 %collective-permute-start.3 = (f32[18,36,1,128]{3,1,2,0:T(8,128)S(1)}, f32[18,36,1,128]{3,1,2,0:T(8,128)S(1)}, u32[]{:S(2)}, u32[]{:S(2)}) collective-permute-start(f32[18,36,1,128]{3,1,2,0:T(8,128)S(1)} %copy.47), channel_id=1, source_target_pairs={{32,0},{64,32},{96,64},{128,96},{160,128},{192,160},{224,192},{33,... | collective-permute-start | bytes 995336 | tf_op jit(solution)/shard_map/ppermute | solution.py:17
  7.2 0.8 copy.46
  8.0 1.9 %collective-permute-start.2 = (f32[18,36,1,128]{3,1,2,0:T(8,128)}, f32[18,36,1,128]{3,1,2,0:T(8,128)}, u32[]{:S(2)}, u32[]{:S(2)}) collective-permute-start(f32[18,36,1,128]{3,1,2,0:T(8,128)} %copy.46), channel_id=1, source_target_pairs={{0,32},{32,64},{64,96},{96,128},{128,160},{160,192},{192,224},{1,3... | collective-permute-start | bytes 995336 | tf_op jit(solution)/shard_map/ppermute | solution.py:16
  9.9 1.8 %fusion.40 = (f32[18,36,4,1]{3,2,1,0:T(4,128)S(1)}, f32[18,36,4,1]{3,2,1,0:T(4,128)}) fusion(f32[18,36,4,128]{3,2,1,0:T(4,128)S(1)} %copy-done.3), kind=kLoop, calls=%fused_computation.78 | loop fusion | bytes 41472 | tf_op jit(solution)/shard_map/slice | solution.py:14
  11.7 1.9 %copy.45 = f32[18,36,4,1]{1,2,3,0:T(4,128)S(1)} copy(f32[18,36,4,1]{3,2,1,0:T(4,128)} %get-tuple-element.58) | data formatting | bytes 20736
  13.7 4.6 %collective-permute-start.1 = (f32[18,36,4,1]{1,2,3,0:T(4,128)S(1)}, f32[18,36,4,1]{1,2,3,0:T(4,128)S(1)}, u32[]{:S(2)}, u32[]{:S(2)}) collective-permute-start(f32[18,36,4,1]{1,2,3,0:T(4,128)S(1)} %copy.45), channel_id=1, source_target_pairs={{2,0},{4,2},{6,4},{8,6},{10,8},{12,10},{14,12},{16,14},{18,16},{20... | collective-permute-start | bytes 31112 | tf_op jit(solution)/shard_map/ppermute | solution.py:17
  18.2 1.2 copy.44
  19.5 0.0 collective-permute-start
  19.6 0.3 copy.41
  19.9 2.9 %gather_fusion = s32[936,2]{1,0:T(8,128)S(1)} fusion(s32[2,1296]{0,1:T(8,128)S(1)} %copy.41, s32[1024]{0:T(1024)S(1)} %pad_clamp_fusion.2), kind=kCustom, calls=%fused_computation.4 | custom fusion | bytes 18720 | tf_op jit(solution)/shard_map/jit(_take)/gather | solution.py:125
  22.7 0.2 clamp_bitcast_fusion
  22.9 0.5 slice_reduce_fusion
  23.4 0.6 compare_and_fusion
  24.1 0.0 copy-start.1
  24.1 5.9 %gather_fusion.2 = f32[936]{0:T(1024)S(1)} fusion(f32[1296]{0:T(1024)S(1)} %copy-done, s32[1024]{0:T(1024)S(1)} %pad_clamp_fusion.3), kind=kCustom, calls=%fused_computation.2.clone | custom fusion | bytes 11232 | tf_op jit(solution)/shard_map/jit(_take)/gather | solution.py:127
  29.9 0.0 copy-start.13
  30.0 0.0 copy-start.11
  30.0 5.9 %gather_fusion.1 = f32[936]{0:T(1024)S(1)} fusion(f32[1296]{0:T(1024)S(1)} %copy-done.1, s32[1024]{0:T(1024)S(1)} %pad_clamp_fusion.3), kind=kCustom, calls=%fused_computation.clone | custom fusion | bytes 11232 | tf_op jit(solution)/shard_map/jit(_take)/gather | solution.py:128
  35.9 0.1 multiply_maximum_fusion.1
  36.0 0.6 convert_bitcast_fusion
  36.6 0.6 iota_multiply_fusion
  37.2 0.1 dynamic-slice
  37.2 0.0 collective-permute-done
  37.2 1.7 %copy.34 = f32[18,36,4,1]{3,2,1,0:T(4,128)} copy(f32[18,36,4,1]{1,2,3,0:T(4,128)S(1)} %collective-permute-done) | data formatting | bytes 20736 | tf_op jit(solution)/shard_map/ppermute | solution.py:16
  39.0 0.0 collective-permute-done.1
  39.0 1.7 %copy.36 = f32[18,36,4,1]{3,2,1,0:T(4,128)} copy(f32[18,36,4,1]{1,2,3,0:T(4,128)S(1)} %collective-permute-done.1) | data formatting | bytes 20736 | tf_op jit(solution)/shard_map/ppermute | solution.py:17
  40.7 0.3 copy.40
  41.0 0.0 collective-permute-done.2
  41.0 1.4 %copy.38 = f32[18,36,1,128]{3,2,1,0:T(1,128)S(1)} copy(f32[18,36,1,128]{3,1,2,0:T(8,128)} %collective-permute-done.2) | data formatting | bytes 663552 | tf_op jit(solution)/shard_map/ppermute | solution.py:16
  42.4 0.0 copy-start.6
  42.4 0.0 copy-start.10
  42.4 7.3 %fusion.37 = (f32[4,128]{1,0:T(4,128)S(1)}, f32[18,36,4,128]{3,2,1,0:T(4,128)S(1)}) fusion(f32[4,128]{1,0:T(4,128)S(1)} %get-tuple-element.62, f32[18,36,4,128]{3,2,1,0:T(4,128)S(1)} %copy-done.3, f32[18,36,1,128]{3,2,1,0:T(1,128)S(1)} %copy.40, f32[18,36]{1,0:T(8,128)S(1)} %get-tuple-element.67, f32[18,36,1,128]{3,2,1,0:T(1,128)S(1)} %copy.38, ...), kind=kLoop, calls=%fused_computation.76 | loop fusion | flops 5971456 | bytes 3352960 | tf_op jit(solution)/shard_map/reduce_sum | solution.py:129
  49.7 0.0 copy-start.14
  49.8 0.8 fusion.30
  50.6 0.0 copy-done.15
  50.6 7.9 %while.10 = (s32[]{:T(128)}, f32[2,2048,2]{1,2,0:T(2,128)}, s32[2]{0:T(128)S(1)}, s32[]{:T(128)}, s32[4,128]{1,0:T(4,128)S(1)}, /*index=5*/f32[512,2]{0,1:T(2,128)S(1)}, s32[]{:T(128)}) while((s32[]{:T(128)}, f32[2,2048,2]{1,2,0:T(2,128)}, s32[2]{0:T(128)S(1)}, s32[]{:T(128)}, s32[4,128]{1,0:T(4,128)S(1)}, /*index=5*/f32[512,2]{0,1:T(2,128)S(1)}, ...), condition=%wide.region_5.8_spmd, body=%wide.region_4.7_spmd.sunk | while | flops 26216452 | bytes 39029 | solution.py:114
  50.6 0.6 dynamic_slice.12
  51.8 2.7 %fusion.48 = f32[2,2048,2]{1,2,0:T(2,128)} fusion(f32[2,2048,2]{1,2,0:T(2,128)} %get-tuple-element.122, s32[]{:T(128)S(6)} %copy.67, f32[512,2]{0,1:T(2,128)S(1)} %get-tuple-element.133, s32[512]{0:T(512)S(1)} %bitcast.58, s32[2048]{0:T(1024)S(1)} %iota_add_fusion.2), kind=kOutput, calls=%fused_computation.10.clone.1 | convolution fusion | flops 26214400 | bytes 30724 | tf_op jit(solution)/shard_map/while/body/eval_jaxpr/dot_general | solution.py:107
  54.6 0.6 dynamic_slice.12
  55.8 2.7 %fusion.48 = f32[2,2048,2]{1,2,0:T(2,128)} fusion(f32[2,2048,2]{1,2,0:T(2,128)} %get-tuple-element.122, s32[]{:T(128)S(6)} %copy.67, f32[512,2]{0,1:T(2,128)S(1)} %get-tuple-element.133, s32[512]{0:T(512)S(1)} %bitcast.58, s32[2048]{0:T(1024)S(1)} %iota_add_fusion.2), kind=kOutput, calls=%fused_computation.10.clone.1 | convolution fusion | flops 26214400 | bytes 30724 | tf_op jit(solution)/shard_map/while/body/eval_jaxpr/dot_general | solution.py:107
  58.5 0.6 broadcast_in_dim.58
  59.1 3.2 %all-to-all-start = ((f32[2,1,512]{2,1,0:T(1,128)}), f32[2,1,512]{2,1,0:T(1,128)S(1)}, u32[]{:S(2)}, u32[]{:S(2)}) async-start(f32[2,1,512]{2,1,0:T(1,128)} %broadcast_in_dim.58), calls=%async_computation | async-start | bytes 8192 | tf_op jit(solution)/shard_map/all_to_all | solution.py:35
  62.4 3.9 %collective-permute-start.4 = (f32[4,36,4,128]{3,2,1,0:T(4,128)S(1)}, f32[4,36,4,128]{3,2,1,0:T(4,128)S(1)}, u32[]{:S(2)}, u32[]{:S(2)}) collective-permute-start(f32[4,36,4,128]{3,2,1,0:T(4,128)S(1)} %get-tuple-element.55), channel_id=1, source_target_pairs={{0,1},{2,3},{4,5},{6,7},{8,9},{10,11},{12,13},{14,15},{16,17},{18,... | collective-permute-start | bytes 884744 | tf_op jit(solution)/shard_map/ppermute | solution.py:16
  66.3 1.3 collective-permute-start.5
  67.6 0.0 all-to-all-done
  67.6 3.9 %all-to-all-start.1 = ((f32[2,2048,2]{1,2,0:T(2,128)}), f32[2,2048,2]{1,2,0:T(2,128)S(1)}, u32[]{:S(2)}, u32[]{:S(2)}) async-start(f32[2,2048,2]{1,2,0:T(2,128)} %get-tuple-element.36), calls=%async_computation.1 | async-start | bytes 65536 | tf_op jit(solution)/shard_map/all_to_all | solution.py:29
  71.6 3.9 %all-to-all-done.1 = f32[2,2048,2]{1,2,0:T(2,128)S(1)} async-done(((f32[2,2048,2]{1,2,0:T(2,128)}), f32[2,2048,2]{1,2,0:T(2,128)S(1)}, u32[]{:S(2)}, u32[]{:S(2)}) %all-to-all-start.1) | async-done | bytes 32800 | tf_op jit(solution)/shard_map/all_to_all | solution.py:29
  75.5 0.7 broadcast_in_dim.60
  76.2 8.3 %all-to-all-start.2 = ((f32[8,2048,2]{1,2,0:T(2,128)}), f32[8,2048,2]{1,2,0:T(2,128)S(1)}, u32[]{:S(2)}, u32[]{:S(2)}) async-start(f32[8,2048,2]{1,2,0:T(2,128)} %broadcast_in_dim.60), calls=%async_computation.2 | async-start | bytes 262144 | tf_op jit(solution)/shard_map/all_to_all | solution.py:35
  84.6 6.6 %all-to-all-done.2 = f32[8,2048,2]{1,2,0:T(2,128)S(1)} async-done(((f32[8,2048,2]{1,2,0:T(2,128)}), f32[8,2048,2]{1,2,0:T(2,128)S(1)}, u32[]{:S(2)}, u32[]{:S(2)}) %all-to-all-start.2) | async-done | bytes 131104 | tf_op jit(solution)/shard_map/all_to_all | solution.py:35
  91.2 0.7 reduce_sum.39
  91.8 0.0 collective-permute-done.4
  91.8 0.4 pad_maximum_fusion
  92.2 0.2 copy.61
  92.4 1.1 copy-done.2
  93.5 4.8 %gather_fusion.3 = f32[936,512]{1,0:T(8,128)} fusion(f32[936,512]{1,0:T(8,128)S(1)} %bitcast.44, s32[1024]{0:T(1024)S(1)} %pad_clamp_fusion.1), kind=kCustom, calls=%fused_computation.1.clone | custom fusion | bytes 3837600 | tf_op jit(solution)/shard_map/jit(_take)/gather | solution.py:46
  98.3 4.8 %gather_fusion.4 = f32[936,512]{1,0:T(8,128)} fusion(f32[936,512]{1,0:T(8,128)S(1)} %bitcast.45, s32[1024]{0:T(1024)S(1)} %pad_clamp_fusion), kind=kCustom, calls=%fused_computation.3.clone | custom fusion | bytes 3837600 | tf_op jit(solution)/shard_map/jit(_take)/gather | solution.py:47
  103.1 4.7 %subtract_multiply_fusion = (f32[936,512]{1,0:T(8,128)}, f32[936,512]{1,0:T(8,128)}) fusion(f32[936,512]{1,0:T(8,128)} %gather_fusion.4, f32[936,512]{1,0:T(8,128)} %gather_fusion.3, f32[936]{0:T(1024)S(1)} %get-tuple-element.71, pred[936]{0:T(1024)(128)(4,1)S(1)} %copy-done.8, pred[936]{0:T(1024)(128)(4,1)S(1)} %copy-done.9, ...), kind=kLoop, calls=%fused_computation.16 | loop fusion | flops 5750784 | bytes 9596048 | tf_op jit(solution)/shard_map/mul | solution.py:48
  107.8 10.2 %scatter_fusion = f32[936,512]{1,0:T(8,128)} fusion(f32[936,512]{1,0:T(8,128)} %get-tuple-element.54, s32[936]{0:T(1024)S(1)} %bitcast.54, f32[936,512]{1,0:T(8,128)} %get-tuple-element.53), kind=kCustom, calls=%fused_computation.5 | custom fusion | flops 479232 | bytes 5754528 | tf_op jit(solution)/shard_map/scatter-add | solution.py:51
  118.0 10.2 %scatter_fusion.1 = f32[936,512]{1,0:T(8,128)} fusion(f32[936,512]{1,0:T(8,128)} %scatter_fusion, s32[936]{0:T(1024)S(1)} %bitcast.53, f32[936,512]{1,0:T(8,128)} %get-tuple-element.53), kind=kCustom, calls=%fused_computation.6 | custom fusion | flops 479232 | bytes 5754528 | tf_op jit(solution)/shard_map/scatter-add | solution.py:51
  128.1 2.2 %fusion.16 = f32[648,512]{1,0:T(8,128)S(1)} fusion(f32[936,512]{1,0:T(8,128)} %scatter_fusion.1, f32[936,512]{1,0:T(8,128)} %get-tuple-element.53, f32[936,512]{1,0:T(8,128)S(1)} %bitcast.46, f32[512]{0:T(512)S(1)} %copy-done.7, f32[512]{0:T(512)S(1)} %bitcast_multiply_fusion), kind=kLoop, calls=%fused_computation.25 | loop fusion | flops 2322432 | bytes 5312512 | tf_op jit(solution)/shard_map/mul | solution.py:58
  130.4 1.5 %reshape.255 = f32[18,36,4,128]{3,2,1,0:T(4,128)} reshape(f32[648,512]{1,0:T(8,128)S(1)} %fusion.16) | data formatting | bytes 2654208 | tf_op jit(solution)/shard_map/reshape | solution.py:141
  (45 shorter events, 0.3 us)
Async XLA Ops:
  0.6 23.4 %copy-start = (f32[1296]{0:T(1024)S(1)}, f32[1296]{0:T(1024)}, u32[]{:S(2)}) copy-start(f32[1296]{0:T(1024)} %param.22) | copy-start | bytes 15556
  0.6 9.3 %copy-start.3 = (f32[18,36,4,128]{3,2,1,0:T(4,128)S(1)}, f32[18,36,4,128]{3,2,1,0:T(4,128)}, u32[]{:S(2)}) copy-start(f32[18,36,4,128]{3,2,1,0:T(4,128)} %param.16) | copy-start | bytes 3981316
  3.1 37.5 %collective-permute-start.3 = (f32[18,36,1,128]{3,1,2,0:T(8,128)S(1)}, f32[18,36,1,128]{3,1,2,0:T(8,128)S(1)}, u32[]{:S(2)}, u32[]{:S(2)}) collective-permute-start(f32[18,36,1,128]{3,1,2,0:T(8,128)S(1)} %copy.47), channel_id=1, source_target_pairs={{32,0},{64,32},{96,64},{128,96},{160,128},{192,160},{224,192},{33,... | collective-permute-start | bytes 995336 | tf_op jit(solution)/shard_map/ppermute | solution.py:17
  8.0 33.0 %collective-permute-start.2 = (f32[18,36,1,128]{3,1,2,0:T(8,128)}, f32[18,36,1,128]{3,1,2,0:T(8,128)}, u32[]{:S(2)}, u32[]{:S(2)}) collective-permute-start(f32[18,36,1,128]{3,1,2,0:T(8,128)} %copy.46), channel_id=1, source_target_pairs={{0,32},{32,64},{64,96},{96,128},{128,160},{160,192},{192,224},{1,3... | collective-permute-start | bytes 995336 | tf_op jit(solution)/shard_map/ppermute | solution.py:16
  11.7 7.9 %copy-start.5 = (s32[2,1296]{1,0:T(2,128)S(1)}, s32[2,1296]{1,0:T(2,128)}, u32[]{:S(2)}) copy-start(s32[2,1296]{1,0:T(2,128)} %param.24) | copy-start | bytes 31108
  13.7 25.3 %collective-permute-start.1 = (f32[18,36,4,1]{1,2,3,0:T(4,128)S(1)}, f32[18,36,4,1]{1,2,3,0:T(4,128)S(1)}, u32[]{:S(2)}, u32[]{:S(2)}) collective-permute-start(f32[18,36,4,1]{1,2,3,0:T(4,128)S(1)} %copy.45), channel_id=1, source_target_pairs={{2,0},{4,2},{6,4},{8,6},{10,8},{12,10},{14,12},{16,14},{18,16},{20... | collective-permute-start | bytes 31112 | tf_op jit(solution)/shard_map/ppermute | solution.py:17
  19.5 17.8 %collective-permute-start = (f32[18,36,4,1]{1,2,3,0:T(4,128)}, f32[18,36,4,1]{1,2,3,0:T(4,128)S(1)}, u32[]{:S(2)}, u32[]{:S(2)}) collective-permute-start(f32[18,36,4,1]{1,2,3,0:T(4,128)} %copy.44), channel_id=1, source_target_pairs={{0,2},{2,4},{4,6},{6,8},{8,10},{10,12},{12,14},{14,16},{16,18},{18... | collective-permute-start | bytes 31112 | tf_op jit(solution)/shard_map/ppermute | solution.py:16
  24.1 5.9 %copy-start.1 = (f32[1296]{0:T(1024)S(1)}, f32[1296]{0:T(1024)}, u32[]{:S(2)}) copy-start(f32[1296]{0:T(1024)} %param.21) | copy-start | bytes 15556
  29.9 5.9 %copy-start.13 = (f32[18]{0:T(128)S(1)}, f32[18]{0:T(128)}, u32[]{:S(2)}) copy-start(f32[18]{0:T(128)} %param.17) | copy-start | bytes 220
  30.0 6.0 %copy-start.11 = (s32[4,128]{1,0:T(4,128)S(1)}, s32[4,128]{1,0:T(4,128)}, u32[]{:S(2)}) copy-start(s32[4,128]{1,0:T(4,128)} %param.18) | copy-start | bytes 6148
  40.7 1.7 %copy-start.4 = (f32[18,36,4,1]{3,2,1,0:T(4,128)S(1)}, f32[18,36,4,1]{3,2,1,0:T(4,128)}, u32[]{:S(2)}) copy-start(f32[18,36,4,1]{3,2,1,0:T(4,128)} %copy.34) | copy-start | bytes 31108
  42.4 7.3 %copy-start.6 = (f32[4,128]{1,0:T(4,128)S(1)}, f32[4,128]{1,0:T(4,128)}, u32[]{:S(2)}) copy-start(f32[4,128]{1,0:T(4,128)} %param.19) | copy-start | bytes 6148
  42.4 7.3 %copy-start.10 = (f32[2,1296]{1,0:T(2,128)S(1)}, f32[2,1296]{1,0:T(2,128)}, u32[]{:S(2)}) copy-start(f32[2,1296]{1,0:T(2,128)} %param.23) | copy-start | bytes 31108
  49.7 0.8 copy-start.14
  49.7 0.8 copy-start.15
  58.5 26.1 %copy-start.12 = (f32[4,128]{1,0:T(4,128)S(1)}, f32[4,128]{1,0:T(4,128)}, u32[]{:S(2)}) copy-start(f32[4,128]{1,0:T(4,128)} %param.20) | copy-start | bytes 6148
  59.1 8.5 %all-to-all-start = ((f32[2,1,512]{2,1,0:T(1,128)}), f32[2,1,512]{2,1,0:T(1,128)S(1)}, u32[]{:S(2)}, u32[]{:S(2)}) async-start(f32[2,1,512]{2,1,0:T(1,128)} %broadcast_in_dim.58), calls=%async_computation | async-start | bytes 8192 | tf_op jit(solution)/shard_map/all_to_all | solution.py:35
  62.4 29.4 %collective-permute-start.4 = (f32[4,36,4,128]{3,2,1,0:T(4,128)S(1)}, f32[4,36,4,128]{3,2,1,0:T(4,128)S(1)}, u32[]{:S(2)}, u32[]{:S(2)}) collective-permute-start(f32[4,36,4,128]{3,2,1,0:T(4,128)S(1)} %get-tuple-element.55), channel_id=1, source_target_pairs={{0,1},{2,3},{4,5},{6,7},{8,9},{10,11},{12,13},{14,15},{16,17},{18,... | collective-permute-start | bytes 884744 | tf_op jit(solution)/shard_map/ppermute | solution.py:16
  66.3 25.5 %collective-permute-start.5 = (f32[4,36,4,128]{3,2,1,0:T(4,128)S(1)}, f32[4,36,4,128]{3,2,1,0:T(4,128)S(1)}, u32[]{:S(2)}, u32[]{:S(2)}) collective-permute-start(f32[4,36,4,128]{3,2,1,0:T(4,128)S(1)} %get-tuple-element.56), channel_id=1, source_target_pairs={{1,0},{3,2},{5,4},{7,6},{9,8},{11,10},{13,12},{15,14},{17,16},{19,... | collective-permute-start | bytes 884744 | tf_op jit(solution)/shard_map/ppermute | solution.py:17
  67.6 7.9 %all-to-all-start.1 = ((f32[2,2048,2]{1,2,0:T(2,128)}), f32[2,2048,2]{1,2,0:T(2,128)S(1)}, u32[]{:S(2)}, u32[]{:S(2)}) async-start(f32[2,2048,2]{1,2,0:T(2,128)} %get-tuple-element.36), calls=%async_computation.1 | async-start | bytes 65536 | tf_op jit(solution)/shard_map/all_to_all | solution.py:29
  76.2 14.9 %all-to-all-start.2 = ((f32[8,2048,2]{1,2,0:T(2,128)}), f32[8,2048,2]{1,2,0:T(2,128)S(1)}, u32[]{:S(2)}, u32[]{:S(2)}) async-start(f32[8,2048,2]{1,2,0:T(2,128)} %broadcast_in_dim.60), calls=%async_computation.2 | async-start | bytes 262144 | tf_op jit(solution)/shard_map/all_to_all | solution.py:35
  92.2 1.2 copy-start.2
  98.3 4.9 %copy-start.8 = (pred[936]{0:T(1024)(128)(4,1)S(1)}, pred[936]{0:T(1024)(128)(4,1)}, u32[]{:S(2)}) copy-start(pred[936]{0:T(1024)(128)(4,1)} %get-tuple-element.75) | copy-start | bytes 2812
  98.3 4.9 %copy-start.9 = (pred[936]{0:T(1024)(128)(4,1)S(1)}, pred[936]{0:T(1024)(128)(4,1)}, u32[]{:S(2)}) copy-start(pred[936]{0:T(1024)(128)(4,1)} %get-tuple-element.76) | copy-start | bytes 2812
  118.0 10.2 %copy-start.7 = (f32[512]{0:T(512)S(1)}, f32[512]{0:T(512)}, u32[]{:S(2)}) copy-start(f32[512]{0:T(512)} %get-tuple-element.61) | copy-start | bytes 6148
where the time goes:
time: 133 us; the launch traced here: 132 us
  local copies, waits for them, and re-layouts  43.7 us (33%)
  other arithmetic  37.8 us (28%)
  starting transfers between devices  31.3 us (24%)
  waiting for transfers between devices  10.5 us (8%)
  matrix products  6.24 us (5%)
  loops' own time  1.33 us (1%)
    scatter-add x2, other arithmetic, source_update(): jnp.zeros_like(transfer).at[partners[0]].add(transfer).at[partners[1]]  20.3 us
    all_to_all x2, starting transfers between devices, copy_for_each(): return lax.all_to_all(copies, axis, split_axis=0, concat_axis=0, tiled=True)  11.6 us
    ppermute x3, starting transfers between devices, padded(): after = lax.ppermute(leading, axis, down)  9.95 us
    reduce_sum x1, other arithmetic, local(): band_sum = jnp.sum(moved.reshape(band_bins, -1), axis=0)  7.27 us
    all_to_all x2, waiting for transfers between devices, copy_for_each(): return lax.all_to_all(copies, axis, split_axis=0, concat_axis=0, tiled=True)  6.56 us
    gather x1, local copies, waits for them, and re-layouts, local(): coef_rows = jnp.take(nonlinear_coef, global_bins)  5.85 us
    gather x1, local copies, waits for them, and re-layouts, local(): profile_rows = jnp.take(wind_profile, global_bins)  5.85 us
    ppermute x3, starting transfers between devices, padded(): before = lax.ppermute(last, axis, up)  5.84 us
  transfers between devices with their start and end apart: 9, of which 2 were waited for; matrix products, arithmetic and copies ran while one was open for 22% of the time, Pallas kernels for 0%

commit v1 on v0

v1 whole, which is shorter than its diff:
```python
import jax
import jax.numpy as jnp
import numpy as np
from jax import lax
from jax.experimental import pallas as pl
from jax.experimental.pallas import tpu as pltpu
from jax.sharding import PartitionSpec as P

F32 = jnp.float32
NF, ND = 18, 36
NB = NF * ND
TILES = ND // 2
ROWS = NB * 4
BORDER = 4 * ND

angles = (np.float32(2.0 * np.pi) * np.arange(ND, dtype=np.float32) / np.float32(ND)).astype(np.float32)
COS = np.cos(angles).astype(np.float32)
SIN = np.sin(angles).astype(np.float32)
WEST = [bool(c > 0) for c in COS]
WEST_TILES = [k for k in range(TILES) if WEST[2 * k] or WEST[2 * k + 1]]
EAST_TILES = [k for k in range(TILES) if not (WEST[2 * k] and WEST[2 * k + 1])]
LANES_F = 10
FREQS_V = 12

VM = pl.BlockSpec(memory_space=pltpu.VMEM)
SM = pl.BlockSpec(memory_space=pltpu.SMEM)
PARAMS = pltpu.CompilerParams(vmem_limit_bytes=40 * 1024 * 1024)


def in_vmem(shape, dtype=F32):
    return pltpu.VMEM(shape, dtype)


def tile_iota(dim):
    return lax.broadcasted_iota(jnp.int32, (8, 128), dim)


def pack_kernel(e_ref, up_ref, dn_ref, east_ref, west_ref):
    lane = tile_iota(1)
    for f in range(NF):
        up_ref[f * 18 : f * 18 + 18, :] = e_ref[pl.ds(f * 144 + 3, 18, stride=4), :]
        dn_ref[f * 18 : f * 18 + 18, :] = e_ref[pl.ds(f * 144 + 72, 18, stride=4), :]
    for tiles, ref, col in ((WEST_TILES, east_ref, 127), (EAST_TILES, west_ref, 0)):
        for chunk in range(2):
            acc = jnp.zeros((8, 128), F32)
            for f in range(chunk * FREQS_V, min(NF, (chunk + 1) * FREQS_V)):
                for kk, k in enumerate(tiles):
                    pos = (f % FREQS_V) * LANES_F + kk
                    x = e_ref[(f * TILES + k) * 8 : (f * TILES + k) * 8 + 8, :]
                    acc = jnp.where(lane == pos, pltpu.roll(x, (pos - col) % 128, 1), acc)
            ref[:, chunk * 128 : chunk * 128 + 128] = acc


def move_kernel(
    where_ref, gs_ref, mom_ref, prof_ref, e_ref, so_ref, no_ref, hw_ref, he_ref, mask_ref, wind_ref, cell_ref,
    moved_ref, msg_ref, halo_ref,
):
    lat, lon, freq = where_ref[0], where_ref[1], where_ref[2]
    lane, row = tile_iota(1), tile_iota(0)
    first, last = lane == 0, lane == 127
    low = row < 4
    top, bottom = row % 4 == 0, row % 4 == 3
    for f in range(NF):
        halo_ref[pl.ds(f * 144, 18, stride=4), :] = so_ref[f * 18 : f * 18 + 18, :]
        halo_ref[pl.ds(f * 144 + 72 + 3, 18, stride=4), :] = no_ref[f * 18 : f * 18 + 18, :]
    mask4 = mask_ref[...].astype(F32)
    mask8 = jnp.concatenate([mask4, mask4], 0)

    def one_freq(f, carry):
        en, t0, t1 = carry
        chunk = pl.multiple_of((f // FREQS_V) * 128, 128)
        base = (f % FREQS_V) * LANES_F
        back = lax.rem(128 - base, 128)
        hw = pltpu.roll(hw_ref[:, pl.ds(chunk, 128)], back, 1)
        he = pltpu.roll(he_ref[:, pl.ds(chunk, 128)], back, 1)
        gs = gs_ref[f]
        for k in range(TILES):
            at = pl.multiple_of(f * 144 + k * 8, 8)
            x = e_ref[pl.ds(at, 8), :]
            h = halo_ref[pl.ds(at, 8), :]
            west = east = None
            if k in WEST_TILES:
                kk = WEST_TILES.index(k)
                west = jnp.where(first, pltpu.roll(hw, (128 - kk) % 128, 1), pltpu.roll(x, 1, 1))
            if k in EAST_TILES:
                kk = EAST_TILES.index(k)
                east = jnp.where(last, pltpu.roll(he, 127 - kk, 1), pltpu.roll(x, 127, 1))
            if east is None:
                xs = west
            elif west is None:
                xs = east
            else:
                xs = jnp.where(low, west, east) if WEST[2 * k] else jnp.where(low, east, west)
            if k < TILES // 2:
                ys = jnp.where(top, h, pltpu.roll(x, 1, 0))
            else:
                ys = jnp.where(bottom, h, pltpu.roll(x, 7, 0))
            cx = jnp.where(low, float(abs(COS[2 * k])), float(abs(COS[2 * k + 1]))).astype(F32)
            cy = jnp.where(low, float(abs(SIN[2 * k])), float(abs(SIN[2 * k + 1]))).astype(F32)
            m = mask8 * (x - gs * (cx * (x - xs) + cy * (x - ys)))
            moved_ref[pl.ds(at, 8), :] = m
            b = freq * NB + f * ND + 2 * k
            p0, p1 = prof_ref[b], prof_ref[b + 1]
            en = en + m
            t0 = t0 + m * jnp.where(low, mom_ref[0, b] * p0, mom_ref[0, b + 1] * p1)
            t1 = t1 + m * jnp.where(low, mom_ref[1, b] * p0, mom_ref[1, b + 1] * p1)
        return en, t0, t1

    zero = jnp.zeros((8, 128), F32)
    en, t0, t1 = lax.fori_loop(0, NF, one_freq, (zero, zero, zero))
    start = pl.multiple_of((1 - freq) * (14 * 144), 8)
    for k in range(72):
        msg_ref[k * 8 : k * 8 + 8, :] = moved_ref[pl.ds(start + k * 8, 8), :]
    wind = wind_ref[...]
    i4 = lax.broadcasted_iota(jnp.int32, (4, 128), 0) + lat * 4
    j4 = lax.broadcasted_iota(jnp.int32, (4, 128), 1) + lon * 128
    offset = cell_ref[...] - (j4 * 32 + i4)
    for c, t in enumerate((t0, t1)):
        tau = (t[0:4] + t[4:8]) * wind
        at = 4 * BORDER + 8 * c
        msg_ref[at : at + 8, :] = zero
        for d in (-1, 0, 1):
            msg_ref[at + 1 + d : at + 5 + d, :] += jnp.where(offset == d, tau, 0.0)
    msg_ref[4 * BORDER + 16 : 4 * BORDER + 20, :] = en[0:4] + en[4:8]
    msg_ref[4 * BORDER + 20 : 4 * BORDER + 24, :] = jnp.zeros((4, 128), F32)


def transfer_of(e, third, fourth, coef):
    return coef * (e * (e * (third + fourth) - 2.0 * third * fourth))


STEP = 8


def inner_kernel(where_ref, quad_ref, coef_ref, m_ref, a_ref, b_ref):
    freq = where_ref[2]
    zero = jnp.zeros((4, 128), F32)

    def clear(i, _):
        for u in range(8):
            a_ref[i * 8 + u] = zero
            b_ref[i * 8 + u] = zero
        return 0

    lax.fori_loop(0, NB // 8, clear, 0)
    shift = freq * NB
    start = freq * (2 * ND)

    def some(i, _):
        own, q0, q1, t = [], [], [], []
        for u in range(STEP):
            b = start + i * STEP + u
            own.append(b)
            q0.append(quad_ref[0, shift + b] - shift)
            q1.append(quad_ref[1, shift + b] - shift)
            t.append(transfer_of(m_ref[b], m_ref[q0[u]], m_ref[q1[u]], coef_ref[shift + b]))
        for u in range(STEP):
            a_ref[q0[u]] += t[u]
            b_ref[q1[u]] += t[u]
        for u in range(STEP):
            a_ref[own[u]] -= 2.0 * t[u]
        return 0

    lax.fori_loop(0, 16 * ND // STEP, some, 0)


def outer_kernel(
    where_ref, quad_ref, coef_ref, prof_ref, m_ref, a_ref, b_ref, mine_ref, theirs_ref, wind_ref, dis_ref,
    out_ref, ext_ref, acc_ref,
):
    freq = where_ref[2]
    zero = jnp.zeros((4, 128), F32)
    mine = freq * BORDER
    theirs = BORDER - mine

    def fill(i, _):
        for u in range(8):
            k = i * 8 + u
            ext_ref[mine + k] = mine_ref[k]
            ext_ref[theirs + k] = theirs_ref[k]
            acc_ref[k] = zero
            acc_ref[BORDER + k] = zero
        return 0

    lax.fori_loop(0, BORDER // 8, fill, 0)
    shift = 14 * ND

    def some(i, _):
        own, q0, q1, t = [], [], [], []
        for u in range(STEP):
            b = 2 * ND + i * STEP + u
            own.append(b)
            q0.append(quad_ref[0, shift + b] - shift)
            q1.append(quad_ref[1, shift + b] - shift)
            t.append(transfer_of(ext_ref[b], ext_ref[q0[u]], ext_ref[q1[u]], coef_ref[shift + b]))
        for u in range(STEP):
            acc_ref[q0[u]] += t[u]
            acc_ref[q1[u]] += t[u]
            acc_ref[own[u]] -= 2.0 * t[u]
        return 0

    lax.fori_loop(0, BORDER // STEP, some, 0)
    energy = (mine_ref[BORDER + 4] + theirs_ref[BORDER + 4]) * (1.0 / (2 * NB))
    keep = 1.0 - 0.5 * (dis_ref[...] * energy)
    wind = 0.5 * wind_ref[...]
    first = freq * NB

    def finish(b, extra):
        out = m_ref[b] * (keep + wind * prof_ref[first + b])
        total = a_ref[b] + b_ref[b]
        if extra is not None:
            total = total + extra
        out_ref[b] = out + 0.5 * total

    inner = freq * BORDER
    edge = (1 - freq) * (14 * ND)

    def plain(i, _):
        for u in range(8):
            finish(inner + i * 8 + u, None)
        return 0

    lax.fori_loop(0, 14 * ND // 8, plain, 0)

    def bordering(i, _):
        for u in range(8):
            k = i * 8 + u
            finish(edge + k, acc_ref[mine + k])
        return 0

    lax.fori_loop(0, BORDER // 8, bordering, 0)


def half_kernel(where_ref, mine_ref, theirs_ref, out_ref):
    freq = where_ref[2]
    lane = tile_iota(1)
    at = 4 * BORDER
    r0 = mine_ref[at : at + 8, :] + theirs_ref[at : at + 8, :]
    r1 = mine_ref[at + 8 : at + 16, :] + theirs_ref[at + 8 : at + 16, :]
    lower = jnp.where(lane < 64, r0, pltpu.roll(r1, 64, 1))
    upper = jnp.where(lane < 64, pltpu.roll(r0, 64, 1), r1)
    out_ref[...] = jnp.where(freq == 0, lower, upper)


def cells_kernel(where_ref, r_ref, out_ref, z_ref, t_ref):
    lat = where_ref[0]
    z_ref[...] = jnp.zeros_like(z_ref)
    for k in range(8):
        block = r_ref[pl.ds(pl.multiple_of(jnp.bitwise_xor(lat, k) * 8, 8), 8), :]
        z_ref[7 + 4 * k : 13 + 4 * k, :] += block[0:6]
    t_ref[:, 0:32] = jnp.transpose(z_ref[8:40, :])
    t_ref[:, 32:128] = jnp.zeros((128, 96), F32)
    out = jnp.zeros((32, 128), F32)
    for jj in range(4):
        piece = t_ref[pl.ds(jj, 32, stride=4), :]
        out = out + pltpu.roll(piece, jj * 32, 1)
    for c in range(2):
        for g in range(16):
            out_ref[c : c + 1, g * 128 : g * 128 + 128] = out[c * 16 + g : c * 16 + g + 1, :]


def call(kernel, out, in_specs, scratch=()):
    return pl.pallas_call(
        kernel,
        out_shape=out,
        in_specs=in_specs,
        out_specs=jax.tree.map(lambda _: VM, out),
        scratch_shapes=list(scratch),
        compiler_params=PARAMS,
    )


def local(
    spectrum, group_speed, sea_mask, wind_growth, dissipation, wind_profile, nonlinear_coef, momentum, quadruplet,
    ocean_cell,
):
    where = jnp.stack([lax.axis_index(a) for a in ("lat", "lon", "freq")]).astype(jnp.int32)
    flat = spectrum.reshape(ROWS, 128)
    halo = in_vmem((NF * 18, 128))
    edge = in_vmem((8, 256))
    up, dn, to_east, to_west = call(pack_kernel, (halo, halo, edge, edge), [VM])(flat)
    nlat, nlon = lax.axis_size("lat"), lax.axis_size("lon")
    east = [(i, (i + 1) % nlon) for i in range(nlon)]
    north = [(i, i + 1) for i in range(nlat - 1)]
    from_west = lax.ppermute(to_east, "lon", east)
    from_east = lax.ppermute(to_west, "lon", [(j, i) for i, j in east])
    from_south = lax.ppermute(up, "lat", north)
    from_north = lax.ppermute(dn, "lat", [(j, i) for i, j in north])
    moved, message = call(
        move_kernel,
        (in_vmem((ROWS, 128)), in_vmem((4 * BORDER + 24, 128))),
        [SM] * 4 + [VM] * 8,
        [pltpu.VMEM((ROWS, 128), F32)],
    )(
        where, group_speed, momentum, wind_profile, flat, from_south, from_north, from_west, from_east, sea_mask,
        wind_growth, ocean_cell,
    )
    theirs = lax.ppermute(message, "freq", [(0, 1), (1, 0)])
    bins = moved.reshape(NB, 4, 128)
    acc = in_vmem((NB, 4, 128))
    part_a, part_b = call(inner_kernel, (acc, acc), [SM] * 3 + [VM])(where, quadruplet, nonlinear_coef, bins)
    rows = call(half_kernel, in_vmem((8, 128)), [SM, VM, VM])(where, message, theirs)
    for bit in (1, 2, 4):
        other = lax.ppermute(rows, "lat", [(i, i ^ bit) for i in range(nlat)])
        rows = jnp.concatenate([rows, other], 0)
    out = call(
        outer_kernel,
        jax.ShapeDtypeStruct((NB, 4, 128), F32),
        [SM] * 4 + [VM] * 7,
        [pltpu.VMEM((2 * BORDER, 4, 128), F32), pltpu.VMEM((2 * BORDER, 4, 128), F32)],
    )(
        where, quadruplet, nonlinear_coef, wind_profile, bins, part_a, part_b, message.reshape(BORDER + 6, 4, 128),
        theirs.reshape(BORDER + 6, 4, 128), wind_growth, dissipation,
    )
    stress = call(
        cells_kernel,
        jax.ShapeDtypeStruct((2, 2048), F32),
        [SM, VM],
        [pltpu.VMEM((48, 128), F32), pltpu.VMEM((128, 128), F32)],
    )(where, rows)
    return out.reshape(spectrum.shape), stress.T


def solution(mesh):
    return jax.shard_map(
        local,
        mesh=mesh,
        in_specs=(
            P("freq", None, "lat", "lon"),
            P("freq"),
            P("lat", "lon"),
            P("lat", "lon"),
            P("lat", "lon"),
            P(),
            P(),
            P(),
            P(),
            P("lat", "lon"),
        ),
        out_specs=(P("freq", None, "lat", "lon"), P(("lon", "freq"), None)),
        check_vma=False,
    )
```

time: 133 us -> 56.5 us (0.42)
  local copies, waits for them, and re-layouts: 43.7 us -> 1.36 us
  other arithmetic: 37.8 us -> 0.08 us
  Pallas kernels: 0 us -> 19.2 us
  starting transfers between devices: 31.3 us -> 20.6 us
  matrix products: 6.24 us -> 0 us
  waiting for transfers between devices: 10.5 us -> 13.4 us
  loops' own time: 1.33 us -> 0 us
    gather x5 -> x0, local copies, waits for them, and re-layouts: 24.2 us -> none  [the longest x1 5.85 us: local(): coef_rows = jnp.take(nonlinear_coef, global_bins)]
    scatter-add x2 -> x0, other arithmetic: 20.3 us -> none  [source_update(): jnp.zeros_like(transfer).at[partners[0]].add(transfer).at[partners[1]]]
    pallas_call x0 -> x6, Pallas kernels: none -> 19.2 us  [the longest x1 6.45 us: local(): call(inner_kernel, (acc, acc), [SM] * 3 + [VM])]
    all_to_all x3 -> x0, starting transfers between devices: 15.5 us -> none  [the longest x2 11.6 us: copy_for_each(): return lax.all_to_all(copies, axis, split_axis=0, concat_axis=0, tiled=True)]
    ppermute x6 -> x8, waiting for transfers between devices: 0.02 us -> 13.4 us  [the longest x1 6.93 us: local(): theirs = lax.ppermute(message, 'freq', [(0, 1), (1, 0)])]
    all_to_all x3 -> x0, waiting for transfers between devices: 10.5 us -> none  [the longest x2 6.56 us: copy_for_each(): return lax.all_to_all(copies, axis, split_axis=0, concat_axis=0, tiled=True)]
    mul x5 -> x0, other arithmetic: 8.06 us -> none  [the longest x1 4.65 us: source_update(): coef_rows[:, None]]
    reduce_sum x4 -> x0, other arithmetic: 7.97 us -> none  [the longest x1 7.27 us: local(): band_sum = jnp.sum(moved.reshape(band_bins, -1), axis=0)]
  transfers between devices with their start and end apart: 9 -> 8, of which waited for: 2 -> 5; matrix products, arithmetic and copies ran while one was open for 22% -> 0% of each run, Pallas kernels for 0% -> 21%
where the time goes in v1:
time: 56.5 us; the launch traced here: 55.5 us
  starting transfers between devices  20.6 us (36%)
  Pallas kernels  19.2 us (34%)
  waiting for transfers between devices  13.4 us (24%)
  local copies, waits for them, and re-layouts  1.36 us (2%)
  between operations  0.8 us (1%)
    ppermute x3, starting transfers between devices, local(): other = lax.ppermute(rows, 'lat', [(i, i ^ bit) for i in range(nlat)])  8.36 us
    ppermute x1, waiting for transfers between devices, local(): theirs = lax.ppermute(message, 'freq', [(0, 1), (1, 0)])  6.93 us
    pallas_call x1, Pallas kernels, local(): call(inner_kernel, (acc, acc), [SM] * 3 + [VM])  6.45 us
    pallas_call x1, Pallas kernels, local(): call(outer_kernel, jax.ShapeDtypeStruct((NB, 4, 128), F32), [SM] * 4 + [V...  5.33 us
    ppermute x3, waiting for transfers between devices, local(): other = lax.ppermute(rows, 'lat', [(i, i ^ bit) for i in range(nlat)])  5.22 us
    pallas_call x1, Pallas kernels, local(): call(move_kernel, (in_vmem((ROWS, 128)), in_vmem((4 * BORDER + 24, 128)))...  5.02 us
    ppermute x1, starting transfers between devices, local(): from_east = lax.ppermute(to_west, 'lon', [(j, i) for i, j in east])  4.75 us
    ppermute x1, starting transfers between devices, local(): from_south = lax.ppermute(up, 'lat', north)  3.48 us
  transfers between devices with their start and end apart: 8, of which 5 were waited for; matrix products, arithmetic and copies ran while one was open for 0% of the time, Pallas kernels for 21%

profile of v1, /device:TPU:8, one launch (start us, length us, event | category | flops | bytes accessed | tf_op | source)
XLA Modules:
  0.0 55.5 jit_solution(13461631193311619491)
XLA Ops:
  0.6 0.0 copy-start.10
  0.6 0.0 copy-start
  0.7 1.3 %copy-done = f32[18,36,4,128]{3,2,1,0:T(4,128)S(1)} copy-done((f32[18,36,4,128]{3,2,1,0:T(4,128)S(1)}, f32[18,36,4,128]{3,2,1,0:T(4,128)}, u32[]{:S(2)}) %copy-start) | copy-done | bytes 1327128
  2.0 0.0 copy-start.1
  2.0 0.0 copy-start.4
  2.0 0.0 copy-start.5
  2.0 0.0 copy-start.6
  2.0 0.0 copy-start.7
  2.0 0.0 copy-start.8
  2.0 0.4 shard_map.113
  2.4 0.0 copy-start.2
  2.5 0.0 copy-start.3
  2.5 3.5 %collective-permute-start = (f32[324,128]{1,0:T(8,128)S(1)}, f32[324,128]{1,0:T(8,128)S(1)}, u32[]{:S(2)}, u32[]{:S(2)}) collective-permute-start(f32[324,128]{1,0:T(8,128)S(1)} %get-tuple-element.10), channel_id=1, source_target_pairs={{0,32},{32,64},{64,96},{96,128},{128,160},{160,192},{192,224},{1,3... | collective-permute-start | bytes 497672 | tf_op jit(solution)/shard_map/ppermute | solution.py:287
  6.0 2.4 %collective-permute-start.1 = (f32[324,128]{1,0:T(8,128)S(1)}, f32[324,128]{1,0:T(8,128)S(1)}, u32[]{:S(2)}, u32[]{:S(2)}) collective-permute-start(f32[324,128]{1,0:T(8,128)S(1)} %get-tuple-element.11), channel_id=1, source_target_pairs={{32,0},{64,32},{96,64},{128,96},{160,128},{192,160},{224,192},{33,... | collective-permute-start | bytes 497672 | tf_op jit(solution)/shard_map/ppermute | solution.py:288
  8.3 0.0 collective-permute-start.2
  8.4 4.7 %collective-permute-start.3 = (f32[8,256]{1,0:T(8,128)S(1)}, f32[8,256]{1,0:T(8,128)S(1)}, u32[]{:S(2)}, u32[]{:S(2)}) collective-permute-start(f32[8,256]{1,0:T(8,128)S(1)} %get-tuple-element.13), channel_id=1, source_target_pairs={{2,0},{4,2},{6,4},{8,6},{10,8},{12,10},{14,12},{16,14},{18,16},{20... | collective-permute-start | bytes 24584 | tf_op jit(solution)/shard_map/ppermute | solution.py:286
  13.1 0.1 pad_add_fusion.where_ref
  13.2 1.2 %collective-permute-done.2.hw_ref = f32[8,256]{1,0:T(8,128)S(1)} collective-permute-done((f32[8,256]{1,0:T(8,128)S(1)}, f32[8,256]{1,0:T(8,128)S(1)}, u32[]{:S(2)}, u32[]{:S(2)}) %collective-permute-start.2) | collective-permute-done | bytes 8224 | tf_op jit(solution)/shard_map/ppermute | solution.py:285
  14.4 0.1 collective-permute-done.3.he_ref
  14.5 0.0 collective-permute-done.so_ref
  14.5 0.0 collective-permute-done.1.no_ref
  14.5 0.0 copy-done.10
  14.5 0.0 copy-done.1
  14.5 0.0 copy-done.4
  14.5 0.0 copy-done.5
  14.5 0.0 copy-done.6
  14.5 0.0 copy-done.7
  14.5 0.0 copy-done.8
  14.6 5.0 %shard_map.114 = (f32[2592,128]{1,0:T(8,128)S(1)}, f32[600,128]{1,0:T(8,128)S(1)}) custom-call(s32[3]{0:T(128)S(1)} %pad_add_fusion.where_ref, f32[18]{0:T(128)S(1)} %copy-done.10, f32[2,1296]{1,0:T(2,128)S(1)} %copy-done.5, f32[1296]{0:T(1024)S(1)} %copy-done.4, f32[2592,128]{1,0:T(8,128)S(1)} %bitcast.10, f32[324,128]{1,0:T(8,128)S(1)} %collective-permute-done.so_ref, ...), custom_call_target="tpu_custom_call" | custom-call | tf_op jit(solution)/shard_map/pallas_call | solution.py:289
  19.6 0.0 copy-start.9
  19.6 1.6 %collective-permute-start.4 = (f32[600,128]{1,0:T(8,128)S(1)}, f32[600,128]{1,0:T(8,128)S(1)}, u32[]{:S(2)}, u32[]{:S(2)}) collective-permute-start(f32[600,128]{1,0:T(8,128)S(1)} %get-tuple-element.17.mine_ref), channel_id=1, source_target_pairs={{0,1},{1,0},{2,3},{3,2},{4,5},{5,4},{6,7},{7,6},{8,9},{9,8},{10,11... | collective-permute-start | bytes 921608 | tf_op jit(solution)/shard_map/ppermute | solution.py:298
  21.2 6.9 %collective-permute-done.4.theirs_ref = f32[600,128]{1,0:T(8,128)S(1)} collective-permute-done((f32[600,128]{1,0:T(8,128)S(1)}, f32[600,128]{1,0:T(8,128)S(1)}, u32[]{:S(2)}, u32[]{:S(2)}) %collective-permute-start.4) | collective-permute-done | bytes 307232 | tf_op jit(solution)/shard_map/ppermute | solution.py:298
  28.1 0.6 %shard_map.117 = f32[8,128]{1,0:T(8,128)S(1)} custom-call(s32[3]{0:T(128)S(1)} %pad_add_fusion.where_ref, f32[600,128]{1,0:T(8,128)S(1)} %get-tuple-element.17.mine_ref, f32[600,128]{1,0:T(8,128)S(1)} %collective-permute-done.4.theirs_ref), custom_call_target="tpu_custom_call" | custom-call | tf_op jit(solution)/shard_map/pallas_call | solution.py:302
  28.7 0.0 collective-permute-start.5
  28.7 3.6 %collective-permute-done.5 = f32[8,128]{1,0:T(8,128)S(1)} collective-permute-done((f32[8,128]{1,0:T(8,128)S(1)}, f32[8,128]{1,0:T(8,128)S(1)}, u32[]{:S(2)}, u32[]{:S(2)}) %collective-permute-start.5) | collective-permute-done | bytes 4128 | tf_op jit(solution)/shard_map/ppermute | solution.py:304
  32.3 5.5 %collective-permute-start.6 = (f32[16,128]{1,0:T(8,128)S(1)}, f32[16,128]{1,0:T(8,128)S(1)}, u32[]{:S(2)}, u32[]{:S(2)}) collective-permute-start(f32[16,128]{1,0:T(8,128)S(1)} %pad_maximum_fusion.2), channel_id=1, source_target_pairs={{0,64},{32,96},{64,0},{96,32},{128,192},{160,224},{192,128},{224,1... | collective-permute-start | bytes 24584 | tf_op jit(solution)/shard_map/ppermute | solution.py:304
  37.9 1.6 %collective-permute-done.6 = f32[16,128]{1,0:T(8,128)S(1)} collective-permute-done((f32[16,128]{1,0:T(8,128)S(1)}, f32[16,128]{1,0:T(8,128)S(1)}, u32[]{:S(2)}, u32[]{:S(2)}) %collective-permute-start.6) | collective-permute-done | bytes 8224 | tf_op jit(solution)/shard_map/ppermute | solution.py:304
  39.5 2.8 %collective-permute-start.7 = (f32[32,128]{1,0:T(8,128)S(1)}, f32[32,128]{1,0:T(8,128)S(1)}, u32[]{:S(2)}, u32[]{:S(2)}) collective-permute-start(f32[32,128]{1,0:T(8,128)S(1)} %pad_maximum_fusion.1), channel_id=1, source_target_pairs={{0,128},{32,160},{64,192},{96,224},{128,0},{160,32},{192,64},{224,... | collective-permute-start | bytes 49160 | tf_op jit(solution)/shard_map/ppermute | solution.py:304
  42.3 0.0 copy-done.2
  42.3 0.0 copy-done.3
  42.3 6.4 %shard_map.115 = (f32[648,4,128]{2,1,0:T(4,128)S(1)}, f32[648,4,128]{2,1,0:T(4,128)S(1)}) custom-call(s32[3]{0:T(128)S(1)} %pad_add_fusion.where_ref, s32[2,1296]{1,0:T(2,128)S(1)} %copy-done.2, f32[1296]{0:T(1024)S(1)} %copy-done.3, f32[648,4,128]{2,1,0:T(4,128)S(1)} %bitcast.11), custom_call_target="tpu_custom_call" | custom-call | tf_op jit(solution)/shard_map/pallas_call | solution.py:301
  48.8 0.0 copy-done.9
  48.8 5.3 %shard_map.116 = f32[648,4,128]{2,1,0:T(4,128)} custom-call(s32[3]{0:T(128)S(1)} %pad_add_fusion.where_ref, s32[2,1296]{1,0:T(2,128)S(1)} %copy-done.2, f32[1296]{0:T(1024)S(1)} %copy-done.3, f32[1296]{0:T(1024)S(1)} %copy-done.4, f32[648,4,128]{2,1,0:T(4,128)S(1)} %bitcast.12, f32[648,4,128]{2,1,0:T(4,128)S(1)} %get-tuple-element.15.a_ref, ...), custom_call_target="tpu_custom_call" | custom-call | tf_op jit(solution)/shard_map/pallas_call | solution.py:306
  54.1 0.0 collective-permute-done.7
  54.1 1.4 %shard_map.118 = f32[2,2048]{1,0:T(2,128)} custom-call(s32[3]{0:T(128)S(1)} %pad_add_fusion.where_ref, f32[64,128]{1,0:T(8,128)S(1)} %pad_maximum_fusion.r_ref), custom_call_target="tpu_custom_call" | custom-call | tf_op jit(solution)/shard_map/pallas_call | solution.py:315
  (3 shorter events, 0.0 us)
Async XLA Ops:
  0.6 13.9 %copy-start.10 = (f32[18]{0:T(128)S(1)}, f32[18]{0:T(128)}, u32[]{:S(2)}) copy-start(f32[18]{0:T(128)} %gs_ref.1) | copy-start | bytes 220
  0.6 1.3 %copy-start = (f32[18,36,4,128]{3,2,1,0:T(4,128)S(1)}, f32[18,36,4,128]{3,2,1,0:T(4,128)}, u32[]{:S(2)}) copy-start(f32[18,36,4,128]{3,2,1,0:T(4,128)} %param.10) | copy-start | bytes 3981316
  2.0 12.5 %copy-start.1 = (f32[18,36,4,128]{3,2,1,0:T(4,128)S(1)}, f32[18,36,4,128]{3,2,1,0:T(4,128)}, u32[]{:S(2)}) copy-start(f32[18,36,4,128]{3,2,1,0:T(4,128)} %param.10) | copy-start | bytes 3981316
  2.0 12.5 %copy-start.4 = (f32[1296]{0:T(1024)S(1)}, f32[1296]{0:T(1024)}, u32[]{:S(2)}) copy-start(f32[1296]{0:T(1024)} %prof_ref.3) | copy-start | bytes 15556
  2.0 12.5 %copy-start.5 = (f32[2,1296]{1,0:T(2,128)S(1)}, f32[2,1296]{1,0:T(2,128)}, u32[]{:S(2)}) copy-start(f32[2,1296]{1,0:T(2,128)} %mom_ref.1) | copy-start | bytes 31108
  2.0 12.5 %copy-start.6 = (f32[4,128]{1,0:T(4,128)S(1)}, f32[4,128]{1,0:T(4,128)}, u32[]{:S(2)}) copy-start(f32[4,128]{1,0:T(4,128)} %wind_ref.3) | copy-start | bytes 6148
  2.0 12.6 %copy-start.7 = (s32[4,128]{1,0:T(4,128)S(1)}, s32[4,128]{1,0:T(4,128)}, u32[]{:S(2)}) copy-start(s32[4,128]{1,0:T(4,128)} %mask_ref.1) | copy-start | bytes 6148
  2.0 12.6 %copy-start.8 = (s32[4,128]{1,0:T(4,128)S(1)}, s32[4,128]{1,0:T(4,128)}, u32[]{:S(2)}) copy-start(s32[4,128]{1,0:T(4,128)} %cell_ref.1) | copy-start | bytes 6148
  2.4 39.9 %copy-start.2 = (s32[2,1296]{1,0:T(2,128)S(1)}, s32[2,1296]{1,0:T(2,128)}, u32[]{:S(2)}) copy-start(s32[2,1296]{1,0:T(2,128)} %quad_ref.3) | copy-start | bytes 31108
  2.5 39.8 %copy-start.3 = (f32[1296]{0:T(1024)S(1)}, f32[1296]{0:T(1024)}, u32[]{:S(2)}) copy-start(f32[1296]{0:T(1024)} %coef_ref.3) | copy-start | bytes 15556
  2.5 12.0 %collective-permute-start = (f32[324,128]{1,0:T(8,128)S(1)}, f32[324,128]{1,0:T(8,128)S(1)}, u32[]{:S(2)}, u32[]{:S(2)}) collective-permute-start(f32[324,128]{1,0:T(8,128)S(1)} %get-tuple-element.10), channel_id=1, source_target_pairs={{0,32},{32,64},{64,96},{96,128},{128,160},{160,192},{192,224},{1,3... | collective-permute-start | bytes 497672 | tf_op jit(solution)/shard_map/ppermute | solution.py:287
  6.0 8.5 %collective-permute-start.1 = (f32[324,128]{1,0:T(8,128)S(1)}, f32[324,128]{1,0:T(8,128)S(1)}, u32[]{:S(2)}, u32[]{:S(2)}) collective-permute-start(f32[324,128]{1,0:T(8,128)S(1)} %get-tuple-element.11), channel_id=1, source_target_pairs={{32,0},{64,32},{96,64},{128,96},{160,128},{192,160},{224,192},{33,... | collective-permute-start | bytes 497672 | tf_op jit(solution)/shard_map/ppermute | solution.py:288
  8.3 6.1 %collective-permute-start.2 = (f32[8,256]{1,0:T(8,128)S(1)}, f32[8,256]{1,0:T(8,128)S(1)}, u32[]{:S(2)}, u32[]{:S(2)}) collective-permute-start(f32[8,256]{1,0:T(8,128)S(1)} %get-tuple-element.12), channel_id=1, source_target_pairs={{0,2},{2,4},{4,6},{6,8},{8,10},{10,12},{12,14},{14,16},{16,18},{18... | collective-permute-start | bytes 24584 | tf_op jit(solution)/shard_map/ppermute | solution.py:285
  8.4 6.1 %collective-permute-start.3 = (f32[8,256]{1,0:T(8,128)S(1)}, f32[8,256]{1,0:T(8,128)S(1)}, u32[]{:S(2)}, u32[]{:S(2)}) collective-permute-start(f32[8,256]{1,0:T(8,128)S(1)} %get-tuple-element.13), channel_id=1, source_target_pairs={{2,0},{4,2},{6,4},{8,6},{10,8},{12,10},{14,12},{16,14},{18,16},{20... | collective-permute-start | bytes 24584 | tf_op jit(solution)/shard_map/ppermute | solution.py:286
  19.6 29.2 %copy-start.9 = (f32[4,128]{1,0:T(4,128)S(1)}, f32[4,128]{1,0:T(4,128)}, u32[]{:S(2)}) copy-start(f32[4,128]{1,0:T(4,128)} %dis_ref.1) | copy-start | bytes 6148
  19.6 8.5 %collective-permute-start.4 = (f32[600,128]{1,0:T(8,128)S(1)}, f32[600,128]{1,0:T(8,128)S(1)}, u32[]{:S(2)}, u32[]{:S(2)}) collective-permute-start(f32[600,128]{1,0:T(8,128)S(1)} %get-tuple-element.17.mine_ref), channel_id=1, source_target_pairs={{0,1},{1,0},{2,3},{3,2},{4,5},{5,4},{6,7},{7,6},{8,9},{9,8},{10,11... | collective-permute-start | bytes 921608 | tf_op jit(solution)/shard_map/ppermute | solution.py:298
  28.7 3.6 %collective-permute-start.5 = (f32[8,128]{1,0:T(8,128)S(1)}, f32[8,128]{1,0:T(8,128)S(1)}, u32[]{:S(2)}, u32[]{:S(2)}) collective-permute-start(f32[8,128]{1,0:T(8,128)S(1)} %shard_map.117), channel_id=1, source_target_pairs={{0,32},{32,0},{64,96},{96,64},{128,160},{160,128},{192,224},{224,1... | collective-permute-start | bytes 12296 | tf_op jit(solution)/shard_map/ppermute | solution.py:304
  32.3 7.2 %collective-permute-start.6 = (f32[16,128]{1,0:T(8,128)S(1)}, f32[16,128]{1,0:T(8,128)S(1)}, u32[]{:S(2)}, u32[]{:S(2)}) collective-permute-start(f32[16,128]{1,0:T(8,128)S(1)} %pad_maximum_fusion.2), channel_id=1, source_target_pairs={{0,64},{32,96},{64,0},{96,32},{128,192},{160,224},{192,128},{224,1... | collective-permute-start | bytes 24584 | tf_op jit(solution)/shard_map/ppermute | solution.py:304
  39.5 14.6 %collective-permute-start.7 = (f32[32,128]{1,0:T(8,128)S(1)}, f32[32,128]{1,0:T(8,128)S(1)}, u32[]{:S(2)}, u32[]{:S(2)}) collective-permute-start(f32[32,128]{1,0:T(8,128)S(1)} %pad_maximum_fusion.1), channel_id=1, source_target_pairs={{0,128},{32,160},{64,192},{96,224},{128,0},{160,32},{192,64},{224,... | collective-permute-start | bytes 49160 | tf_op jit(solution)/shard_map/ppermute | solution.py:304

commit v2 on v0

v2 whole, which is shorter than its diff:
```python
import jax
import jax.numpy as jnp
import numpy as np
from jax import lax
from jax.experimental import pallas as pl
from jax.experimental.pallas import tpu as pltpu
from jax.sharding import PartitionSpec as P

F32 = jnp.float32
NF, ND = 18, 36
NB = NF * ND
TILES = ND // 2
ROWS = NB * 4
BORDER = 4 * ND

angles = (np.float32(2.0 * np.pi) * np.arange(ND, dtype=np.float32) / np.float32(ND)).astype(np.float32)
COS = np.cos(angles).astype(np.float32)
SIN = np.sin(angles).astype(np.float32)
WEST = [bool(c > 0) for c in COS]
WEST_TILES = [k for k in range(TILES) if WEST[2 * k] or WEST[2 * k + 1]]
EAST_TILES = [k for k in range(TILES) if not (WEST[2 * k] and WEST[2 * k + 1])]
LANES_F = 10
FREQS_V = 6

VM = pl.BlockSpec(memory_space=pltpu.VMEM)
HB = pl.BlockSpec(memory_space=pltpu.HBM)
ANY = pl.BlockSpec(memory_space=pl.ANY)
SM = pl.BlockSpec(memory_space=pltpu.SMEM)
PARAMS = pltpu.CompilerParams(vmem_limit_bytes=16 * 1024 * 1024)


def in_vmem(shape, dtype=F32):
    return pltpu.VMEM(shape, dtype)


def tile_iota(dim):
    return lax.broadcasted_iota(jnp.int32, (8, 128), dim)


def twice(x):
    return jnp.concatenate([x, x], 0)


CHUNK = 6


def pack_kernel(hbm_ref, e_ref, far_ref, near_ref, across_ref, inside_ref, sems):
    lane = tile_iota(1)
    odd_lat = lax.axis_index("lat") % 2 == 1
    odd_lon = lax.axis_index("lon") % 2 == 1
    up, down = 3, 72
    far, near = jnp.where(odd_lat, up, down), jnp.where(odd_lat, down, up)
    copies = []
    for c in range(NF // CHUNK):
        part = pl.ds(c * CHUNK * 144, CHUNK * 144)
        copies.append(pltpu.make_async_copy(hbm_ref.at[part], e_ref.at[part], sems.at[c]))
        copies[c].start()
    acc = [[jnp.zeros((8, 128), F32)] * 3, [jnp.zeros((8, 128), F32)] * 3]
    for f in range(NF):
        if f % CHUNK == 0:
            copies[f // CHUNK].wait()
        far_ref[f * 18 : f * 18 + 18, :] = e_ref[pl.ds(f * 144 + far, 18, stride=4), :]
        near_ref[f * 18 : f * 18 + 18, :] = e_ref[pl.ds(f * 144 + near, 18, stride=4), :]
        chunk = f // FREQS_V
        for side, tiles, col in ((0, WEST_TILES, 127), (1, EAST_TILES, 0)):
            for kk, k in enumerate(tiles):
                pos = (f % FREQS_V) * LANES_F + kk
                x = e_ref[(f * TILES + k) * 8 : (f * TILES + k) * 8 + 8, :]
                acc[side][chunk] = jnp.where(lane == pos, pltpu.roll(x, (pos - col) % 128, 1), acc[side][chunk])
    for chunk in range(3):
        across_ref[:, chunk * 128 : chunk * 128 + 128] = jnp.where(odd_lon, acc[0][chunk], acc[1][chunk])
        inside_ref[:, chunk * 128 : chunk * 128 + 128] = jnp.where(odd_lon, acc[1][chunk], acc[0][chunk])


EXT = 22 * ND
EXT_ROWS = EXT * 4
SUMS = 6


def table_kernel(
    gs_ref, mom_ref, prof_ref, coef_ref, mask_ref, wind_ref, cx_ref, cy_ref, w0_ref, w1_ref, pw_ref, half_ref, *zeros
):
    freq = lax.axis_index("freq")
    first = freq * NB
    low = tile_iota(0) < 4
    mask8 = twice(mask_ref[...].astype(F32))
    wind8 = twice(wind_ref[...]) * 0.5
    zero = jnp.zeros((8, 128), F32)

    def one_freq(f, _):
        speed = gs_ref[f] * mask8
        for k in range(TILES):
            at = pl.ds(pl.multiple_of(f * 144 + k * 8, 8), 8)
            b = first + f * ND + 2 * k
            p0, p1 = prof_ref[b], prof_ref[b + 1]
            cx_ref[at, :] = speed * jnp.where(low, float(abs(COS[2 * k])), float(abs(COS[2 * k + 1])))
            cy_ref[at, :] = speed * jnp.where(low, float(abs(SIN[2 * k])), float(abs(SIN[2 * k + 1])))
            pt = jnp.where(low, p0, p1)
            w0_ref[at, :] = pt * jnp.where(low, mom_ref[0, b], mom_ref[0, b + 1])
            w1_ref[at, :] = pt * jnp.where(low, mom_ref[1, b], mom_ref[1, b + 1])
            pw_ref[at, :] = wind8 * pt
        return 0

    lax.fori_loop(0, NF, one_freq, 0)

    def one_ext(f, _):
        for k in range(TILES):
            at = pl.ds(pl.multiple_of(f * 144 + k * 8, 8), 8)
            b = freq * (14 * ND) + f * ND + 2 * k
            half_ref[at, :] = jnp.where(low, 0.5 * coef_ref[b], 0.5 * coef_ref[b + 1])
            for z in zeros:
                z[at, :] = zero
        return 0

    lax.fori_loop(0, EXT // ND, one_ext, 0)


def move_kernel(
    e_ref, far_ref, near_ref, across_ref, inside_ref, mask_ref, wind_ref, cell_ref, cx_ref, cy_ref, w0_ref, w1_ref,
    moved_ref, big_ref, small_ref, own_ref, halo_ref, half_ref,
):
    lat, lon, freq = lax.axis_index("lat"), lax.axis_index("lon"), lax.axis_index("freq")
    lane, row = tile_iota(1), tile_iota(0)
    first, last = lane == 0, lane == 127
    low = row < 4
    top, bottom = row % 4 == 0, row % 4 == 3
    odd_lat, odd_lon = lat % 2 == 1, lon % 2 == 1
    south, north = 0, 75
    far, near = jnp.where(odd_lat, north, south), jnp.where(odd_lat, south, north)
    for f in range(NF):
        halo_ref[pl.ds(f * 144 + far, 18, stride=4), :] = far_ref[f * 18 : f * 18 + 18, :]
        halo_ref[pl.ds(f * 144 + near, 18, stride=4), :] = near_ref[f * 18 : f * 18 + 18, :]
    mask8 = twice(mask_ref[...].astype(F32))
    own = freq * (4 * BORDER)

    def some_freqs(c, carry):
        en, t0, t1 = carry
        across = across_ref[:, pl.ds(pl.multiple_of(c * 128, 128), 128)]
        inside = inside_ref[:, pl.ds(pl.multiple_of(c * 128, 128), 128)]
        hw, he = jnp.where(odd_lon, inside, across), jnp.where(odd_lon, across, inside)
        for f in range(FREQS_V):
            for k in range(TILES):
                at = pl.multiple_of((c * FREQS_V + f) * 144 + k * 8, 8)
                x = e_ref[pl.ds(at, 8), :]
                h = halo_ref[pl.ds(at, 8), :]
                west = east = None
                if k in WEST_TILES:
                    pos = f * LANES_F + WEST_TILES.index(k)
                    west = jnp.where(first, pltpu.roll(hw, (128 - pos) % 128, 1), pltpu.roll(x, 1, 1))
                if k in EAST_TILES:
                    pos = f * LANES_F + EAST_TILES.index(k)
                    east = jnp.where(last, pltpu.roll(he, 127 - pos, 1), pltpu.roll(x, 127, 1))
                if east is None:
                    side = west
                elif west is None:
                    side = east
                else:
                    side = jnp.where(low, west, east) if WEST[2 * k] else jnp.where(low, east, west)
                if k < TILES // 2:
                    beside = jnp.where(top, h, pltpu.roll(x, 1, 0))
                else:
                    beside = jnp.where(bottom, h, pltpu.roll(x, 7, 0))
                m = mask8 * x - cx_ref[pl.ds(at, 8), :] * (x - side) - cy_ref[pl.ds(at, 8), :] * (x - beside)
                moved_ref[pl.ds(pl.multiple_of(own + at, 8), 8), :] = m
                en = en + m
                t0 = t0 + m * w0_ref[pl.ds(at, 8), :]
                t1 = t1 + m * w1_ref[pl.ds(at, 8), :]
        return en, t0, t1

    zero = jnp.zeros((8, 128), F32)
    en, t0, t1 = lax.fori_loop(0, NF // FREQS_V, some_freqs, (zero, zero, zero))
    start = pl.multiple_of(own + (1 - freq) * (14 * 144), 8)
    for k in range(72):
        big_ref[k * 8 : k * 8 + 8, :] = moved_ref[pl.ds(start + k * 8, 8), :]
    wind = wind_ref[...]
    i4 = lax.broadcasted_iota(jnp.int32, (4, 128), 0) + lat * 4
    j4 = lax.broadcasted_iota(jnp.int32, (4, 128), 1) + lon * 128
    offset = cell_ref[...] - (j4 * 32 + i4)
    for c, t in enumerate((t0, t1)):
        tau = (t[0:4] + t[4:8]) * wind
        half_ref[8 * c : 8 * c + 8, :] = zero
        for d in (-1, 0, 1):
            half_ref[8 * c + 1 + d : 8 * c + 5 + d, :] += jnp.where(offset == d, tau, 0.0)
    r0, r1 = half_ref[0:8, :], half_ref[8:16, :]
    lower = jnp.where(lane < 64, r0, pltpu.roll(r1, 64, 1))
    upper = jnp.where(lane < 64, pltpu.roll(r0, 64, 1), r1)
    own_ref[0:8, :] = jnp.where(freq == 0, lower, upper)
    small_ref[0:8, :] = jnp.where(freq == 0, upper, lower)
    total = twice(en[0:4] + en[4:8])
    own_ref[8:16, :] = total
    small_ref[8:16, :] = total


def transfers(own, quads, m_ref, half_ref):
    q0, q1 = quads
    e, third, fourth = [m_ref[b] for b in own], [m_ref[b] for b in q0], [m_ref[b] for b in q1]
    half = [half_ref[b] for b in own]
    return [
        half[i] * (e[i] * (e[i] * (third[i] + fourth[i]) - 2.0 * third[i] * fourth[i])) for i in range(len(own))
    ]


def add_all(quads, t, refs):
    q0, q1 = quads
    n = range(len(t))
    up = [refs[i % 3][q0[i]] for i in n]
    down = [refs[3 + i % 3][q1[i]] for i in n]
    for i in n:
        refs[i % 3][q0[i]] = up[i] + t[i]
    for i in n:
        refs[3 + i % 3][q1[i]] = down[i] + t[i]


def inner_kernel(up_ref, down_ref, half_ref, m_ref, *rest):
    refs, t_ref = rest[SUMS : 2 * SUMS], rest[2 * SUMS]
    freq = lax.axis_index("freq")
    start = freq * (6 * ND)
    shift = freq * (14 * ND)

    def one_dir(d, _):
        own = [start + d + f * ND for f in range(16)]
        quads = [[ref[shift + b] - shift for b in own] for ref in (up_ref, down_ref)]
        t = transfers(own, quads, m_ref, half_ref)
        add_all(quads, t, refs)
        for b, x in zip(own, t):
            t_ref[b] = x
        return 0

    lax.fori_loop(0, ND, one_dir, 0)


def keep_of(mine_ref, theirs_ref, dis_ref):
    energy = (mine_ref[8:16, :] + theirs_ref[8:16, :]) * (1.0 / (2 * NB))
    return 1.0 - 0.5 * (twice(dis_ref[...]) * energy)


def finish(at, own, keep, m_ref, pw_ref, parts, t_ref):
    here = pl.ds(pl.multiple_of(at, 8), 8)
    total = parts[0][here, :]
    for part in parts[1:]:
        total = total + part[here, :]
    grown = m_ref[here, :] * (keep + pw_ref[pl.ds(pl.multiple_of(at - own, 8), 8), :])
    return grown + (total - 2.0 * t_ref[here, :])


PLAIN = 14 * 144


def plain_kernel(m_ref, pw_ref, *rest):
    parts, (t_ref, mine_ref, theirs_ref, dis_ref, hbm_ref, out_ref, sems) = rest[:SUMS], rest[SUMS:]
    freq = lax.axis_index("freq")
    own = freq * (4 * BORDER)
    start = freq * (8 * 144)
    keep = keep_of(mine_ref, theirs_ref, dis_ref)
    copies = []
    for c in range(2):
        def some(i, _):
            for u in range(TILES):
                to = c * (PLAIN // 2) + i * 144 + u * 8
                out_ref[pl.ds(pl.multiple_of(to, 8), 8), :] = finish(start + to, own, keep, m_ref, pw_ref, parts, t_ref)
            return 0

        lax.fori_loop(0, 7, some, 0)
        copies.append(
            pltpu.make_async_copy(
                out_ref.at[pl.ds(c * (PLAIN // 2), PLAIN // 2)],
                hbm_ref.at[pl.ds(pl.multiple_of(own + c * (PLAIN // 2), 8), PLAIN // 2)],
                sems.at[c],
            )
        )
        copies[c].start()
    for copy in copies:
        copy.wait()


def extend_kernel(up_ref, down_ref, half_ref, theirs_ref, *rest):
    m_ref, *refs, t_ref = rest[SUMS + 2 :]
    freq = lax.axis_index("freq")
    to = (1 - freq) * NB
    for k in range(BORDER):
        m_ref[to + k] = theirs_ref[k]
    shift = freq * (14 * ND)
    start = 16 * ND - shift

    def some(i, _):
        for u in range(2):
            own = [start + i * 2 + u + f * ND for f in range(4)]
            quads = [[ref[shift + b] - shift for b in own] for ref in (up_ref, down_ref)]
            t = transfers(own, quads, m_ref, half_ref)
            add_all(quads, t, refs)
            for b, x in zip(own, t):
                t_ref[b] = x
        return 0

    lax.fori_loop(0, ND // 2, some, 0)


def outer_kernel(m_ref, pw_ref, *rest):
    parts, (t_ref, mine_ref, theirs_ref, dis_ref, _, hbm_ref, out_ref, sem) = rest[:SUMS], rest[SUMS:]
    freq = lax.axis_index("freq")
    own = freq * (4 * BORDER)
    start = 14 * 144 - freq * (10 * 144)
    keep = keep_of(mine_ref, theirs_ref, dis_ref)
    for u in range(72):
        out_ref[u * 8 : u * 8 + 8, :] = finish(start + u * 8, own, keep, m_ref, pw_ref, parts, t_ref)
    copy = pltpu.make_async_copy(
        out_ref, hbm_ref.at[pl.ds(pl.multiple_of((1 - freq) * (14 * 144), 8), 4 * BORDER)], sem
    )
    copy.start()
    copy.wait()


def cells_kernel(r_ref, out_ref, z_ref, t_ref):
    lat = lax.axis_index("lat")
    z_ref[...] = jnp.zeros_like(z_ref)
    for k in range(8):
        block = r_ref[pl.ds(pl.multiple_of(jnp.bitwise_xor(lat, k) * 8, 8), 8), :]
        z_ref[7 + 4 * k : 13 + 4 * k, :] += block[0:6]
    t_ref[:, 0:32] = jnp.transpose(z_ref[8:40, :])
    t_ref[:, 32:128] = jnp.zeros((128, 96), F32)
    out = jnp.zeros((32, 128), F32)
    for jj in range(4):
        piece = t_ref[pl.ds(jj, 32, stride=4), :]
        out = out + pltpu.roll(piece, jj * 32, 1)
    for c in range(2):
        for g in range(16):
            out_ref[c : c + 1, g * 128 : g * 128 + 128] = out[c * 16 + g : c * 16 + g + 1, :]


def call(kernel, out, in_specs, scratch=(), out_specs=None, us=1.0, aliases=None):
    return pl.pallas_call(
        kernel,
        out_shape=out,
        in_specs=in_specs,
        out_specs=jax.tree.map(lambda _: VM, out) if out_specs is None else out_specs,
        scratch_shapes=list(scratch),
        compiler_params=PARAMS,
        input_output_aliases=aliases or {},
        cost_estimate=pl.CostEstimate(flops=0, transcendentals=0, bytes_accessed=int(us * 3.0e6)),
    )


def local(
    spectrum, group_speed, sea_mask, wind_growth, dissipation, wind_profile, nonlinear_coef, momentum, quadruplet,
    ocean_cell,
):
    grid = in_vmem((ROWS, 128))
    halo = in_vmem((NF * 18, 128))
    edge = in_vmem((8, 384))
    flat, far, near, across, inside = call(
        pack_kernel, (grid, halo, halo, edge, edge), [HB], [pltpu.SemaphoreType.DMA((NF // CHUNK,))]
    )(pltpu.with_memory_space_constraint(spectrum.reshape(ROWS, 128), pltpu.HBM))
    nlat, nlon = lax.axis_size("lat"), lax.axis_size("lon")

    def pairs(first, count, size):
        both = [(i, (i + 1) % size) for i in range(first, first + 2 * count, 2)]
        return both + [(j, i) for i, j in both]

    swap = pairs(0, 1, 2)
    far = lax.ppermute(far, "lat", pairs(1, nlat // 2 - 1, nlat))
    near = lax.ppermute(near, "lat", pairs(0, nlat // 2, nlat))
    across = lax.ppermute(across, "lon", pairs(1, nlon // 2, nlon))
    inside = lax.ppermute(inside, "lon", pairs(0, nlon // 2, nlon))
    wide = in_vmem((EXT_ROWS, 128))
    cx, cy, w0, w1, pw, half, *zeros = call(table_kernel, (grid,) * 5 + (wide,) * (1 + SUMS), [SM] * 4 + [VM] * 2, us=4.0)(
        group_speed, momentum, wind_profile, nonlinear_coef, sea_mask, wind_growth
    )
    quads = [jnp.maximum(quadruplet[r], 0) for r in range(2)]
    sums = in_vmem((16, 128))
    moved, big, small, own = call(
        move_kernel,
        (wide, in_vmem((4 * BORDER, 128)), sums, sums),
        [VM] * 12,
        [pltpu.VMEM((ROWS, 128), F32), pltpu.VMEM((16, 128), F32)],
    )(
        flat, far, near, across, inside, sea_mask, wind_growth, ocean_cell, cx, cy, w0, w1
    )
    their_small = lax.ppermute(small, "freq", swap)
    theirs = lax.ppermute(big, "freq", swap)
    as_bins = lambda x: x.reshape(-1, 4, 128)
    as_rows = lambda x: x.reshape(-1, 128)
    acc = in_vmem((EXT, 4, 128))
    half = as_bins(half)
    parts = call(
        inner_kernel,
        (acc,) * (SUMS + 1),
        [SM] * 2 + [VM] * (2 + SUMS),
        us=3.0,
        aliases={4 + i: i for i in range(SUMS)},
    )(*quads, half, as_bins(moved), *map(as_bins, zeros))

    def gather(rows, bit):
        return lax.ppermute(rows, "lat", [(i, i ^ bit) for i in range(nlat)])

    their_small, *parts = lax.optimization_barrier((their_small, *parts))
    rows = own[0:8] + their_small[0:8]
    other = gather(rows, 1)
    whole = jax.ShapeDtypeStruct((ROWS, 128), F32)
    plain = call(
        plain_kernel,
        whole,
        [VM] * (6 + SUMS),
        [pltpu.VMEM((PLAIN, 128), F32), pltpu.SemaphoreType.DMA((2,))],
        out_specs=ANY,
        us=2.0,
    )(moved, pw, *map(as_rows, parts), own, their_small, dissipation)
    other, plain = lax.optimization_barrier((other, plain))
    rows = jnp.concatenate([rows, other], 0)
    other = gather(rows, 2)
    theirs, rows = lax.optimization_barrier((theirs, rows))
    extended = call(
        extend_kernel,
        (acc,) * (SUMS + 2),
        [SM] * 2 + [VM] * (4 + SUMS),
        us=1.5,
        aliases={4 + i: i for i in range(SUMS + 2)},
    )(*quads, half, as_bins(theirs), as_bins(moved), *parts)
    other, *extended = lax.optimization_barrier((other, *extended))
    rows = jnp.concatenate([rows, other], 0)
    other = gather(rows, 4)
    rows = jnp.concatenate([rows, other], 0)
    out = call(
        outer_kernel,
        whole,
        [VM] * (6 + SUMS) + [ANY],
        [pltpu.VMEM((4 * BORDER, 128), F32), pltpu.SemaphoreType.DMA(())],
        out_specs=ANY,
        us=1.0,
        aliases={6 + SUMS: 0},
    )(as_rows(extended[0]), pw, *map(as_rows, extended[1:]), own, their_small, dissipation, plain)
    stress = call(
        cells_kernel,
        jax.ShapeDtypeStruct((2, 2048), F32),
        [VM],
        [pltpu.VMEM((48, 128), F32), pltpu.VMEM((128, 128), F32)],
    )(rows)
    return out.reshape(spectrum.shape), stress.T


def solution(mesh):
    return jax.shard_map(
        local,
        mesh=mesh,
        in_specs=(
            P("freq", None, "lat", "lon"),
            P("freq"),
            P("lat", "lon"),
            P("lat", "lon"),
            P("lat", "lon"),
            P(),
            P(),
            P(),
            P(),
            P("lat", "lon"),
        ),
        out_specs=(P("freq", None, "lat", "lon"), P(("lon", "freq"), None)),
        check_vma=False,
    )
```

time: 133 us -> 44.5 us (0.33)
  the two profiles are of different devices: /device:TPU:8 before, /device:TPU:14 now
where the time goes in v2:
time: 44.5 us; the launch traced here: 44.1 us
  Pallas kernels  15.2 us (34%)
  starting transfers between devices  13.6 us (31%)
  waiting for transfers between devices  9.6 us (22%)
  local copies, waits for them, and re-layouts  4.8 us (11%)
  between operations  0.78 us (2%)
    ppermute x3, waiting for transfers between devices, gather(): return lax.ppermute(rows, 'lat', [(i, i ^ bit) for i in range(nlat)])  9.39 us
    unnamed x18, local copies, waits for them, and re-layouts  4.8 us
    ppermute x1, starting transfers between devices, local(): across = lax.ppermute(across, 'lon', pairs(1, nlon // 2, nlon))  4.74 us
    pallas_call x1, Pallas kernels, local(): call(table_kernel, (grid,) * 5 + (wide,) * (1 + SUMS), [SM] * 4 + [VM] *...  3.88 us
    pallas_call x1, Pallas kernels, local(): call(inner_kernel, (acc,) * (SUMS + 1), [SM] * 2 + [VM] * (2 + SUMS), us=...  3.58 us
    ppermute x1, starting transfers between devices, local(): far = lax.ppermute(far, 'lat', pairs(1, nlat // 2 - 1, nlat))  3.48 us
    ppermute x1, starting transfers between devices, local(): near = lax.ppermute(near, 'lat', pairs(0, nlat // 2, nlat))  2.82 us
    ppermute x1, starting transfers between devices, local(): theirs = lax.ppermute(big, 'freq', swap)  2.09 us
  transfers between devices with their start and end apart: 9, of which 4 were waited for; matrix products, arithmetic and copies ran while one was open for 0% of the time, Pallas kernels for 26%

profile of v2, /device:TPU:14, one launch (start us, length us, event | category | flops | bytes accessed | tf_op | source)
XLA Modules:
  0.0 44.1 jit_solution(1507660452039852174)
XLA Ops:
  0.6 1.6 %shard_map.113 = (f32[2592,128]{1,0:T(8,128)S(1)}, f32[324,128]{1,0:T(8,128)S(1)}, f32[324,128]{1,0:T(8,128)S(1)}, f32[8,384]{1,0:T(8,128)S(1)}, f32[8,384]{1,0:T(8,128)S(1)}) custom-call(f32[2592,128]{1,0:T(8,128)} %bitcast.54), custom_call_target="tpu_custom_call" | custom-call | bytes 3000000 | tf_op jit(solution)/shard_map/pallas_call | solution.py:350
  2.3 3.5 %collective-permute-start = (f32[324,128]{1,0:T(8,128)S(1)}, f32[324,128]{1,0:T(8,128)S(1)}, u32[]{:S(2)}, u32[]{:S(2)}) collective-permute-start(f32[324,128]{1,0:T(8,128)S(1)} %get-tuple-element.60), channel_id=1, source_target_pairs={{32,64},{96,128},{160,192},{64,32},{128,96},{192,160},{33,65},{97,... | collective-permute-start | bytes 497672 | tf_op jit(solution)/shard_map/ppermute | solution.py:360
  5.8 2.8 %collective-permute-start.1 = (f32[324,128]{1,0:T(8,128)S(1)}, f32[324,128]{1,0:T(8,128)S(1)}, u32[]{:S(2)}, u32[]{:S(2)}) collective-permute-start(f32[324,128]{1,0:T(8,128)S(1)} %get-tuple-element.61), channel_id=1, source_target_pairs={{0,32},{64,96},{128,160},{192,224},{32,0},{96,64},{160,128},{224,1... | collective-permute-start | bytes 497672 | tf_op jit(solution)/shard_map/ppermute | solution.py:361
  8.6 4.7 %collective-permute-start.2 = (f32[8,384]{1,0:T(8,128)S(1)}, f32[8,384]{1,0:T(8,128)S(1)}, u32[]{:S(2)}, u32[]{:S(2)}) collective-permute-start(f32[8,384]{1,0:T(8,128)S(1)} %get-tuple-element.62), channel_id=1, source_target_pairs={{2,4},{6,8},{10,12},{14,16},{18,20},{22,24},{26,28},{30,0},{4,2},{... | collective-permute-start | bytes 36872 | tf_op jit(solution)/shard_map/ppermute | solution.py:362
  13.3 0.0 collective-permute-start.3
  13.3 0.0 copy-start
  13.3 0.7 %copy-done = f32[2,1296]{1,0:T(2,128)S(1)} copy-done((f32[2,1296]{1,0:T(2,128)S(1)}, f32[2,1296]{1,0:T(2,128)}, u32[]{:S(2)}) %copy-start) | copy-done | bytes 10392
  14.0 0.0 copy-start.2
  14.0 0.7 %copy-done.2 = s32[4,128]{1,0:T(4,128)S(1)} copy-done((s32[4,128]{1,0:T(4,128)S(1)}, s32[4,128]{1,0:T(4,128)}, u32[]{:S(2)}) %copy-start.2) | copy-done | bytes 2072
  14.7 0.0 copy-start.3
  14.7 0.7 %copy-done.3 = f32[4,128]{1,0:T(4,128)S(1)} copy-done((f32[4,128]{1,0:T(4,128)S(1)}, f32[4,128]{1,0:T(4,128)}, u32[]{:S(2)}) %copy-start.3) | copy-done | bytes 2072
  15.4 0.0 copy-start.4
  15.4 0.7 %copy-done.4 = f32[1296]{0:T(1024)S(1)} copy-done((f32[1296]{0:T(1024)S(1)}, f32[1296]{0:T(1024)}, u32[]{:S(2)}) %copy-start.4) | copy-done | bytes 5208
  16.1 0.0 copy-start.5
  16.1 0.7 %copy-done.5 = f32[1296]{0:T(1024)S(1)} copy-done((f32[1296]{0:T(1024)S(1)}, f32[1296]{0:T(1024)}, u32[]{:S(2)}) %copy-start.5) | copy-done | bytes 5208
  16.8 0.0 copy-start.7
  16.8 0.7 %copy-done.7 = f32[18]{0:T(128)S(1)} copy-done((f32[18]{0:T(128)S(1)}, f32[18]{0:T(128)}, u32[]{:S(2)}) %copy-start.7) | copy-done | bytes 96
  17.4 3.9 %shard_map.114 = (f32[2592,128]{1,0:T(8,128)S(1)}, f32[2592,128]{1,0:T(8,128)S(1)}, f32[2592,128]{1,0:T(8,128)S(1)}, f32[2592,128]{1,0:T(8,128)S(1)}, f32[2592,1...) custom-call(f32[18]{0:T(128)S(1)} %copy-done.7, ...), custom_call_target="tpu_custom_call" | custom-call | bytes 12000000 | tf_op jit(solution)/shard_map/pallas_call | solution.py:365
  21.3 0.0 collective-permute-done.2.across_ref
  21.3 0.0 collective-permute-done.3.inside_ref
  21.4 0.0 collective-permute-done.far_ref
  21.4 0.0 collective-permute-done.1.near_ref
  21.4 0.0 copy-start.6
  21.4 0.7 %copy-done.6 = s32[4,128]{1,0:T(4,128)S(1)} copy-done((s32[4,128]{1,0:T(4,128)S(1)}, s32[4,128]{1,0:T(4,128)}, u32[]{:S(2)}) %copy-start.6) | copy-done | bytes 2072
  22.1 0.0 copy-start.8
  22.1 1.3 %shard_map.115 = (f32[3168,128]{1,0:T(8,128)S(1)}, f32[576,128]{1,0:T(8,128)S(1)}, f32[16,128]{1,0:T(8,128)S(1)}, f32[16,128]{1,0:T(8,128)S(1)}) custom-call(f32[2592,128]{1,0:T(8,128)S(1)} %get-tuple-element.59.e_ref, f32[324,128]{1,0:T(8,128)S(1)} %collective-permute-done.far_ref, f32[324,128]{1,0:T(8,128)S(1)} %collective-permute-done.1.near_ref, ...), custom_call_target="tpu_custom_call" | custom-call | bytes 3000000 | tf_op jit(solution)/shard_map/pallas_call | solution.py:370
  23.3 0.0 collective-permute-start.4
  23.4 0.0 copy-done.8
  23.4 2.1 %collective-permute-start.7 = (f32[576,128]{1,0:T(8,128)S(1)}, f32[576,128]{1,0:T(8,128)S(1)}, u32[]{:S(2)}, u32[]{:S(2)}) collective-permute-start(f32[576,128]{1,0:T(8,128)S(1)} %get-tuple-element.95), channel_id=1, source_target_pairs={{0,1},{1,0},{2,3},{3,2},{4,5},{5,4},{6,7},{7,6},{8,9},{9,8},{10,11... | collective-permute-start | bytes 884744 | tf_op jit(solution)/shard_map/ppermute | solution.py:379
  25.5 0.0 copy-start.1
  25.5 3.6 %shard_map.116 = (f32[792,4,128]{2,1,0:T(4,128)S(1)}, f32[792,4,128]{2,1,0:T(4,128)S(1)}, f32[792,4,128]{2,1,0:T(4,128)S(1)}, f32[792,4,128]{2,1,0:T(4,128)S(1)}...) custom-call(s32[1296]{0:T(1024)S(1)} %get-tuple-element.117.up_ref, ...), custom_call_target="tpu_custom_call", output_to_operand_aliasing={{0}: (4, {}), {1}: (5, {}), {2}: (6, {}), {3}: (7, {}), {4}... | custom-call | bytes 9000000 | tf_op jit(solution)/shard_map/pallas_call | solution.py:384
  29.1 0.0 collective-permute-done.4.rest_8_
  29.1 0.5 %collective-permute-start.5 = (f32[8,128]{1,0:T(8,128)S(1)}, f32[8,128]{1,0:T(8,128)S(1)}, u32[]{:S(2)}, u32[]{:S(2)}) collective-permute-start(f32[8,128]{1,0:T(8,128)S(1)} %slice_add_fusion), channel_id=1, source_target_pairs={{0,32},{32,0},{64,96},{96,64},{128,160},{160,128},{192,224},{224,1... | collective-permute-start | bytes 12296 | tf_op jit(solution)/shard_map/ppermute | solution.py:393
  29.6 0.0 copy-done.1
  29.6 1.5 %shard_map.117.rest_10_ = f32[2592,128]{1,0:T(8,128)} custom-call(f32[3168,128]{1,0:T(8,128)S(1)} %get-tuple-element.71.m_ref, f32[2592,128]{1,0:T(8,128)S(1)} %get-tuple-element.86.pw_ref, f32[3168,128]{1,0:T(8,128)S(1)} %bitcast.31, f32[3168,128]{1,0:T(8,128)S(1)} %bitcast.34, f32[3168,128]{1,0:T(8,128)S(1)} %bitcast.37, f32[3168,128]{1,0:T(8,128)S(1)} %bitcast.40, ...), custom_call_target="tpu_custom_call" | custom-call | bytes 6000000 | tf_op jit(solution)/shard_map/pallas_call | solution.py:399
  31.1 1.7 %collective-permute-done.5 = f32[8,128]{1,0:T(8,128)S(1)} collective-permute-done((f32[8,128]{1,0:T(8,128)S(1)}, f32[8,128]{1,0:T(8,128)S(1)}, u32[]{:S(2)}, u32[]{:S(2)}) %collective-permute-start.5) | collective-permute-done | bytes 4128 | tf_op jit(solution)/shard_map/ppermute | solution.py:393
  32.8 0.0 collective-permute-start.6
  32.8 0.2 collective-permute-done.7
  33.0 1.4 %shard_map.118 = (f32[792,4,128]{2,1,0:T(4,128)S(1)}, f32[792,4,128]{2,1,0:T(4,128)S(1)}, f32[792,4,128]{2,1,0:T(4,128)S(1)}, f32[792,4,128]{2,1,0:T(4,128)S(1)}...) custom-call(s32[1296]{0:T(1024)S(1)} %get-tuple-element.117.up_ref, ...), custom_call_target="tpu_custom_call", output_to_operand_aliasing={{0}: (4, {}), {1}: (5, {}), {2}: (6, {}), {3}: (7, {}), {4}... | custom-call | bytes 4500000 | tf_op jit(solution)/shard_map/pallas_call | solution.py:411
  34.5 3.5 %collective-permute-done.6 = f32[16,128]{1,0:T(8,128)S(1)} collective-permute-done((f32[16,128]{1,0:T(8,128)S(1)}, f32[16,128]{1,0:T(8,128)S(1)}, u32[]{:S(2)}, u32[]{:S(2)}) %collective-permute-start.6) | collective-permute-done | bytes 8224 | tf_op jit(solution)/shard_map/ppermute | solution.py:393
  38.0 0.0 collective-permute-start.8
  38.0 1.1 %shard_map.119 = f32[2592,128]{1,0:T(8,128)} custom-call(f32[3168,128]{1,0:T(8,128)S(1)} %bitcast.29, f32[2592,128]{1,0:T(8,128)S(1)} %get-tuple-element.86.pw_ref, f32[3168,128]{1,0:T(8,128)S(1)} %bitcast.32, f32[3168,128]{1,0:T(8,128)S(1)} %bitcast.35, f32[3168,128]{1,0:T(8,128)S(1)} %bitcast.38, ...), custom_call_target="tpu_custom_call", output_to_operand_aliasing={{}: (12, {})} | custom-call | bytes 3000000 | tf_op jit(solution)/shard_map/pallas_call | solution.py:422
  39.1 4.2 %collective-permute-done.8 = f32[32,128]{1,0:T(8,128)S(1)} collective-permute-done((f32[32,128]{1,0:T(8,128)S(1)}, f32[32,128]{1,0:T(8,128)S(1)}, u32[]{:S(2)}, u32[]{:S(2)}) %collective-permute-start.8) | collective-permute-done | bytes 16416 | tf_op jit(solution)/shard_map/ppermute | solution.py:393
  43.2 0.8 %shard_map.120 = f32[2,2048]{1,0:T(2,128)} custom-call(f32[64,128]{1,0:T(8,128)S(1)} %pad_maximum_fusion.r_ref), custom_call_target="tpu_custom_call" | custom-call | bytes 3000000 | tf_op jit(solution)/shard_map/pallas_call | solution.py:431
  (5 shorter events, 0.1 us)
Async XLA Ops:
  2.3 19.1 %collective-permute-start = (f32[324,128]{1,0:T(8,128)S(1)}, f32[324,128]{1,0:T(8,128)S(1)}, u32[]{:S(2)}, u32[]{:S(2)}) collective-permute-start(f32[324,128]{1,0:T(8,128)S(1)} %get-tuple-element.60), channel_id=1, source_target_pairs={{32,64},{96,128},{160,192},{64,32},{128,96},{192,160},{33,65},{97,... | collective-permute-start | bytes 497672 | tf_op jit(solution)/shard_map/ppermute | solution.py:360
  5.8 15.6 %collective-permute-start.1 = (f32[324,128]{1,0:T(8,128)S(1)}, f32[324,128]{1,0:T(8,128)S(1)}, u32[]{:S(2)}, u32[]{:S(2)}) collective-permute-start(f32[324,128]{1,0:T(8,128)S(1)} %get-tuple-element.61), channel_id=1, source_target_pairs={{0,32},{64,96},{128,160},{192,224},{32,0},{96,64},{160,128},{224,1... | collective-permute-start | bytes 497672 | tf_op jit(solution)/shard_map/ppermute | solution.py:361
  8.6 12.8 %collective-permute-start.2 = (f32[8,384]{1,0:T(8,128)S(1)}, f32[8,384]{1,0:T(8,128)S(1)}, u32[]{:S(2)}, u32[]{:S(2)}) collective-permute-start(f32[8,384]{1,0:T(8,128)S(1)} %get-tuple-element.62), channel_id=1, source_target_pairs={{2,4},{6,8},{10,12},{14,16},{18,20},{22,24},{26,28},{30,0},{4,2},{... | collective-permute-start | bytes 36872 | tf_op jit(solution)/shard_map/ppermute | solution.py:362
  13.3 8.0 %collective-permute-start.3 = (f32[8,384]{1,0:T(8,128)S(1)}, f32[8,384]{1,0:T(8,128)S(1)}, u32[]{:S(2)}, u32[]{:S(2)}) collective-permute-start(f32[8,384]{1,0:T(8,128)S(1)} %get-tuple-element.63), channel_id=1, source_target_pairs={{0,2},{4,6},{8,10},{12,14},{16,18},{20,22},{24,26},{28,30},{2,0},{... | collective-permute-start | bytes 36872 | tf_op jit(solution)/shard_map/ppermute | solution.py:363
  13.3 0.7 %copy-start = (f32[2,1296]{1,0:T(2,128)S(1)}, f32[2,1296]{1,0:T(2,128)}, u32[]{:S(2)}) copy-start(f32[2,1296]{1,0:T(2,128)} %mom_ref.1) | copy-start | bytes 31108
  14.0 0.7 %copy-start.2 = (s32[4,128]{1,0:T(4,128)S(1)}, s32[4,128]{1,0:T(4,128)}, u32[]{:S(2)}) copy-start(s32[4,128]{1,0:T(4,128)} %mask_ref.3) | copy-start | bytes 6148
  14.7 0.7 %copy-start.3 = (f32[4,128]{1,0:T(4,128)S(1)}, f32[4,128]{1,0:T(4,128)}, u32[]{:S(2)}) copy-start(f32[4,128]{1,0:T(4,128)} %wind_ref.3) | copy-start | bytes 6148
  15.4 0.7 %copy-start.4 = (f32[1296]{0:T(1024)S(1)}, f32[1296]{0:T(1024)}, u32[]{:S(2)}) copy-start(f32[1296]{0:T(1024)} %prof_ref.1) | copy-start | bytes 15556
  16.1 0.7 %copy-start.5 = (f32[1296]{0:T(1024)S(1)}, f32[1296]{0:T(1024)}, u32[]{:S(2)}) copy-start(f32[1296]{0:T(1024)} %coef_ref.1) | copy-start | bytes 15556
  16.8 0.7 %copy-start.7 = (f32[18]{0:T(128)S(1)}, f32[18]{0:T(128)}, u32[]{:S(2)}) copy-start(f32[18]{0:T(128)} %gs_ref.1) | copy-start | bytes 220
  21.4 0.7 %copy-start.6 = (s32[4,128]{1,0:T(4,128)S(1)}, s32[4,128]{1,0:T(4,128)}, u32[]{:S(2)}) copy-start(s32[4,128]{1,0:T(4,128)} %cell_ref.1) | copy-start | bytes 6148
  22.1 1.3 %copy-start.8 = (s32[2,1296]{1,0:T(2,128)S(1)}, s32[2,1296]{1,0:T(2,128)}, u32[]{:S(2)}) copy-start(s32[2,1296]{1,0:T(2,128)} %param.18) | copy-start | bytes 31108
  23.3 5.8 %collective-permute-start.4 = (f32[16,128]{1,0:T(8,128)S(1)}, f32[16,128]{1,0:T(8,128)S(1)}, u32[]{:S(2)}, u32[]{:S(2)}) collective-permute-start(f32[16,128]{1,0:T(8,128)S(1)} %get-tuple-element.69), channel_id=1, source_target_pairs={{0,1},{1,0},{2,3},{3,2},{4,5},{5,4},{6,7},{7,6},{8,9},{9,8},{10,11... | collective-permute-start | bytes 24584 | tf_op jit(solution)/shard_map/ppermute | solution.py:378
  23.4 9.6 %collective-permute-start.7 = (f32[576,128]{1,0:T(8,128)S(1)}, f32[576,128]{1,0:T(8,128)S(1)}, u32[]{:S(2)}, u32[]{:S(2)}) collective-permute-start(f32[576,128]{1,0:T(8,128)S(1)} %get-tuple-element.95), channel_id=1, source_target_pairs={{0,1},{1,0},{2,3},{3,2},{4,5},{5,4},{6,7},{7,6},{8,9},{9,8},{10,11... | collective-permute-start | bytes 884744 | tf_op jit(solution)/shard_map/ppermute | solution.py:379
  25.5 4.1 %copy-start.1 = (f32[4,128]{1,0:T(4,128)S(1)}, f32[4,128]{1,0:T(4,128)}, u32[]{:S(2)}) copy-start(f32[4,128]{1,0:T(4,128)} %rest_9_.3) | copy-start | bytes 6148
  29.1 3.7 %collective-permute-start.5 = (f32[8,128]{1,0:T(8,128)S(1)}, f32[8,128]{1,0:T(8,128)S(1)}, u32[]{:S(2)}, u32[]{:S(2)}) collective-permute-start(f32[8,128]{1,0:T(8,128)S(1)} %slice_add_fusion), channel_id=1, source_target_pairs={{0,32},{32,0},{64,96},{96,64},{128,160},{160,128},{192,224},{224,1... | collective-permute-start | bytes 12296 | tf_op jit(solution)/shard_map/ppermute | solution.py:393
  32.8 5.2 %collective-permute-start.6 = (f32[16,128]{1,0:T(8,128)S(1)}, f32[16,128]{1,0:T(8,128)S(1)}, u32[]{:S(2)}, u32[]{:S(2)}) collective-permute-start(f32[16,128]{1,0:T(8,128)S(1)} %pad_maximum_fusion.2), channel_id=1, source_target_pairs={{0,64},{32,96},{64,0},{96,32},{128,192},{160,224},{192,128},{224,1... | collective-permute-start | bytes 24584 | tf_op jit(solution)/shard_map/ppermute | solution.py:393
  38.0 5.2 %collective-permute-start.8 = (f32[32,128]{1,0:T(8,128)S(1)}, f32[32,128]{1,0:T(8,128)S(1)}, u32[]{:S(2)}, u32[]{:S(2)}) collective-permute-start(f32[32,128]{1,0:T(8,128)S(1)} %pad_maximum_fusion.1), channel_id=1, source_target_pairs={{0,128},{32,160},{64,192},{96,224},{128,0},{160,32},{192,64},{224,... | collective-permute-start | bytes 49160 | tf_op jit(solution)/shard_map/ppermute | solution.py:393

commit v3 on v2

v3 whole, which is shorter than its diff:
```python
import functools

import jax
import jax.numpy as jnp
import numpy as np
from jax import lax
from jax.experimental import pallas as pl
from jax.experimental.pallas import tpu as pltpu
from jax.sharding import PartitionSpec as P

F32 = jnp.float32
NF, ND = 18, 36
NB = NF * ND
TILES = ND // 2
ROWS = NB * 4
BORDER = 4 * ND

angles = (np.float32(2.0 * np.pi) * np.arange(ND, dtype=np.float32) / np.float32(ND)).astype(np.float32)
COS = np.cos(angles).astype(np.float32)
SIN = np.sin(angles).astype(np.float32)
WEST = [bool(c > 0) for c in COS]
WEST_TILES = [k for k in range(TILES) if WEST[2 * k] or WEST[2 * k + 1]]
EAST_TILES = [k for k in range(TILES) if not (WEST[2 * k] and WEST[2 * k + 1])]
LANES_F = 10
FREQS_V = 6

VM = pl.BlockSpec(memory_space=pltpu.VMEM)
HB = pl.BlockSpec(memory_space=pltpu.HBM)
ANY = pl.BlockSpec(memory_space=pl.ANY)
SM = pl.BlockSpec(memory_space=pltpu.SMEM)
PARAMS = pltpu.CompilerParams(vmem_limit_bytes=16 * 1024 * 1024)


def in_vmem(shape, dtype=F32):
    return pltpu.VMEM(shape, dtype)


def tile_iota(dim):
    return lax.broadcasted_iota(jnp.int32, (8, 128), dim)


def twice(x):
    return jnp.concatenate([x, x], 0)


EXT = 22 * ND
EXT_ROWS = EXT * 4
SUMS = 6
EARLY = 4


def clear(refs, own):
    zero = jnp.zeros((8, 128), F32)

    def one_freq(f, _):
        for k in range(TILES):
            for ref in refs:
                ref[pl.ds(pl.multiple_of(own + f * 144 + k * 8, 8), 8), :] = zero
        return 0

    lax.fori_loop(0, NF, one_freq, 0)


CHUNK = 6


def pack_kernel(hbm_ref, e_ref, raw_ref, far_ref, near_ref, across_ref, inside_ref, *rest):
    *zeros, sems = rest
    lane = tile_iota(1)
    odd_lat = lax.axis_index("lat") % 2 == 1
    odd_lon = lax.axis_index("lon") % 2 == 1
    up, down = 3, 72
    far, near = jnp.where(odd_lat, up, down), jnp.where(odd_lat, down, up)
    copies = []
    for c in range(NF // CHUNK):
        part = pl.ds(c * CHUNK * 144, CHUNK * 144)
        copies.append(pltpu.make_async_copy(hbm_ref.at[part], e_ref.at[part], sems.at[c]))
        copies[c].start()
    clear(zeros, lax.axis_index("freq") * (4 * BORDER))
    acc = [[jnp.zeros((8, 128), F32)] * 3, [jnp.zeros((8, 128), F32)] * 3]
    for f in range(NF):
        if f % CHUNK == 0:
            copies[f // CHUNK].wait()
        far_ref[f * 18 : f * 18 + 18, :] = e_ref[pl.ds(f * 144 + far, 18, stride=4), :]
        near_ref[f * 18 : f * 18 + 18, :] = e_ref[pl.ds(f * 144 + near, 18, stride=4), :]
        chunk = f // FREQS_V
        for side, tiles, col in ((0, WEST_TILES, 127), (1, EAST_TILES, 0)):
            for kk, k in enumerate(tiles):
                pos = (f % FREQS_V) * LANES_F + kk
                x = e_ref[(f * TILES + k) * 8 : (f * TILES + k) * 8 + 8, :]
                acc[side][chunk] = jnp.where(lane == pos, pltpu.roll(x, (pos - col) % 128, 1), acc[side][chunk])
    start = pl.multiple_of((1 - lax.axis_index("freq")) * (14 * 144), 8)
    for k in range(72):
        raw_ref[k * 8 : k * 8 + 8, :] = e_ref[pl.ds(start + k * 8, 8), :]
    for chunk in range(3):
        across_ref[:, chunk * 128 : chunk * 128 + 128] = jnp.where(odd_lon, acc[0][chunk], acc[1][chunk])
        inside_ref[:, chunk * 128 : chunk * 128 + 128] = jnp.where(odd_lon, acc[1][chunk], acc[0][chunk])


def table_kernel(gs_ref, mom_ref, prof_ref, mask_ref, cx_ref, cy_ref, w0_ref, w1_ref, speed_ref):
    freq = lax.axis_index("freq")
    first = freq * NB
    low = tile_iota(0) < 4
    mask8 = twice(mask_ref[...].astype(F32))
    for f in range(4):
        speed_ref[f * 8 : f * 8 + 8, :] = jnp.full((8, 128), gs_ref[(1 - freq) * 14 + f])

    def one_freq(f, _):
        speed = gs_ref[f] * mask8
        for k in range(TILES):
            at = pl.ds(pl.multiple_of(f * 144 + k * 8, 8), 8)
            b = first + f * ND + 2 * k
            cx_ref[at, :] = speed * jnp.where(low, float(abs(COS[2 * k])), float(abs(COS[2 * k + 1])))
            cy_ref[at, :] = speed * jnp.where(low, float(abs(SIN[2 * k])), float(abs(SIN[2 * k + 1])))
            pt = jnp.where(low, prof_ref[b], prof_ref[b + 1])
            w0_ref[at, :] = pt * jnp.where(low, mom_ref[0, b], mom_ref[0, b + 1])
            w1_ref[at, :] = pt * jnp.where(low, mom_ref[1, b], mom_ref[1, b + 1])
        return 0

    lax.fori_loop(0, NF, one_freq, 0)


def input_kernel(prof_ref, wind_ref, _, pw_ref):
    freq = lax.axis_index("freq")
    low = tile_iota(0) < 4
    wind8 = twice(wind_ref[...]) * 0.5

    def one_freq(f, _):
        for k in range(TILES):
            at = pl.ds(pl.multiple_of(f * 144 + k * 8, 8), 8)
            b = freq * NB + f * ND + 2 * k
            pw_ref[at, :] = wind8 * jnp.where(low, prof_ref[b], prof_ref[b + 1])
        return 0

    lax.fori_loop(0, NF, one_freq, 0)


def half_kernel(coef_ref, _, half_ref, *zeros):
    freq = lax.axis_index("freq")
    low = tile_iota(0) < 4

    def one_freq(f, _):
        for k in range(TILES):
            b = freq * (2 * ND) + f * ND + 2 * k
            at = pl.ds(pl.multiple_of(b * 4, 8), 8)
            b = freq * (14 * ND) + b
            half_ref[at, :] = jnp.where(low, 0.5 * coef_ref[b], 0.5 * coef_ref[b + 1])
        return 0

    lax.fori_loop(0, 20, one_freq, 0)
    clear(zeros, freq * (4 * BORDER))


BORDER_HALO = 4 * 18
FIX_ROWS = 2 * BORDER_HALO + 6 * 8


def fix_kernel(far_ref, near_ref, across_ref, inside_ref, speed_ref, fix_ref):
    lower = lax.axis_index("freq") == 0
    for i, ref in enumerate((far_ref, near_ref)):
        fix_ref[i * BORDER_HALO : (i + 1) * BORDER_HALO, :] = jnp.where(
            lower, ref[14 * 18 : 18 * 18, :], ref[0:BORDER_HALO, :]
        )
    for i, ref in enumerate((across_ref, inside_ref)):
        at = 2 * BORDER_HALO + 8 * i
        fix_ref[at : at + 8, :] = jnp.where(lower, pltpu.roll(ref[:, 256:384], 108, 1), ref[:, 0:128])
    at = 2 * BORDER_HALO + 16
    fix_ref[at : at + 32, :] = speed_ref[...]


def neighbours(x, h, hw, he, k, f, places):
    first, last, low, top, bottom = places
    west = east = None
    if k in WEST_TILES:
        pos = f * LANES_F + WEST_TILES.index(k)
        west = jnp.where(first, pltpu.roll(hw, (128 - pos) % 128, 1), pltpu.roll(x, 1, 1))
    if k in EAST_TILES:
        pos = f * LANES_F + EAST_TILES.index(k)
        east = jnp.where(last, pltpu.roll(he, 127 - pos, 1), pltpu.roll(x, 127, 1))
    if east is None:
        side = west
    elif west is None:
        side = east
    else:
        side = jnp.where(low, west, east) if WEST[2 * k] else jnp.where(low, east, west)
    if k < TILES // 2:
        return side, jnp.where(top, h, pltpu.roll(x, 1, 0))
    return side, jnp.where(bottom, h, pltpu.roll(x, 7, 0))


def places_of():
    lane, row = tile_iota(1), tile_iota(0)
    return lane == 0, lane == 127, row < 4, row % 4 == 0, row % 4 == 3


def halo_starts():
    odd = lax.axis_index("lat") % 2 == 1
    south, north = 0, 75
    return jnp.where(odd, north, south), jnp.where(odd, south, north)


def move_kernel(
    e_ref, far_ref, near_ref, across_ref, inside_ref, mask_ref, wind_ref, cell_ref, cx_ref, cy_ref, w0_ref, w1_ref,
    moved_ref, small_ref, own_ref, halo_ref, half_ref,
):
    lat, lon, freq = lax.axis_index("lat"), lax.axis_index("lon"), lax.axis_index("freq")
    lane = tile_iota(1)
    places = places_of()
    odd_lon = lon % 2 == 1
    far, near = halo_starts()
    for f in range(NF):
        halo_ref[pl.ds(f * 144 + far, 18, stride=4), :] = far_ref[f * 18 : f * 18 + 18, :]
        halo_ref[pl.ds(f * 144 + near, 18, stride=4), :] = near_ref[f * 18 : f * 18 + 18, :]
    mask8 = twice(mask_ref[...].astype(F32))
    own = freq * (4 * BORDER)

    def some_freqs(c, carry):
        en, t0, t1 = carry
        across = across_ref[:, pl.ds(pl.multiple_of(c * 128, 128), 128)]
        inside = inside_ref[:, pl.ds(pl.multiple_of(c * 128, 128), 128)]
        hw, he = jnp.where(odd_lon, inside, across), jnp.where(odd_lon, across, inside)
        for f in range(FREQS_V):
            for k in range(TILES):
                at = pl.multiple_of((c * FREQS_V + f) * 144 + k * 8, 8)
                here = pl.ds(at, 8)
                x = e_ref[here, :]
                side, beside = neighbours(x, halo_ref[here, :], hw, he, k, f, places)
                m = mask8 * x - cx_ref[here, :] * (x - side) - cy_ref[here, :] * (x - beside)
                moved_ref[pl.ds(pl.multiple_of(own + at, 8), 8), :] = m
                en = en + m
                t0 = t0 + m * w0_ref[here, :]
                t1 = t1 + m * w1_ref[here, :]
        return en, t0, t1

    zero = jnp.zeros((8, 128), F32)
    en, t0, t1 = lax.fori_loop(0, NF // FREQS_V, some_freqs, (zero, zero, zero))
    wind = wind_ref[...]
    i4 = lax.broadcasted_iota(jnp.int32, (4, 128), 0) + lat * 4
    j4 = lax.broadcasted_iota(jnp.int32, (4, 128), 1) + lon * 128
    offset = cell_ref[...] - (j4 * 32 + i4)
    for c, t in enumerate((t0, t1)):
        tau = (t[0:4] + t[4:8]) * wind
        half_ref[8 * c : 8 * c + 8, :] = zero
        for d in (-1, 0, 1):
            half_ref[8 * c + 1 + d : 8 * c + 5 + d, :] += jnp.where(offset == d, tau, 0.0)
    r0, r1 = half_ref[0:8, :], half_ref[8:16, :]
    lower = jnp.where(lane < 64, r0, pltpu.roll(r1, 64, 1))
    upper = jnp.where(lane < 64, pltpu.roll(r0, 64, 1), r1)
    own_ref[0:8, :] = jnp.where(freq == 0, lower, upper)
    small_ref[0:8, :] = jnp.where(freq == 0, upper, lower)
    total = twice(en[0:4] + en[4:8])
    own_ref[8:16, :] = total
    small_ref[8:16, :] = total


def extend_kernel(raw_ref, fix_ref, mask_ref, _, moved_ref, halo_ref):
    places = places_of()
    low = places[2]
    freq = lax.axis_index("freq")
    far, near = halo_starts()
    for f in range(4):
        halo_ref[pl.ds(f * 144 + far, 18, stride=4), :] = fix_ref[f * 18 : f * 18 + 18, :]
        halo_ref[pl.ds(f * 144 + near, 18, stride=4), :] = fix_ref[BORDER_HALO + f * 18 : BORDER_HALO + f * 18 + 18, :]
    mask8 = twice(mask_ref[...].astype(F32))
    at = 2 * BORDER_HALO
    across, inside = fix_ref[at : at + 8, :], fix_ref[at + 8 : at + 16, :]
    odd_lon = lax.axis_index("lon") % 2 == 1
    hw, he = jnp.where(odd_lon, inside, across), jnp.where(odd_lon, across, inside)
    to = pl.multiple_of((1 - freq) * ROWS, 8)
    for f in range(4):
        speed = fix_ref[at + 16 + f * 8 : at + 24 + f * 8, :] * mask8
        for k in range(TILES):
            here = f * 144 + k * 8
            x = raw_ref[here : here + 8, :]
            side, beside = neighbours(x, halo_ref[here : here + 8, :], hw, he, k, f, places)
            cx = speed * jnp.where(low, float(abs(COS[2 * k])), float(abs(COS[2 * k + 1])))
            cy = speed * jnp.where(low, float(abs(SIN[2 * k])), float(abs(SIN[2 * k + 1])))
            moved_ref[pl.ds(to + here, 8), :] = mask8 * x - cx * (x - side) - cy * (x - beside)


def transfers(own, quads, m_ref, half_ref):
    q0, q1 = quads
    e, third, fourth = [m_ref[b] for b in own], [m_ref[b] for b in q0], [m_ref[b] for b in q1]
    half = [half_ref[b] for b in own]
    return [
        half[i] * (e[i] * (e[i] * (third[i] + fourth[i]) - 2.0 * third[i] * fourth[i])) for i in range(len(own))
    ]


def add_all(quads, t, refs):
    q0, q1 = quads
    n = range(len(t))
    up = [refs[i % 3][q0[i]] for i in n]
    down = [refs[3 + i % 3][q1[i]] for i in n]
    for i in n:
        refs[i % 3][q0[i]] = up[i] + t[i]
    for i in n:
        refs[3 + i % 3][q1[i]] = down[i] + t[i]


SPLIT = 24


def interact_kernel(first, stop, up_ref, down_ref, half_ref, m_ref, *rest):
    refs, t_ref = rest[-SUMS - 1 : -1], rest[-1]
    freq = lax.axis_index("freq")
    start = freq * (2 * ND)
    shift = freq * (14 * ND)

    def one_dir(d, _):
        for group in range(0, 20, 10):
            own = [start + d + f * ND for f in range(group, group + 10)]
            quads = [[ref[shift + b] - shift for b in own] for ref in (up_ref, down_ref)]
            t = transfers(own, quads, m_ref, half_ref)
            add_all(quads, t, refs)
            for b, x in zip(own, t):
                t_ref[b] = x
        return 0

    lax.fori_loop(first, stop, one_dir, 0)


def keep_of(mine_ref, theirs_ref, dis_ref):
    energy = (mine_ref[8:16, :] + theirs_ref[8:16, :]) * (1.0 / (2 * NB))
    return 1.0 - 0.5 * (twice(dis_ref[...]) * energy)


def finish(at, own, keep, m_ref, pw_ref, parts, t_ref):
    here = pl.ds(pl.multiple_of(at, 8), 8)
    total = parts[0][here, :]
    for part in parts[1:]:
        total = total + part[here, :]
    grown = m_ref[here, :] * (keep + pw_ref[pl.ds(pl.multiple_of(at - own, 8), 8), :])
    return grown + (total - 2.0 * t_ref[here, :])


def finish_kernel(m_ref, pw_ref, *rest):
    parts, (t_ref, mine_ref, theirs_ref, dis_ref, hbm_ref, out_ref, sems) = rest[:SUMS], rest[SUMS:]
    own = lax.axis_index("freq") * (4 * BORDER)
    keep = keep_of(mine_ref, theirs_ref, dis_ref)
    copies = []
    for c in range(3):
        def some(f, _):
            for u in range(TILES):
                to = pl.multiple_of((c * FREQS_V + f) * 144 + u * 8, 8)
                out_ref[pl.ds(to, 8), :] = finish(own + to, own, keep, m_ref, pw_ref, parts, t_ref)
            return 0

        lax.fori_loop(0, FREQS_V, some, 0)
        part = pl.ds(c * FREQS_V * 144, FREQS_V * 144)
        copies.append(pltpu.make_async_copy(out_ref.at[part], hbm_ref.at[part], sems.at[c]))
        copies[c].start()
    for copy in copies:
        copy.wait()


def cells_kernel(r_ref, out_ref, z_ref, t_ref):
    lat = lax.axis_index("lat")
    z_ref[...] = jnp.zeros_like(z_ref)
    for k in range(8):
        block = r_ref[pl.ds(pl.multiple_of(jnp.bitwise_xor(lat, k) * 8, 8), 8), :]
        z_ref[7 + 4 * k : 13 + 4 * k, :] += block[0:6]
    t_ref[:, 0:32] = jnp.transpose(z_ref[8:40, :])
    t_ref[:, 32:128] = jnp.zeros((128, 96), F32)
    out = jnp.zeros((32, 128), F32)
    for jj in range(4):
        piece = t_ref[pl.ds(jj, 32, stride=4), :]
        out = out + pltpu.roll(piece, jj * 32, 1)
    for c in range(2):
        for g in range(16):
            out_ref[c : c + 1, g * 128 : g * 128 + 128] = out[c * 16 + g : c * 16 + g + 1, :]


def call(kernel, out, in_specs, scratch=(), out_specs=None, us=1.0, aliases=None):
    return pl.pallas_call(
        kernel,
        out_shape=out,
        in_specs=in_specs,
        out_specs=jax.tree.map(lambda _: VM, out) if out_specs is None else out_specs,
        scratch_shapes=list(scratch),
        compiler_params=PARAMS,
        input_output_aliases=aliases or {},
        cost_estimate=pl.CostEstimate(flops=0, transcendentals=0, bytes_accessed=int(us * 3.0e6)),
    )


def local(
    spectrum, group_speed, sea_mask, wind_growth, dissipation, wind_profile, nonlinear_coef, momentum, quadruplet,
    ocean_cell,
):
    grid = in_vmem((ROWS, 128))
    halo = in_vmem((NF * 18, 128))
    edge = in_vmem((8, 384))
    border = in_vmem((4 * BORDER, 128))
    wide = in_vmem((EXT_ROWS, 128))
    flat, raw, far, near, across, inside, *zeros = call(
        pack_kernel, (grid, border, halo, halo, edge, edge) + (wide,) * EARLY, [HB], [pltpu.SemaphoreType.DMA((NF // CHUNK,))]
    )(pltpu.with_memory_space_constraint(spectrum.reshape(ROWS, 128), pltpu.HBM))
    nlat, nlon = lax.axis_size("lat"), lax.axis_size("lon")

    def pairs(first, count, size):
        both = [(i, (i + 1) % size) for i in range(first, first + 2 * count, 2)]
        return both + [(j, i) for i, j in both]

    swap = pairs(0, 1, 2)
    far = lax.ppermute(far, "lat", pairs(1, nlat // 2 - 1, nlat))
    near = lax.ppermute(near, "lat", pairs(0, nlat // 2, nlat))
    raw = lax.ppermute(raw, "freq", swap)
    across = lax.ppermute(across, "lon", pairs(1, nlon // 2, nlon))
    inside = lax.ppermute(inside, "lon", pairs(0, nlon // 2, nlon))
    sums = in_vmem((16, 128))
    as_bins = lambda x: x.reshape(-1, 4, 128)
    as_rows = lambda x: x.reshape(-1, 128)
    acc = in_vmem((EXT, 4, 128))

    def gather(rows, bit):
        return lax.ppermute(rows, "lat", [(i, i ^ bit) for i in range(nlat)])

    cx, cy, w0, w1, speed = call(table_kernel, (grid,) * 4 + (in_vmem((32, 128)),), [SM] * 3 + [VM], us=2.5)(
        group_speed, momentum, wind_profile, sea_mask
    )
    raw, w1 = lax.optimization_barrier((raw, w1))
    moved, small, own = call(
        move_kernel,
        (wide, sums, sums),
        [VM] * 12,
        [pltpu.VMEM((ROWS, 128), F32), pltpu.VMEM((16, 128), F32)],
        us=1.5,
    )(flat, far, near, across, inside, sea_mask, wind_growth, ocean_cell, cx, cy, w0, w1)
    theirs = lax.ppermute(small, "freq", swap)
    fix = call(fix_kernel, in_vmem((FIX_ROWS, 128)), [VM] * 5, us=0.3)(far, near, across, inside, speed)
    their_fix = lax.ppermute(fix, "freq", swap)
    pw = call(input_kernel, grid, [SM] + [VM] * 2, us=1.5)(wind_profile, wind_growth, fix)
    theirs, pw = lax.optimization_barrier((theirs, pw))
    rows = own[0:8] + theirs[0:8]
    other = gather(rows, 1)
    their_fix, rows = lax.optimization_barrier((their_fix, rows))
    half, *more = call(half_kernel, (wide,) * (1 + SUMS - EARLY), [SM] + [VM], us=1.5)(nonlinear_coef, rows)
    other, half = lax.optimization_barrier((other, half))
    rows = jnp.concatenate([rows, other], 0)
    other = gather(rows, 2)
    their_fix, rows = lax.optimization_barrier((their_fix, rows))
    moved = call(
        extend_kernel, wide, [VM] * 4, [pltpu.VMEM((4 * BORDER, 128), F32)], us=1.0, aliases={3: 0}
    )(raw, their_fix, sea_mask, moved)
    quads = [jnp.maximum(quadruplet[r], 0) for r in range(2)]
    fixed = (*quads, as_bins(half), as_bins(moved))
    parts = list(map(as_bins, (*zeros, *more)))
    for first, stop in ((0, SPLIT), (SPLIT, ND)):
        if first:
            other, *parts = lax.optimization_barrier((other, *parts))
            rows = jnp.concatenate([rows, other], 0)
            other = gather(rows, 4)
            *parts, rows = lax.optimization_barrier((*parts, rows))
        parts = call(
            functools.partial(interact_kernel, first, stop),
            (acc,) * (SUMS + 1),
            [SM] * 2 + [VM] * (2 + len(parts)),
            us=3.0,
            aliases={4 + i: i for i in range(len(parts))},
        )(*fixed, *parts)
    out = call(
        finish_kernel,
        jax.ShapeDtypeStruct((ROWS, 128), F32),
        [VM] * (6 + SUMS),
        [pltpu.VMEM((ROWS, 128), F32), pltpu.SemaphoreType.DMA((3,))],
        out_specs=ANY,
        us=2.0,
    )(moved, pw, *map(as_rows, parts), own, theirs, dissipation)
    other, out = lax.optimization_barrier((other, out))
    stress = call(
        cells_kernel,
        jax.ShapeDtypeStruct((2, 2048), F32),
        [VM],
        [pltpu.VMEM((48, 128), F32), pltpu.VMEM((128, 128), F32)],
    )(jnp.concatenate([rows, other], 0))
    return out.reshape(spectrum.shape), stress.T


def solution(mesh):
    return jax.shard_map(
        local,
        mesh=mesh,
        in_specs=(
            P("freq", None, "lat", "lon"),
            P("freq"),
            P("lat", "lon"),
            P("lat", "lon"),
            P("lat", "lon"),
            P(),
            P(),
            P(),
            P(),
            P("lat", "lon"),
        ),
        out_specs=(P("freq", None, "lat", "lon"), P(("lon", "freq"), None)),
        check_vma=False,
    )
```

time: 44.5 us -> 43 us (0.966)
  the two profiles are of different devices: /device:TPU:14 before, /device:TPU:8 now
where the time goes in v3:
time: 43 us; the launch traced here: 42.7 us
  starting transfers between devices  20.4 us (47%)
  Pallas kernels  16.5 us (38%)
  local copies, waits for them, and re-layouts  4.13 us (10%)
  between operations  0.84 us (2%)
  waiting for transfers between devices  0.77 us (2%)
    ppermute x3, starting transfers between devices, gather(): return lax.ppermute(rows, 'lat', [(i, i ^ bit) for i in range(nlat)])  8.38 us
    pallas_call x2, Pallas kernels, local(): call(functools.partial(interact_kernel, first, stop), (acc,) * (SUMS + 1)...  5.15 us
    ppermute x1, starting transfers between devices, local(): across = lax.ppermute(across, 'lon', pairs(1, nlon // 2, nlon))  4.82 us
    unnamed x24, local copies, waits for them, and re-layouts  4.12 us
    ppermute x1, starting transfers between devices, local(): far = lax.ppermute(far, 'lat', pairs(1, nlat // 2 - 1, nlat))  3.47 us
    pallas_call x1, Pallas kernels, local(): call(table_kernel, (grid,) * 4 + (in_vmem((32, 128)),), [SM] * 3 + [VM],...  2.69 us
    pallas_call x1, Pallas kernels, local(): call(finish_kernel, jax.ShapeDtypeStruct((ROWS, 128), F32), [VM] * (6 + S...  1.75 us
    pallas_call x1, Pallas kernels, local(): call(pack_kernel, (grid, border, halo, halo, edge, edge) + (wide,) * EARL...  1.67 us
  transfers between devices with their start and end apart: 10, of which 2 were waited for; matrix products, arithmetic and copies ran while one was open for 0% of the time, Pallas kernels for 30%

profile of v3, /device:TPU:8, one launch (start us, length us, event | category | flops | bytes accessed | tf_op | source)
XLA Modules:
  0.0 42.7 jit_solution(17957911728908790733)
XLA Ops:
  0.6 1.7 %shard_map.113 = (f32[2592,128]{1,0:T(8,128)S(1)}, f32[576,128]{1,0:T(8,128)S(1)}, f32[324,128]{1,0:T(8,128)S(1)}, f32[324,128]{1,0:T(8,128)S(1)}, f32[8,384]{1,...) custom-call(f32[2592,128]{1,0:T(8,128)} %bitcast.36), custom_call_target="tpu_custom_call" | custom-call | bytes 3000000 | tf_op jit(solution)/shard_map/pallas_call | solution.py:396
  2.3 1.6 %collective-permute-start.5 = (f32[576,128]{1,0:T(8,128)S(1)}, f32[576,128]{1,0:T(8,128)S(1)}, u32[]{:S(2)}, u32[]{:S(2)}) collective-permute-start(f32[576,128]{1,0:T(8,128)S(1)} %get-tuple-element.74), channel_id=1, source_target_pairs={{0,1},{1,0},{2,3},{3,2},{4,5},{5,4},{6,7},{7,6},{8,9},{9,8},{10,11... | collective-permute-start | bytes 884744 | tf_op jit(solution)/shard_map/ppermute | solution.py:408
  3.9 3.5 %collective-permute-start = (f32[324,128]{1,0:T(8,128)S(1)}, f32[324,128]{1,0:T(8,128)S(1)}, u32[]{:S(2)}, u32[]{:S(2)}) collective-permute-start(f32[324,128]{1,0:T(8,128)S(1)} %get-tuple-element.65), channel_id=1, source_target_pairs={{32,64},{96,128},{160,192},{64,32},{128,96},{192,160},{33,65},{97,... | collective-permute-start | bytes 497672 | tf_op jit(solution)/shard_map/ppermute | solution.py:406
  7.4 0.1 collective-permute-start.1
  7.5 4.8 %collective-permute-start.2 = (f32[8,384]{1,0:T(8,128)S(1)}, f32[8,384]{1,0:T(8,128)S(1)}, u32[]{:S(2)}, u32[]{:S(2)}) collective-permute-start(f32[8,384]{1,0:T(8,128)S(1)} %get-tuple-element.67), channel_id=1, source_target_pairs={{2,4},{6,8},{10,12},{14,16},{18,20},{22,24},{26,28},{30,0},{4,2},{... | collective-permute-start | bytes 36872 | tf_op jit(solution)/shard_map/ppermute | solution.py:409
  12.3 0.0 collective-permute-start.3
  12.3 0.0 copy-start
  12.3 0.7 %copy-done = f32[1296]{0:T(1024)S(1)} copy-done((f32[1296]{0:T(1024)S(1)}, f32[1296]{0:T(1024)}, u32[]{:S(2)}) %copy-start) | copy-done | bytes 5208
  13.0 0.0 copy-start.1
  13.0 0.7 %copy-done.1 = s32[4,128]{1,0:T(4,128)S(1)} copy-done((s32[4,128]{1,0:T(4,128)S(1)}, s32[4,128]{1,0:T(4,128)}, u32[]{:S(2)}) %copy-start.1) | copy-done | bytes 2072
  13.7 0.0 copy-start.3
  13.7 0.7 %copy-done.3 = f32[2,1296]{1,0:T(2,128)S(1)} copy-done((f32[2,1296]{1,0:T(2,128)S(1)}, f32[2,1296]{1,0:T(2,128)}, u32[]{:S(2)}) %copy-start.3) | copy-done | bytes 10392
  14.4 0.0 copy-start.9
  14.4 0.7 %copy-done.9 = f32[18]{0:T(128)S(1)} copy-done((f32[18]{0:T(128)S(1)}, f32[18]{0:T(128)}, u32[]{:S(2)}) %copy-start.9) | copy-done | bytes 96
  15.0 2.7 %shard_map.114 = (f32[2592,128]{1,0:T(8,128)S(1)}, f32[2592,128]{1,0:T(8,128)S(1)}, f32[2592,128]{1,0:T(8,128)S(1)}, f32[2592,128]{1,0:T(8,128)S(1)}, f32[32,128]{1,0:T(8,128)S(1)}) custom-call(f32[18]{0:T(128)S(1)} %copy-done.9, f32[2,1296]{1,0:T(2,128)S(1)} %copy-done.3, f32[1296]{0:T(1024)S(1)} %copy-done, s32[4,128]{1,0:T(4,128)S(1)} %copy-done.1), custom_call_target="tpu_custom_call" | custom-call | bytes 7500000 | tf_op jit(solution)/shard_map/pallas_call | solution.py:419
  17.7 0.0 collective-permute-done.5.raw_ref
  17.7 0.0 collective-permute-done.2.across_ref
  17.7 0.0 collective-permute-done.3.inside_ref
  17.8 0.0 collective-permute-done.far_ref
  17.8 0.0 collective-permute-done.1.near_ref
  17.8 0.0 copy-start.4
  17.8 0.7 %copy-done.4 = f32[4,128]{1,0:T(4,128)S(1)} copy-done((f32[4,128]{1,0:T(4,128)S(1)}, f32[4,128]{1,0:T(4,128)}, u32[]{:S(2)}) %copy-start.4) | copy-done | bytes 2072
  18.5 0.0 copy-start.7
  18.5 0.7 %copy-done.7 = s32[4,128]{1,0:T(4,128)S(1)} copy-done((s32[4,128]{1,0:T(4,128)S(1)}, s32[4,128]{1,0:T(4,128)}, u32[]{:S(2)}) %copy-start.7) | copy-done | bytes 2072
  19.1 0.0 copy-start.10
  19.1 0.0 copy-start.5
  19.1 1.3 %shard_map.116 = (f32[3168,128]{1,0:T(8,128)S(1)}, f32[16,128]{1,0:T(8,128)S(1)}, f32[16,128]{1,0:T(8,128)S(1)}) custom-call(f32[2592,128]{1,0:T(8,128)S(1)} %get-tuple-element.70.e_ref, f32[324,128]{1,0:T(8,128)S(1)} %collective-permute-done.far_ref, f32[324,128]{1,0:T(8,128)S(1)} %collective-permute-done.1.near_ref, ...), custom_call_target="tpu_custom_call" | custom-call | bytes 4500000 | tf_op jit(solution)/shard_map/pallas_call | solution.py:423
  20.4 0.0 copy-start.6
  20.4 0.0 copy-start.2
  20.4 0.6 %collective-permute-start.6 = (f32[16,128]{1,0:T(8,128)S(1)}, f32[16,128]{1,0:T(8,128)S(1)}, u32[]{:S(2)}, u32[]{:S(2)}) collective-permute-start(f32[16,128]{1,0:T(8,128)S(1)} %get-tuple-element.78), channel_id=1, source_target_pairs={{0,1},{1,0},{2,3},{3,2},{4,5},{5,4},{6,7},{7,6},{8,9},{9,8},{10,11... | collective-permute-start | bytes 24584 | tf_op jit(solution)/shard_map/ppermute | solution.py:430
  21.0 0.0 copy-done.10
  21.0 0.1 shard_map.115._
  21.1 1.5 %collective-permute-start.4 = (f32[192,128]{1,0:T(8,128)S(1)}, f32[192,128]{1,0:T(8,128)S(1)}, u32[]{:S(2)}, u32[]{:S(2)}) collective-permute-start(f32[192,128]{1,0:T(8,128)S(1)} %shard_map.115._), channel_id=1, source_target_pairs={{0,1},{1,0},{2,3},{3,2},{4,5},{5,4},{6,7},{7,6},{8,9},{9,8},{10,11... | collective-permute-start | bytes 294920 | tf_op jit(solution)/shard_map/ppermute | solution.py:432
  22.6 0.0 copy-done.5
  22.6 1.1 %shard_map.117.pw_ref = f32[2592,128]{1,0:T(8,128)S(1)} custom-call(f32[1296]{0:T(1024)S(1)} %copy-done, f32[4,128]{1,0:T(4,128)S(1)} %copy-done.5, f32[192,128]{1,0:T(8,128)S(1)} %shard_map.115._), custom_call_target="tpu_custom_call" | custom-call | bytes 4500000 | tf_op jit(solution)/shard_map/pallas_call | solution.py:433
  23.8 0.4 collective-permute-done.6.rest_8_
  24.2 1.6 %collective-permute-start.7 = (f32[8,128]{1,0:T(8,128)S(1)}, f32[8,128]{1,0:T(8,128)S(1)}, u32[]{:S(2)}, u32[]{:S(2)}) collective-permute-start(f32[8,128]{1,0:T(8,128)S(1)} %slice_add_fusion._), channel_id=1, source_target_pairs={{0,32},{32,0},{64,96},{96,64},{128,160},{160,128},{192,224},{224,1... | collective-permute-start | bytes 12296 | tf_op jit(solution)/shard_map/ppermute | solution.py:417
  25.8 0.3 collective-permute-done.4.fix_ref
  26.2 0.0 copy-done.6
  26.2 1.7 %shard_map.118 = (f32[3168,128]{1,0:T(8,128)S(1)}, f32[3168,128]{1,0:T(8,128)S(1)}, f32[3168,128]{1,0:T(8,128)S(1)}) custom-call(f32[1296]{0:T(1024)S(1)} %copy-done.6, f32[8,128]{1,0:T(8,128)S(1)} %slice_add_fusion._), custom_call_target="tpu_custom_call" | custom-call | bytes 4500000 | tf_op jit(solution)/shard_map/pallas_call | solution.py:438
  27.8 0.0 collective-permute-done.7
  27.9 3.1 %collective-permute-start.8 = (f32[16,128]{1,0:T(8,128)S(1)}, f32[16,128]{1,0:T(8,128)S(1)}, u32[]{:S(2)}, u32[]{:S(2)}) collective-permute-start(f32[16,128]{1,0:T(8,128)S(1)} %constant_dynamic-update-slice_fusion), channel_id=1, source_target_pairs={{0,64},{32,96},{64,0},{96,32},{128,192},{160,224},{192,128},{224,1... | collective-permute-start | bytes 24584 | tf_op jit(solution)/shard_map/ppermute | solution.py:417
  30.9 0.0 copy-done.2
  30.9 0.3 shard_map.119.m_ref
  31.2 3.2 %shard_map.120 = (f32[792,4,128]{2,1,0:T(4,128)S(1)}, f32[792,4,128]{2,1,0:T(4,128)S(1)}, f32[792,4,128]{2,1,0:T(4,128)S(1)}, f32[792,4,128]{2,1,0:T(4,128)S(1)}...) custom-call(s32[1296]{0:T(1024)S(1)} %get-tuple-element.129.up_ref, ...), custom_call_target="tpu_custom_call", output_to_operand_aliasing={{0}: (4, {}), {1}: (5, {}), {2}: (6, {}), {3}: (7, {}), {4}... | custom-call | bytes 9000000 | tf_op jit(solution)/shard_map/pallas_call | solution.py:455
  34.4 0.0 collective-permute-done.8
  34.4 0.0 copy-start.8
  34.4 3.7 %collective-permute-start.9 = (f32[32,128]{1,0:T(8,128)S(1)}, f32[32,128]{1,0:T(8,128)S(1)}, u32[]{:S(2)}, u32[]{:S(2)}) collective-permute-start(f32[32,128]{1,0:T(8,128)S(1)} %constant_dynamic-update-slice_fusion.2), channel_id=1, source_target_pairs={{0,128},{32,160},{64,192},{96,224},{128,0},{160,32},{192,64},{224,... | collective-permute-start | bytes 49160 | tf_op jit(solution)/shard_map/ppermute | solution.py:417
  38.1 1.9 %shard_map.121 = (f32[792,4,128]{2,1,0:T(4,128)S(1)}, f32[792,4,128]{2,1,0:T(4,128)S(1)}, f32[792,4,128]{2,1,0:T(4,128)S(1)}, f32[792,4,128]{2,1,0:T(4,128)S(1)}...) custom-call(s32[1296]{0:T(1024)S(1)} %get-tuple-element.129.up_ref, ...), custom_call_target="tpu_custom_call", output_to_operand_aliasing={{0}: (4, {}), {1}: (5, {}), {2}: (6, {}), {3}: (7, {}), {4}... | custom-call | bytes 9000000 | tf_op jit(solution)/shard_map/pallas_call | solution.py:455
  40.1 0.0 copy-done.8
  40.1 1.7 %shard_map.122 = f32[2592,128]{1,0:T(8,128)} custom-call(f32[3168,128]{1,0:T(8,128)S(1)} %shard_map.119.m_ref, f32[2592,128]{1,0:T(8,128)S(1)} %shard_map.117.pw_ref, f32[3168,128]{1,0:T(8,128)S(1)} %bitcast.21, f32[3168,128]{1,0:T(8,128)S(1)} %bitcast.23, f32[3168,128]{1,0:T(8,128)S(1)} %bitcast.25, f32[3168,128]{1,0:T(8,128)S(1)} %bitcast.27, ...), custom_call_target="tpu_custom_call" | custom-call | bytes 6000000 | tf_op jit(solution)/shard_map/pallas_call | solution.py:462
  41.8 0.0 collective-permute-done.9
  41.8 0.9 %shard_map.123 = f32[2,2048]{1,0:T(2,128)} custom-call(f32[64,128]{1,0:T(8,128)S(1)} %pad_maximum_fusion.r_ref), custom_call_target="tpu_custom_call" | custom-call | bytes 3000000 | tf_op jit(solution)/shard_map/pallas_call | solution.py:471
  (7 shorter events, 0.1 us)
Async XLA Ops:
  2.3 15.4 %collective-permute-start.5 = (f32[576,128]{1,0:T(8,128)S(1)}, f32[576,128]{1,0:T(8,128)S(1)}, u32[]{:S(2)}, u32[]{:S(2)}) collective-permute-start(f32[576,128]{1,0:T(8,128)S(1)} %get-tuple-element.74), channel_id=1, source_target_pairs={{0,1},{1,0},{2,3},{3,2},{4,5},{5,4},{6,7},{7,6},{8,9},{9,8},{10,11... | collective-permute-start | bytes 884744 | tf_op jit(solution)/shard_map/ppermute | solution.py:408
  3.9 13.9 %collective-permute-start = (f32[324,128]{1,0:T(8,128)S(1)}, f32[324,128]{1,0:T(8,128)S(1)}, u32[]{:S(2)}, u32[]{:S(2)}) collective-permute-start(f32[324,128]{1,0:T(8,128)S(1)} %get-tuple-element.65), channel_id=1, source_target_pairs={{32,64},{96,128},{160,192},{64,32},{128,96},{192,160},{33,65},{97,... | collective-permute-start | bytes 497672 | tf_op jit(solution)/shard_map/ppermute | solution.py:406
  7.4 10.4 %collective-permute-start.1 = (f32[324,128]{1,0:T(8,128)S(1)}, f32[324,128]{1,0:T(8,128)S(1)}, u32[]{:S(2)}, u32[]{:S(2)}) collective-permute-start(f32[324,128]{1,0:T(8,128)S(1)} %get-tuple-element.66), channel_id=1, source_target_pairs={{0,32},{64,96},{128,160},{192,224},{32,0},{96,64},{160,128},{224,1... | collective-permute-start | bytes 497672 | tf_op jit(solution)/shard_map/ppermute | solution.py:407
  7.5 10.3 %collective-permute-start.2 = (f32[8,384]{1,0:T(8,128)S(1)}, f32[8,384]{1,0:T(8,128)S(1)}, u32[]{:S(2)}, u32[]{:S(2)}) collective-permute-start(f32[8,384]{1,0:T(8,128)S(1)} %get-tuple-element.67), channel_id=1, source_target_pairs={{2,4},{6,8},{10,12},{14,16},{18,20},{22,24},{26,28},{30,0},{4,2},{... | collective-permute-start | bytes 36872 | tf_op jit(solution)/shard_map/ppermute | solution.py:409
  12.3 5.5 %collective-permute-start.3 = (f32[8,384]{1,0:T(8,128)S(1)}, f32[8,384]{1,0:T(8,128)S(1)}, u32[]{:S(2)}, u32[]{:S(2)}) collective-permute-start(f32[8,384]{1,0:T(8,128)S(1)} %get-tuple-element.68), channel_id=1, source_target_pairs={{0,2},{4,6},{8,10},{12,14},{16,18},{20,22},{24,26},{28,30},{2,0},{... | collective-permute-start | bytes 36872 | tf_op jit(solution)/shard_map/ppermute | solution.py:410
  12.3 0.7 %copy-start = (f32[1296]{0:T(1024)S(1)}, f32[1296]{0:T(1024)}, u32[]{:S(2)}) copy-start(f32[1296]{0:T(1024)} %prof_ref.3) | copy-start | bytes 15556
  13.0 0.7 %copy-start.1 = (s32[4,128]{1,0:T(4,128)S(1)}, s32[4,128]{1,0:T(4,128)}, u32[]{:S(2)}) copy-start(s32[4,128]{1,0:T(4,128)} %mask_ref.5) | copy-start | bytes 6148
  13.7 0.7 %copy-start.3 = (f32[2,1296]{1,0:T(2,128)S(1)}, f32[2,1296]{1,0:T(2,128)}, u32[]{:S(2)}) copy-start(f32[2,1296]{1,0:T(2,128)} %mom_ref.1) | copy-start | bytes 31108
  14.4 0.7 %copy-start.9 = (f32[18]{0:T(128)S(1)}, f32[18]{0:T(128)}, u32[]{:S(2)}) copy-start(f32[18]{0:T(128)} %gs_ref.1) | copy-start | bytes 220
  17.8 0.7 %copy-start.4 = (f32[4,128]{1,0:T(4,128)S(1)}, f32[4,128]{1,0:T(4,128)}, u32[]{:S(2)}) copy-start(f32[4,128]{1,0:T(4,128)} %wind_ref.3) | copy-start | bytes 6148
  18.5 0.7 %copy-start.7 = (s32[4,128]{1,0:T(4,128)S(1)}, s32[4,128]{1,0:T(4,128)}, u32[]{:S(2)}) copy-start(s32[4,128]{1,0:T(4,128)} %cell_ref.1) | copy-start | bytes 6148
  19.1 1.8 %copy-start.10 = (s32[2,1296]{1,0:T(2,128)S(1)}, s32[2,1296]{1,0:T(2,128)}, u32[]{:S(2)}) copy-start(s32[2,1296]{1,0:T(2,128)} %param.18) | copy-start | bytes 31108
  19.1 3.5 %copy-start.5 = (f32[4,128]{1,0:T(4,128)S(1)}, f32[4,128]{1,0:T(4,128)}, u32[]{:S(2)}) copy-start(f32[4,128]{1,0:T(4,128)} %wind_ref.3) | copy-start | bytes 6148
  20.4 5.8 %copy-start.6 = (f32[1296]{0:T(1024)S(1)}, f32[1296]{0:T(1024)}, u32[]{:S(2)}) copy-start(f32[1296]{0:T(1024)} %coef_ref.1) | copy-start | bytes 15556
  20.4 10.5 %copy-start.2 = (s32[4,128]{1,0:T(4,128)S(1)}, s32[4,128]{1,0:T(4,128)}, u32[]{:S(2)}) copy-start(s32[4,128]{1,0:T(4,128)} %mask_ref.5) | copy-start | bytes 6148
  20.4 3.8 %collective-permute-start.6 = (f32[16,128]{1,0:T(8,128)S(1)}, f32[16,128]{1,0:T(8,128)S(1)}, u32[]{:S(2)}, u32[]{:S(2)}) collective-permute-start(f32[16,128]{1,0:T(8,128)S(1)} %get-tuple-element.78), channel_id=1, source_target_pairs={{0,1},{1,0},{2,3},{3,2},{4,5},{5,4},{6,7},{7,6},{8,9},{9,8},{10,11... | collective-permute-start | bytes 24584 | tf_op jit(solution)/shard_map/ppermute | solution.py:430
  21.1 5.1 %collective-permute-start.4 = (f32[192,128]{1,0:T(8,128)S(1)}, f32[192,128]{1,0:T(8,128)S(1)}, u32[]{:S(2)}, u32[]{:S(2)}) collective-permute-start(f32[192,128]{1,0:T(8,128)S(1)} %shard_map.115._), channel_id=1, source_target_pairs={{0,1},{1,0},{2,3},{3,2},{4,5},{5,4},{6,7},{7,6},{8,9},{9,8},{10,11... | collective-permute-start | bytes 294920 | tf_op jit(solution)/shard_map/ppermute | solution.py:432
  24.2 3.6 %collective-permute-start.7 = (f32[8,128]{1,0:T(8,128)S(1)}, f32[8,128]{1,0:T(8,128)S(1)}, u32[]{:S(2)}, u32[]{:S(2)}) collective-permute-start(f32[8,128]{1,0:T(8,128)S(1)} %slice_add_fusion._), channel_id=1, source_target_pairs={{0,32},{32,0},{64,96},{96,64},{128,160},{160,128},{192,224},{224,1... | collective-permute-start | bytes 12296 | tf_op jit(solution)/shard_map/ppermute | solution.py:417
  27.9 6.5 %collective-permute-start.8 = (f32[16,128]{1,0:T(8,128)S(1)}, f32[16,128]{1,0:T(8,128)S(1)}, u32[]{:S(2)}, u32[]{:S(2)}) collective-permute-start(f32[16,128]{1,0:T(8,128)S(1)} %constant_dynamic-update-slice_fusion), channel_id=1, source_target_pairs={{0,64},{32,96},{64,0},{96,32},{128,192},{160,224},{192,128},{224,1... | collective-permute-start | bytes 24584 | tf_op jit(solution)/shard_map/ppermute | solution.py:417
  34.4 5.7 %copy-start.8 = (f32[4,128]{1,0:T(4,128)S(1)}, f32[4,128]{1,0:T(4,128)}, u32[]{:S(2)}) copy-start(f32[4,128]{1,0:T(4,128)} %rest_9_.1) | copy-start | bytes 6148
  34.4 7.4 %collective-permute-start.9 = (f32[32,128]{1,0:T(8,128)S(1)}, f32[32,128]{1,0:T(8,128)S(1)}, u32[]{:S(2)}, u32[]{:S(2)}) collective-permute-start(f32[32,128]{1,0:T(8,128)S(1)} %constant_dynamic-update-slice_fusion.2), channel_id=1, source_target_pairs={{0,128},{32,160},{64,192},{96,224},{128,0},{160,32},{192,64},{224,... | collective-permute-start | bytes 49160 | tf_op jit(solution)/shard_map/ppermute | solution.py:417

commit v4 on v3

--- a/solution.py
+++ b/solution.py
@@ -64,8 +64,13 @@
 CHUNK = 6
 
 
-def pack_kernel(hbm_ref, e_ref, raw_ref, far_ref, near_ref, across_ref, inside_ref, *rest):
-    *zeros, sems = rest
+SMALL = 8
+
+
+def pack_kernel(hbm_ref, *rest):
+    small_hbm, rest = rest[:SMALL], rest[SMALL:]
+    e_ref, raw_ref, far_ref, near_ref, across_ref, inside_ref = rest[:6]
+    zeros, small_refs, (sems, small_sems) = rest[6 : 6 + EARLY], rest[6 + EARLY : -2], rest[-2:]
     lane = tile_iota(1)
     odd_lat = lax.axis_index("lat") % 2 == 1
     odd_lon = lax.axis_index("lon") % 2 == 1
@@ -76,6 +81,9 @@
         part = pl.ds(c * CHUNK * 144, CHUNK * 144)
         copies.append(pltpu.make_async_copy(hbm_ref.at[part], e_ref.at[part], sems.at[c]))
         copies[c].start()
+    smalls = [pltpu.make_async_copy(a, b, small_sems.at[i]) for i, (a, b) in enumerate(zip(small_hbm, small_refs))]
+    for copy in smalls:
+        copy.start()
     clear(zeros, lax.axis_index("freq") * (4 * BORDER))
     acc = [[jnp.zeros((8, 128), F32)] * 3, [jnp.zeros((8, 128), F32)] * 3]
     for f in range(NF):
@@ -95,6 +103,8 @@
     for chunk in range(3):
         across_ref[:, chunk * 128 : chunk * 128 + 128] = jnp.where(odd_lon, acc[0][chunk], acc[1][chunk])
         inside_ref[:, chunk * 128 : chunk * 128 + 128] = jnp.where(odd_lon, acc[1][chunk], acc[0][chunk])
+    for copy in smalls:
+        copy.wait()
 
 
 def table_kernel(gs_ref, mom_ref, prof_ref, mask_ref, cx_ref, cy_ref, w0_ref, w1_ref, speed_ref):
@@ -393,9 +403,17 @@
     edge = in_vmem((8, 384))
     border = in_vmem((4 * BORDER, 128))
     wide = in_vmem((EXT_ROWS, 128))
-    flat, raw, far, near, across, inside, *zeros = call(
-        pack_kernel, (grid, border, halo, halo, edge, edge) + (wide,) * EARLY, [HB], [pltpu.SemaphoreType.DMA((NF // CHUNK,))]
-    )(pltpu.with_memory_space_constraint(spectrum.reshape(ROWS, 128), pltpu.HBM))
+    small_args = (
+        group_speed, momentum, wind_profile, nonlinear_coef, sea_mask, wind_growth, dissipation, ocean_cell
+    )
+    flat, raw, far, near, across, inside, *rest = call(
+        pack_kernel,
+        (grid, border, halo, halo, edge, edge) + (wide,) * EARLY + tuple(in_vmem(x.shape, x.dtype) for x in small_args),
+        [HB] * (1 + SMALL),
+        [pltpu.SemaphoreType.DMA((NF // CHUNK,)), pltpu.SemaphoreType.DMA((SMALL,))],
+    )(*(pltpu.with_memory_space_constraint(x, pltpu.HBM) for x in (spectrum.reshape(ROWS, 128), *small_args)))
+    zeros = rest[:EARLY]
+    group_speed, momentum, wind_profile, nonlinear_coef, sea_mask, wind_growth, dissipation, ocean_cell = rest[EARLY:]
     nlat, nlon = lax.axis_size("lat"), lax.axis_size("lon")
 
     def pairs(first, count, size):

time: 43 us -> 39.1 us (0.909)
  local copies, waits for them, and re-layouts: 4.13 us -> 0.02 us
    unnamed x24 -> x4, local copies, waits for them, and re-layouts: 4.12 us -> 0.01 us
  transfers between devices with their start and end apart: 10 -> 10, of which waited for: 2 -> 2; matrix products, arithmetic and copies ran while one was open for 0% -> 0% of each run, Pallas kernels for 30% -> 33%
where the time goes in v4:
time: 39.1 us; the launch traced here: 38.6 us
  starting transfers between devices  20.4 us (52%)
  Pallas kernels  16.5 us (42%)
  between operations  0.81 us (2%)
  waiting for transfers between devices  0.77 us (2%)
    ppermute x3, starting transfers between devices, gather(): return lax.ppermute(rows, 'lat', [(i, i ^ bit) for i in range(nlat)])  8.39 us
    pallas_call x2, Pallas kernels, local(): call(functools.partial(interact_kernel, first, stop), (acc,) * (SUMS + 1)...  5.15 us
    ppermute x1, starting transfers between devices, local(): across = lax.ppermute(across, 'lon', pairs(1, nlon // 2, nlon))  4.82 us
    ppermute x1, starting transfers between devices, local(): far = lax.ppermute(far, 'lat', pairs(1, nlat // 2 - 1, nlat))  3.47 us
    pallas_call x1, Pallas kernels, local(): call(table_kernel, (grid,) * 4 + (in_vmem((32, 128)),), [SM] * 3 + [VM],...  2.69 us
    pallas_call x1, Pallas kernels, local(): call(pack_kernel, (grid, border, halo, halo, edge, edge) + (wide,) * EARL...  1.84 us
    pallas_call x1, Pallas kernels, local(): call(half_kernel, (wide,) * (1 + SUMS - EARLY), [SM] + [VM], us=1.5)  1.66 us
    pallas_call x1, Pallas kernels, local(): call(finish_kernel, jax.ShapeDtypeStruct((ROWS, 128), F32), [VM] * (6 + S...  1.64 us
  transfers between devices with their start and end apart: 10, of which 2 were waited for; matrix products, arithmetic and copies ran while one was open for 0% of the time, Pallas kernels for 33%

profile of v4, /device:TPU:8, one launch (start us, length us, event | category | flops | bytes accessed | tf_op | source)
XLA Modules:
  0.0 38.6 jit_solution(14652414848537876678)
XLA Ops:
  0.6 1.8 %shard_map.113 = (f32[2592,128]{1,0:T(8,128)S(1)}, f32[576,128]{1,0:T(8,128)S(1)}, f32[324,128]{1,0:T(8,128)S(1)}, f32[324,128]{1,0:T(8,128)S(1)}, f32[8,384]{1,...) custom-call(f32[2592,128]{1,0:T(8,128)} %bitcast.36, ...), custom_call_target="tpu_custom_call" | custom-call | bytes 3000000 | tf_op jit(solution)/shard_map/pallas_call | solution.py:409
  2.5 1.6 %collective-permute-start.5 = (f32[576,128]{1,0:T(8,128)S(1)}, f32[576,128]{1,0:T(8,128)S(1)}, u32[]{:S(2)}, u32[]{:S(2)}) collective-permute-start(f32[576,128]{1,0:T(8,128)S(1)} %get-tuple-element.88), channel_id=1, source_target_pairs={{0,1},{1,0},{2,3},{3,2},{4,5},{5,4},{6,7},{7,6},{8,9},{9,8},{10,11... | collective-permute-start | bytes 884744 | tf_op jit(solution)/shard_map/ppermute | solution.py:426
  4.1 3.5 %collective-permute-start = (f32[324,128]{1,0:T(8,128)S(1)}, f32[324,128]{1,0:T(8,128)S(1)}, u32[]{:S(2)}, u32[]{:S(2)}) collective-permute-start(f32[324,128]{1,0:T(8,128)S(1)} %get-tuple-element.73), channel_id=1, source_target_pairs={{32,64},{96,128},{160,192},{64,32},{128,96},{192,160},{33,65},{97,... | collective-permute-start | bytes 497672 | tf_op jit(solution)/shard_map/ppermute | solution.py:424
  7.5 0.1 collective-permute-start.1
  7.6 4.8 %collective-permute-start.2 = (f32[8,384]{1,0:T(8,128)S(1)}, f32[8,384]{1,0:T(8,128)S(1)}, u32[]{:S(2)}, u32[]{:S(2)}) collective-permute-start(f32[8,384]{1,0:T(8,128)S(1)} %get-tuple-element.75), channel_id=1, source_target_pairs={{2,4},{6,8},{10,12},{14,16},{18,20},{22,24},{26,28},{30,0},{4,2},{... | collective-permute-start | bytes 36872 | tf_op jit(solution)/shard_map/ppermute | solution.py:427
  12.5 0.0 collective-permute-start.3
  12.5 2.7 %shard_map.114 = (f32[2592,128]{1,0:T(8,128)S(1)}, f32[2592,128]{1,0:T(8,128)S(1)}, f32[2592,128]{1,0:T(8,128)S(1)}, f32[2592,128]{1,0:T(8,128)S(1)}, f32[32,128]{1,0:T(8,128)S(1)}) custom-call(f32[18]{0:T(128)S(1)} %get-tuple-element.77.gs_ref, f32[2,1296]{1,0:T(2,128)S(1)} %get-tuple-element.78.mom_ref, f32[1296]{0:T(1024)S(1)} %get-tuple-element.79.prof_ref, ...), custom_call_target="tpu_custom_call" | custom-call | bytes 7500000 | tf_op jit(solution)/shard_map/pallas_call | solution.py:437
  15.2 0.0 collective-permute-done.5.raw_ref
  15.2 0.0 collective-permute-done.2.across_ref
  15.2 0.0 collective-permute-done.3.inside_ref
  15.2 0.0 collective-permute-done.far_ref
  15.2 0.0 collective-permute-done.1.near_ref
  15.2 0.0 copy-start
  15.2 1.2 %shard_map.116 = (f32[3168,128]{1,0:T(8,128)S(1)}, f32[16,128]{1,0:T(8,128)S(1)}, f32[16,128]{1,0:T(8,128)S(1)}) custom-call(f32[2592,128]{1,0:T(8,128)S(1)} %get-tuple-element.82.e_ref, f32[324,128]{1,0:T(8,128)S(1)} %collective-permute-done.far_ref, f32[324,128]{1,0:T(8,128)S(1)} %collective-permute-done.1.near_ref, ...), custom_call_target="tpu_custom_call" | custom-call | bytes 4500000 | tf_op jit(solution)/shard_map/pallas_call | solution.py:441
  16.4 0.5 %collective-permute-start.6 = (f32[16,128]{1,0:T(8,128)S(1)}, f32[16,128]{1,0:T(8,128)S(1)}, u32[]{:S(2)}, u32[]{:S(2)}) collective-permute-start(f32[16,128]{1,0:T(8,128)S(1)} %get-tuple-element.92), channel_id=1, source_target_pairs={{0,1},{1,0},{2,3},{3,2},{4,5},{5,4},{6,7},{7,6},{8,9},{9,8},{10,11... | collective-permute-start | bytes 24584 | tf_op jit(solution)/shard_map/ppermute | solution.py:448
  17.0 0.0 copy-done
  17.0 0.1 shard_map.115._
  17.1 1.5 %collective-permute-start.4 = (f32[192,128]{1,0:T(8,128)S(1)}, f32[192,128]{1,0:T(8,128)S(1)}, u32[]{:S(2)}, u32[]{:S(2)}) collective-permute-start(f32[192,128]{1,0:T(8,128)S(1)} %shard_map.115._), channel_id=1, source_target_pairs={{0,1},{1,0},{2,3},{3,2},{4,5},{5,4},{6,7},{7,6},{8,9},{9,8},{10,11... | collective-permute-start | bytes 294920 | tf_op jit(solution)/shard_map/ppermute | solution.py:450
  18.6 1.1 %shard_map.117.pw_ref = f32[2592,128]{1,0:T(8,128)S(1)} custom-call(f32[1296]{0:T(1024)S(1)} %get-tuple-element.79.prof_ref, f32[4,128]{1,0:T(4,128)S(1)} %get-tuple-element.83.wind_ref, f32[192,128]{1,0:T(8,128)S(1)} %shard_map.115._), custom_call_target="tpu_custom_call" | custom-call | bytes 4500000 | tf_op jit(solution)/shard_map/pallas_call | solution.py:451
  19.8 0.4 %collective-permute-done.6.rest_8_ = f32[16,128]{1,0:T(8,128)S(1)} collective-permute-done((f32[16,128]{1,0:T(8,128)S(1)}, f32[16,128]{1,0:T(8,128)S(1)}, u32[]{:S(2)}, u32[]{:S(2)}) %collective-permute-start.6) | collective-permute-done | bytes 8224 | tf_op jit(solution)/shard_map/ppermute | solution.py:448
  20.2 1.6 %collective-permute-start.7 = (f32[8,128]{1,0:T(8,128)S(1)}, f32[8,128]{1,0:T(8,128)S(1)}, u32[]{:S(2)}, u32[]{:S(2)}) collective-permute-start(f32[8,128]{1,0:T(8,128)S(1)} %slice_add_fusion._), channel_id=1, source_target_pairs={{0,32},{32,0},{64,96},{96,64},{128,160},{160,128},{192,224},{224,1... | collective-permute-start | bytes 12296 | tf_op jit(solution)/shard_map/ppermute | solution.py:435
  21.8 0.3 collective-permute-done.4.fix_ref
  22.2 1.7 %shard_map.118 = (f32[3168,128]{1,0:T(8,128)S(1)}, f32[3168,128]{1,0:T(8,128)S(1)}, f32[3168,128]{1,0:T(8,128)S(1)}) custom-call(f32[1296]{0:T(1024)S(1)} %get-tuple-element.96.coef_ref, f32[8,128]{1,0:T(8,128)S(1)} %slice_add_fusion._), custom_call_target="tpu_custom_call" | custom-call | bytes 4500000 | tf_op jit(solution)/shard_map/pallas_call | solution.py:456
  23.8 0.0 collective-permute-done.7
  23.9 3.7 %collective-permute-start.8 = (f32[16,128]{1,0:T(8,128)S(1)}, f32[16,128]{1,0:T(8,128)S(1)}, u32[]{:S(2)}, u32[]{:S(2)}) collective-permute-start(f32[16,128]{1,0:T(8,128)S(1)} %constant_dynamic-update-slice_fusion), channel_id=1, source_target_pairs={{0,64},{32,96},{64,0},{96,32},{128,192},{160,224},{192,128},{224,1... | collective-permute-start | bytes 24584 | tf_op jit(solution)/shard_map/ppermute | solution.py:435
  27.6 0.3 shard_map.119.m_ref
  27.9 3.2 %shard_map.120 = (f32[792,4,128]{2,1,0:T(4,128)S(1)}, f32[792,4,128]{2,1,0:T(4,128)S(1)}, f32[792,4,128]{2,1,0:T(4,128)S(1)}, f32[792,4,128]{2,1,0:T(4,128)S(1)}...) custom-call(s32[1296]{0:T(1024)S(1)} %get-tuple-element.145.up_ref, ...), custom_call_target="tpu_custom_call", output_to_operand_aliasing={{0}: (4, {}), {1}: (5, {}), {2}: (6, {}), {3}: (7, {}), {4}... | custom-call | bytes 9000000 | tf_op jit(solution)/shard_map/pallas_call | solution.py:473
  31.1 0.0 collective-permute-done.8
  31.1 3.0 %collective-permute-start.9 = (f32[32,128]{1,0:T(8,128)S(1)}, f32[32,128]{1,0:T(8,128)S(1)}, u32[]{:S(2)}, u32[]{:S(2)}) collective-permute-start(f32[32,128]{1,0:T(8,128)S(1)} %constant_dynamic-update-slice_fusion.2), channel_id=1, source_target_pairs={{0,128},{32,160},{64,192},{96,224},{128,0},{160,32},{192,64},{224,... | collective-permute-start | bytes 49160 | tf_op jit(solution)/shard_map/ppermute | solution.py:435
  34.1 1.9 %shard_map.121 = (f32[792,4,128]{2,1,0:T(4,128)S(1)}, f32[792,4,128]{2,1,0:T(4,128)S(1)}, f32[792,4,128]{2,1,0:T(4,128)S(1)}, f32[792,4,128]{2,1,0:T(4,128)S(1)}...) custom-call(s32[1296]{0:T(1024)S(1)} %get-tuple-element.145.up_ref, ...), custom_call_target="tpu_custom_call", output_to_operand_aliasing={{0}: (4, {}), {1}: (5, {}), {2}: (6, {}), {3}: (7, {}), {4}... | custom-call | bytes 9000000 | tf_op jit(solution)/shard_map/pallas_call | solution.py:473
  36.1 1.6 %shard_map.122 = f32[2592,128]{1,0:T(8,128)} custom-call(f32[3168,128]{1,0:T(8,128)S(1)} %shard_map.119.m_ref, f32[2592,128]{1,0:T(8,128)S(1)} %shard_map.117.pw_ref, f32[3168,128]{1,0:T(8,128)S(1)} %bitcast.21, f32[3168,128]{1,0:T(8,128)S(1)} %bitcast.23, f32[3168,128]{1,0:T(8,128)S(1)} %bitcast.25, f32[3168,128]{1,0:T(8,128)S(1)} %bitcast.27, ...), custom_call_target="tpu_custom_call" | custom-call | bytes 6000000 | tf_op jit(solution)/shard_map/pallas_call | solution.py:480
  37.7 0.0 collective-permute-done.9
  37.7 0.9 %shard_map.123 = f32[2,2048]{1,0:T(2,128)} custom-call(f32[64,128]{1,0:T(8,128)S(1)} %pad_maximum_fusion.r_ref), custom_call_target="tpu_custom_call" | custom-call | bytes 3000000 | tf_op jit(solution)/shard_map/pallas_call | solution.py:489
  (7 shorter events, 0.1 us)
Async XLA Ops:
  2.5 12.7 %collective-permute-start.5 = (f32[576,128]{1,0:T(8,128)S(1)}, f32[576,128]{1,0:T(8,128)S(1)}, u32[]{:S(2)}, u32[]{:S(2)}) collective-permute-start(f32[576,128]{1,0:T(8,128)S(1)} %get-tuple-element.88), channel_id=1, source_target_pairs={{0,1},{1,0},{2,3},{3,2},{4,5},{5,4},{6,7},{7,6},{8,9},{9,8},{10,11... | collective-permute-start | bytes 884744 | tf_op jit(solution)/shard_map/ppermute | solution.py:426
  4.1 11.1 %collective-permute-start = (f32[324,128]{1,0:T(8,128)S(1)}, f32[324,128]{1,0:T(8,128)S(1)}, u32[]{:S(2)}, u32[]{:S(2)}) collective-permute-start(f32[324,128]{1,0:T(8,128)S(1)} %get-tuple-element.73), channel_id=1, source_target_pairs={{32,64},{96,128},{160,192},{64,32},{128,96},{192,160},{33,65},{97,... | collective-permute-start | bytes 497672 | tf_op jit(solution)/shard_map/ppermute | solution.py:424
  7.5 7.7 %collective-permute-start.1 = (f32[324,128]{1,0:T(8,128)S(1)}, f32[324,128]{1,0:T(8,128)S(1)}, u32[]{:S(2)}, u32[]{:S(2)}) collective-permute-start(f32[324,128]{1,0:T(8,128)S(1)} %get-tuple-element.74), channel_id=1, source_target_pairs={{0,32},{64,96},{128,160},{192,224},{32,0},{96,64},{160,128},{224,1... | collective-permute-start | bytes 497672 | tf_op jit(solution)/shard_map/ppermute | solution.py:425
  7.6 7.5 %collective-permute-start.2 = (f32[8,384]{1,0:T(8,128)S(1)}, f32[8,384]{1,0:T(8,128)S(1)}, u32[]{:S(2)}, u32[]{:S(2)}) collective-permute-start(f32[8,384]{1,0:T(8,128)S(1)} %get-tuple-element.75), channel_id=1, source_target_pairs={{2,4},{6,8},{10,12},{14,16},{18,20},{22,24},{26,28},{30,0},{4,2},{... | collective-permute-start | bytes 36872 | tf_op jit(solution)/shard_map/ppermute | solution.py:427
  12.5 2.7 %collective-permute-start.3 = (f32[8,384]{1,0:T(8,128)S(1)}, f32[8,384]{1,0:T(8,128)S(1)}, u32[]{:S(2)}, u32[]{:S(2)}) collective-permute-start(f32[8,384]{1,0:T(8,128)S(1)} %get-tuple-element.76), channel_id=1, source_target_pairs={{0,2},{4,6},{8,10},{12,14},{16,18},{20,22},{24,26},{28,30},{2,0},{... | collective-permute-start | bytes 36872 | tf_op jit(solution)/shard_map/ppermute | solution.py:428
  15.2 1.8 %copy-start = (s32[2,1296]{1,0:T(2,128)S(1)}, s32[2,1296]{1,0:T(2,128)}, u32[]{:S(2)}) copy-start(s32[2,1296]{1,0:T(2,128)} %param.18) | copy-start | bytes 31108
  16.4 3.7 %collective-permute-start.6 = (f32[16,128]{1,0:T(8,128)S(1)}, f32[16,128]{1,0:T(8,128)S(1)}, u32[]{:S(2)}, u32[]{:S(2)}) collective-permute-start(f32[16,128]{1,0:T(8,128)S(1)} %get-tuple-element.92), channel_id=1, source_target_pairs={{0,1},{1,0},{2,3},{3,2},{4,5},{5,4},{6,7},{7,6},{8,9},{9,8},{10,11... | collective-permute-start | bytes 24584 | tf_op jit(solution)/shard_map/ppermute | solution.py:448
  17.1 5.1 %collective-permute-start.4 = (f32[192,128]{1,0:T(8,128)S(1)}, f32[192,128]{1,0:T(8,128)S(1)}, u32[]{:S(2)}, u32[]{:S(2)}) collective-permute-start(f32[192,128]{1,0:T(8,128)S(1)} %shard_map.115._), channel_id=1, source_target_pairs={{0,1},{1,0},{2,3},{3,2},{4,5},{5,4},{6,7},{7,6},{8,9},{9,8},{10,11... | collective-permute-start | bytes 294920 | tf_op jit(solution)/shard_map/ppermute | solution.py:450
  20.2 3.6 %collective-permute-start.7 = (f32[8,128]{1,0:T(8,128)S(1)}, f32[8,128]{1,0:T(8,128)S(1)}, u32[]{:S(2)}, u32[]{:S(2)}) collective-permute-start(f32[8,128]{1,0:T(8,128)S(1)} %slice_add_fusion._), channel_id=1, source_target_pairs={{0,32},{32,0},{64,96},{96,64},{128,160},{160,128},{192,224},{224,1... | collective-permute-start | bytes 12296 | tf_op jit(solution)/shard_map/ppermute | solution.py:435
  23.9 7.2 %collective-permute-start.8 = (f32[16,128]{1,0:T(8,128)S(1)}, f32[16,128]{1,0:T(8,128)S(1)}, u32[]{:S(2)}, u32[]{:S(2)}) collective-permute-start(f32[16,128]{1,0:T(8,128)S(1)} %constant_dynamic-update-slice_fusion), channel_id=1, source_target_pairs={{0,64},{32,96},{64,0},{96,32},{128,192},{160,224},{192,128},{224,1... | collective-permute-start | bytes 24584 | tf_op jit(solution)/shard_map/ppermute | solution.py:435
  31.1 6.6 %collective-permute-start.9 = (f32[32,128]{1,0:T(8,128)S(1)}, f32[32,128]{1,0:T(8,128)S(1)}, u32[]{:S(2)}, u32[]{:S(2)}) collective-permute-start(f32[32,128]{1,0:T(8,128)S(1)} %constant_dynamic-update-slice_fusion.2), channel_id=1, source_target_pairs={{0,128},{32,160},{64,192},{96,224},{128,0},{160,32},{192,64},{224,... | collective-permute-start | bytes 49160 | tf_op jit(solution)/shard_map/ppermute | solution.py:435

commit v5 on v4

--- a/solution.py
+++ b/solution.py
@@ -113,7 +113,7 @@
     low = tile_iota(0) < 4
     mask8 = twice(mask_ref[...].astype(F32))
     for f in range(4):
-        speed_ref[f * 8 : f * 8 + 8, :] = jnp.full((8, 128), gs_ref[(1 - freq) * 14 + f])
+        speed_ref[f * 2 : f * 2 + 2, :] = jnp.full((2, 128), gs_ref[(1 - freq) * 14 + f])
 
     def one_freq(f, _):
         speed = gs_ref[f] * mask8
@@ -162,7 +162,7 @@
 
 
 BORDER_HALO = 4 * 18
-FIX_ROWS = 2 * BORDER_HALO + 6 * 8
+FIX_ROWS = 2 * BORDER_HALO + 3 * 8
 
 
 def fix_kernel(far_ref, near_ref, across_ref, inside_ref, speed_ref, fix_ref):
@@ -175,7 +175,7 @@
         at = 2 * BORDER_HALO + 8 * i
         fix_ref[at : at + 8, :] = jnp.where(lower, pltpu.roll(ref[:, 256:384], 108, 1), ref[:, 0:128])
     at = 2 * BORDER_HALO + 16
-    fix_ref[at : at + 32, :] = speed_ref[...]
+    fix_ref[at : at + 8, :] = speed_ref[...]
 
 
 def neighbours(x, h, hw, he, k, f, places):
@@ -278,7 +278,7 @@
     hw, he = jnp.where(odd_lon, inside, across), jnp.where(odd_lon, across, inside)
     to = pl.multiple_of((1 - freq) * ROWS, 8)
     for f in range(4):
-        speed = fix_ref[at + 16 + f * 8 : at + 24 + f * 8, :] * mask8
+        speed = jnp.broadcast_to(fix_ref[at + 16 + f * 2 : at + 17 + f * 2, :], (8, 128)) * mask8
         for k in range(TILES):
             here = f * 144 + k * 8
             x = raw_ref[here : here + 8, :]
@@ -434,7 +434,7 @@
     def gather(rows, bit):
         return lax.ppermute(rows, "lat", [(i, i ^ bit) for i in range(nlat)])
 
-    cx, cy, w0, w1, speed = call(table_kernel, (grid,) * 4 + (in_vmem((32, 128)),), [SM] * 3 + [VM], us=2.5)(
+    cx, cy, w0, w1, speed = call(table_kernel, (grid,) * 4 + (in_vmem((8, 128)),), [SM] * 3 + [VM], us=2.5)(
         group_speed, momentum, wind_profile, sea_mask
     )
     raw, w1 = lax.optimization_barrier((raw, w1))

time: 39.1 us -> 39 us (level)
  transfers between devices with their start and end apart: 10 -> 10, of which waited for: 2 -> 3; matrix products, arithmetic and copies ran while one was open for 0% -> 0% of each run, Pallas kernels for 33% -> 33%
where the time goes in v5:
time: 39 us; the launch traced here: 38.4 us
  starting transfers between devices  20.2 us (52%)
  Pallas kernels  16.5 us (42%)
  between operations  0.8 us (2%)
  waiting for transfers between devices  0.73 us (2%)
    ppermute x3, starting transfers between devices, gather(): return lax.ppermute(rows, 'lat', [(i, i ^ bit) for i in range(nlat)])  8.18 us
    pallas_call x2, Pallas kernels, local(): call(functools.partial(interact_kernel, first, stop), (acc,) * (SUMS + 1)...  5.15 us
    ppermute x1, starting transfers between devices, local(): across = lax.ppermute(across, 'lon', pairs(1, nlon // 2, nlon))  4.82 us
    ppermute x1, starting transfers between devices, local(): far = lax.ppermute(far, 'lat', pairs(1, nlat // 2 - 1, nlat))  3.47 us
    pallas_call x1, Pallas kernels, local(): call(table_kernel, (grid,) * 4 + (in_vmem((8, 128)),), [SM] * 3 + [VM], u...  2.69 us
    pallas_call x1, Pallas kernels, local(): call(pack_kernel, (grid, border, halo, halo, edge, edge) + (wide,) * EARL...  1.84 us
    pallas_call x1, Pallas kernels, local(): call(finish_kernel, jax.ShapeDtypeStruct((ROWS, 128), F32), [VM] * (6 + S...  1.67 us
    pallas_call x1, Pallas kernels, local(): call(half_kernel, (wide,) * (1 + SUMS - EARLY), [SM] + [VM], us=1.5)  1.66 us
  transfers between devices with their start and end apart: 10, of which 3 were waited for; matrix products, arithmetic and copies ran while one was open for 0% of the time, Pallas kernels for 33%

profile of v5, /device:TPU:8, one launch (start us, length us, event | category | flops | bytes accessed | tf_op | source)
XLA Modules:
  0.0 38.4 jit_solution(16902888874055206952)
XLA Ops:
  0.6 1.8 %shard_map.113 = (f32[2592,128]{1,0:T(8,128)S(1)}, f32[576,128]{1,0:T(8,128)S(1)}, f32[324,128]{1,0:T(8,128)S(1)}, f32[324,128]{1,0:T(8,128)S(1)}, f32[8,384]{1,...) custom-call(f32[2592,128]{1,0:T(8,128)} %bitcast.36, ...), custom_call_target="tpu_custom_call" | custom-call | bytes 3000000 | tf_op jit(solution)/shard_map/pallas_call | solution.py:409
  2.5 1.6 %collective-permute-start.5 = (f32[576,128]{1,0:T(8,128)S(1)}, f32[576,128]{1,0:T(8,128)S(1)}, u32[]{:S(2)}, u32[]{:S(2)}) collective-permute-start(f32[576,128]{1,0:T(8,128)S(1)} %get-tuple-element.88), channel_id=1, source_target_pairs={{0,1},{1,0},{2,3},{3,2},{4,5},{5,4},{6,7},{7,6},{8,9},{9,8},{10,11... | collective-permute-start | bytes 884744 | tf_op jit(solution)/shard_map/ppermute | solution.py:426
  4.1 3.5 %collective-permute-start = (f32[324,128]{1,0:T(8,128)S(1)}, f32[324,128]{1,0:T(8,128)S(1)}, u32[]{:S(2)}, u32[]{:S(2)}) collective-permute-start(f32[324,128]{1,0:T(8,128)S(1)} %get-tuple-element.73), channel_id=1, source_target_pairs={{32,64},{96,128},{160,192},{64,32},{128,96},{192,160},{33,65},{97,... | collective-permute-start | bytes 497672 | tf_op jit(solution)/shard_map/ppermute | solution.py:424
  7.5 0.1 collective-permute-start.1
  7.6 4.8 %collective-permute-start.2 = (f32[8,384]{1,0:T(8,128)S(1)}, f32[8,384]{1,0:T(8,128)S(1)}, u32[]{:S(2)}, u32[]{:S(2)}) collective-permute-start(f32[8,384]{1,0:T(8,128)S(1)} %get-tuple-element.75), channel_id=1, source_target_pairs={{2,4},{6,8},{10,12},{14,16},{18,20},{22,24},{26,28},{30,0},{4,2},{... | collective-permute-start | bytes 36872 | tf_op jit(solution)/shard_map/ppermute | solution.py:427
  12.5 0.0 collective-permute-start.3
  12.5 2.7 %shard_map.114 = (f32[2592,128]{1,0:T(8,128)S(1)}, f32[2592,128]{1,0:T(8,128)S(1)}, f32[2592,128]{1,0:T(8,128)S(1)}, f32[2592,128]{1,0:T(8,128)S(1)}, f32[8,128]{1,0:T(8,128)S(1)}) custom-call(f32[18]{0:T(128)S(1)} %get-tuple-element.77.gs_ref, f32[2,1296]{1,0:T(2,128)S(1)} %get-tuple-element.78.mom_ref, f32[1296]{0:T(1024)S(1)} %get-tuple-element.79.prof_ref, ...), custom_call_target="tpu_custom_call" | custom-call | bytes 7500000 | tf_op jit(solution)/shard_map/pallas_call | solution.py:437
  15.2 0.0 collective-permute-done.5.raw_ref
  15.2 0.0 collective-permute-done.2.across_ref
  15.2 0.0 collective-permute-done.3.inside_ref
  15.2 0.0 collective-permute-done.far_ref
  15.2 0.0 collective-permute-done.1.near_ref
  15.2 0.0 copy-start
  15.2 1.2 %shard_map.116 = (f32[3168,128]{1,0:T(8,128)S(1)}, f32[16,128]{1,0:T(8,128)S(1)}, f32[16,128]{1,0:T(8,128)S(1)}) custom-call(f32[2592,128]{1,0:T(8,128)S(1)} %get-tuple-element.82.e_ref, f32[324,128]{1,0:T(8,128)S(1)} %collective-permute-done.far_ref, f32[324,128]{1,0:T(8,128)S(1)} %collective-permute-done.1.near_ref, ...), custom_call_target="tpu_custom_call" | custom-call | bytes 4500000 | tf_op jit(solution)/shard_map/pallas_call | solution.py:441
  16.4 0.5 %collective-permute-start.6 = (f32[16,128]{1,0:T(8,128)S(1)}, f32[16,128]{1,0:T(8,128)S(1)}, u32[]{:S(2)}, u32[]{:S(2)}) collective-permute-start(f32[16,128]{1,0:T(8,128)S(1)} %get-tuple-element.92), channel_id=1, source_target_pairs={{0,1},{1,0},{2,3},{3,2},{4,5},{5,4},{6,7},{7,6},{8,9},{9,8},{10,11... | collective-permute-start | bytes 24584 | tf_op jit(solution)/shard_map/ppermute | solution.py:448
  17.0 0.0 copy-done
  17.0 0.1 shard_map.115._
  17.1 1.5 %collective-permute-start.4 = (f32[168,128]{1,0:T(8,128)S(1)}, f32[168,128]{1,0:T(8,128)S(1)}, u32[]{:S(2)}, u32[]{:S(2)}) collective-permute-start(f32[168,128]{1,0:T(8,128)S(1)} %shard_map.115._), channel_id=1, source_target_pairs={{0,1},{1,0},{2,3},{3,2},{4,5},{5,4},{6,7},{7,6},{8,9},{9,8},{10,11... | collective-permute-start | bytes 258056 | tf_op jit(solution)/shard_map/ppermute | solution.py:450
  18.6 1.1 %shard_map.117.pw_ref = f32[2592,128]{1,0:T(8,128)S(1)} custom-call(f32[1296]{0:T(1024)S(1)} %get-tuple-element.79.prof_ref, f32[4,128]{1,0:T(4,128)S(1)} %get-tuple-element.83.wind_ref, f32[168,128]{1,0:T(8,128)S(1)} %shard_map.115._), custom_call_target="tpu_custom_call" | custom-call | bytes 4500000 | tf_op jit(solution)/shard_map/pallas_call | solution.py:451
  19.8 0.4 %collective-permute-done.6.rest_8_ = f32[16,128]{1,0:T(8,128)S(1)} collective-permute-done((f32[16,128]{1,0:T(8,128)S(1)}, f32[16,128]{1,0:T(8,128)S(1)}, u32[]{:S(2)}, u32[]{:S(2)}) %collective-permute-start.6) | collective-permute-done | bytes 8224 | tf_op jit(solution)/shard_map/ppermute | solution.py:448
  20.2 1.6 %collective-permute-start.7 = (f32[8,128]{1,0:T(8,128)S(1)}, f32[8,128]{1,0:T(8,128)S(1)}, u32[]{:S(2)}, u32[]{:S(2)}) collective-permute-start(f32[8,128]{1,0:T(8,128)S(1)} %slice_add_fusion._), channel_id=1, source_target_pairs={{0,32},{32,0},{64,96},{96,64},{128,160},{160,128},{192,224},{224,1... | collective-permute-start | bytes 12296 | tf_op jit(solution)/shard_map/ppermute | solution.py:435
  21.8 0.1 collective-permute-done.4.fix_ref
  21.9 1.7 %shard_map.118 = (f32[3168,128]{1,0:T(8,128)S(1)}, f32[3168,128]{1,0:T(8,128)S(1)}, f32[3168,128]{1,0:T(8,128)S(1)}) custom-call(f32[1296]{0:T(1024)S(1)} %get-tuple-element.96.coef_ref, f32[8,128]{1,0:T(8,128)S(1)} %slice_add_fusion._), custom_call_target="tpu_custom_call" | custom-call | bytes 4500000 | tf_op jit(solution)/shard_map/pallas_call | solution.py:456
  23.6 0.2 collective-permute-done.7
  23.8 3.8 %collective-permute-start.8 = (f32[16,128]{1,0:T(8,128)S(1)}, f32[16,128]{1,0:T(8,128)S(1)}, u32[]{:S(2)}, u32[]{:S(2)}) collective-permute-start(f32[16,128]{1,0:T(8,128)S(1)} %constant_dynamic-update-slice_fusion), channel_id=1, source_target_pairs={{0,64},{32,96},{64,0},{96,32},{128,192},{160,224},{192,128},{224,1... | collective-permute-start | bytes 24584 | tf_op jit(solution)/shard_map/ppermute | solution.py:435
  27.6 0.3 shard_map.119.m_ref
  27.8 3.2 %shard_map.120 = (f32[792,4,128]{2,1,0:T(4,128)S(1)}, f32[792,4,128]{2,1,0:T(4,128)S(1)}, f32[792,4,128]{2,1,0:T(4,128)S(1)}, f32[792,4,128]{2,1,0:T(4,128)S(1)}...) custom-call(s32[1296]{0:T(1024)S(1)} %get-tuple-element.145.up_ref, ...), custom_call_target="tpu_custom_call", output_to_operand_aliasing={{0}: (4, {}), {1}: (5, {}), {2}: (6, {}), {3}: (7, {}), {4}... | custom-call | bytes 9000000 | tf_op jit(solution)/shard_map/pallas_call | solution.py:473
  31.0 0.0 collective-permute-done.8
  31.1 2.8 %collective-permute-start.9 = (f32[32,128]{1,0:T(8,128)S(1)}, f32[32,128]{1,0:T(8,128)S(1)}, u32[]{:S(2)}, u32[]{:S(2)}) collective-permute-start(f32[32,128]{1,0:T(8,128)S(1)} %constant_dynamic-update-slice_fusion.2), channel_id=1, source_target_pairs={{0,128},{32,160},{64,192},{96,224},{128,0},{160,32},{192,64},{224,... | collective-permute-start | bytes 49160 | tf_op jit(solution)/shard_map/ppermute | solution.py:435
  33.8 1.9 %shard_map.121 = (f32[792,4,128]{2,1,0:T(4,128)S(1)}, f32[792,4,128]{2,1,0:T(4,128)S(1)}, f32[792,4,128]{2,1,0:T(4,128)S(1)}, f32[792,4,128]{2,1,0:T(4,128)S(1)}...) custom-call(s32[1296]{0:T(1024)S(1)} %get-tuple-element.145.up_ref, ...), custom_call_target="tpu_custom_call", output_to_operand_aliasing={{0}: (4, {}), {1}: (5, {}), {2}: (6, {}), {3}: (7, {}), {4}... | custom-call | bytes 9000000 | tf_op jit(solution)/shard_map/pallas_call | solution.py:473
  35.8 1.7 %shard_map.122 = f32[2592,128]{1,0:T(8,128)} custom-call(f32[3168,128]{1,0:T(8,128)S(1)} %shard_map.119.m_ref, f32[2592,128]{1,0:T(8,128)S(1)} %shard_map.117.pw_ref, f32[3168,128]{1,0:T(8,128)S(1)} %bitcast.21, f32[3168,128]{1,0:T(8,128)S(1)} %bitcast.23, f32[3168,128]{1,0:T(8,128)S(1)} %bitcast.25, f32[3168,128]{1,0:T(8,128)S(1)} %bitcast.27, ...), custom_call_target="tpu_custom_call" | custom-call | bytes 6000000 | tf_op jit(solution)/shard_map/pallas_call | solution.py:480
  37.5 0.0 collective-permute-done.9
  37.5 0.9 %shard_map.123 = f32[2,2048]{1,0:T(2,128)} custom-call(f32[64,128]{1,0:T(8,128)S(1)} %pad_maximum_fusion.r_ref), custom_call_target="tpu_custom_call" | custom-call | bytes 3000000 | tf_op jit(solution)/shard_map/pallas_call | solution.py:489
  (7 shorter events, 0.1 us)
Async XLA Ops:
  2.5 12.7 %collective-permute-start.5 = (f32[576,128]{1,0:T(8,128)S(1)}, f32[576,128]{1,0:T(8,128)S(1)}, u32[]{:S(2)}, u32[]{:S(2)}) collective-permute-start(f32[576,128]{1,0:T(8,128)S(1)} %get-tuple-element.88), channel_id=1, source_target_pairs={{0,1},{1,0},{2,3},{3,2},{4,5},{5,4},{6,7},{7,6},{8,9},{9,8},{10,11... | collective-permute-start | bytes 884744 | tf_op jit(solution)/shard_map/ppermute | solution.py:426
  4.1 11.1 %collective-permute-start = (f32[324,128]{1,0:T(8,128)S(1)}, f32[324,128]{1,0:T(8,128)S(1)}, u32[]{:S(2)}, u32[]{:S(2)}) collective-permute-start(f32[324,128]{1,0:T(8,128)S(1)} %get-tuple-element.73), channel_id=1, source_target_pairs={{32,64},{96,128},{160,192},{64,32},{128,96},{192,160},{33,65},{97,... | collective-permute-start | bytes 497672 | tf_op jit(solution)/shard_map/ppermute | solution.py:424
  7.5 7.7 %collective-permute-start.1 = (f32[324,128]{1,0:T(8,128)S(1)}, f32[324,128]{1,0:T(8,128)S(1)}, u32[]{:S(2)}, u32[]{:S(2)}) collective-permute-start(f32[324,128]{1,0:T(8,128)S(1)} %get-tuple-element.74), channel_id=1, source_target_pairs={{0,32},{64,96},{128,160},{192,224},{32,0},{96,64},{160,128},{224,1... | collective-permute-start | bytes 497672 | tf_op jit(solution)/shard_map/ppermute | solution.py:425
  7.6 7.5 %collective-permute-start.2 = (f32[8,384]{1,0:T(8,128)S(1)}, f32[8,384]{1,0:T(8,128)S(1)}, u32[]{:S(2)}, u32[]{:S(2)}) collective-permute-start(f32[8,384]{1,0:T(8,128)S(1)} %get-tuple-element.75), channel_id=1, source_target_pairs={{2,4},{6,8},{10,12},{14,16},{18,20},{22,24},{26,28},{30,0},{4,2},{... | collective-permute-start | bytes 36872 | tf_op jit(solution)/shard_map/ppermute | solution.py:427
  12.5 2.7 %collective-permute-start.3 = (f32[8,384]{1,0:T(8,128)S(1)}, f32[8,384]{1,0:T(8,128)S(1)}, u32[]{:S(2)}, u32[]{:S(2)}) collective-permute-start(f32[8,384]{1,0:T(8,128)S(1)} %get-tuple-element.76), channel_id=1, source_target_pairs={{0,2},{4,6},{8,10},{12,14},{16,18},{20,22},{24,26},{28,30},{2,0},{... | collective-permute-start | bytes 36872 | tf_op jit(solution)/shard_map/ppermute | solution.py:428
  15.2 1.8 %copy-start = (s32[2,1296]{1,0:T(2,128)S(1)}, s32[2,1296]{1,0:T(2,128)}, u32[]{:S(2)}) copy-start(s32[2,1296]{1,0:T(2,128)} %param.18) | copy-start | bytes 31108
  16.4 3.7 %collective-permute-start.6 = (f32[16,128]{1,0:T(8,128)S(1)}, f32[16,128]{1,0:T(8,128)S(1)}, u32[]{:S(2)}, u32[]{:S(2)}) collective-permute-start(f32[16,128]{1,0:T(8,128)S(1)} %get-tuple-element.92), channel_id=1, source_target_pairs={{0,1},{1,0},{2,3},{3,2},{4,5},{5,4},{6,7},{7,6},{8,9},{9,8},{10,11... | collective-permute-start | bytes 24584 | tf_op jit(solution)/shard_map/ppermute | solution.py:448
  17.1 4.8 %collective-permute-start.4 = (f32[168,128]{1,0:T(8,128)S(1)}, f32[168,128]{1,0:T(8,128)S(1)}, u32[]{:S(2)}, u32[]{:S(2)}) collective-permute-start(f32[168,128]{1,0:T(8,128)S(1)} %shard_map.115._), channel_id=1, source_target_pairs={{0,1},{1,0},{2,3},{3,2},{4,5},{5,4},{6,7},{7,6},{8,9},{9,8},{10,11... | collective-permute-start | bytes 258056 | tf_op jit(solution)/shard_map/ppermute | solution.py:450
  20.2 3.6 %collective-permute-start.7 = (f32[8,128]{1,0:T(8,128)S(1)}, f32[8,128]{1,0:T(8,128)S(1)}, u32[]{:S(2)}, u32[]{:S(2)}) collective-permute-start(f32[8,128]{1,0:T(8,128)S(1)} %slice_add_fusion._), channel_id=1, source_target_pairs={{0,32},{32,0},{64,96},{96,64},{128,160},{160,128},{192,224},{224,1... | collective-permute-start | bytes 12296 | tf_op jit(solution)/shard_map/ppermute | solution.py:435
  23.8 7.2 %collective-permute-start.8 = (f32[16,128]{1,0:T(8,128)S(1)}, f32[16,128]{1,0:T(8,128)S(1)}, u32[]{:S(2)}, u32[]{:S(2)}) collective-permute-start(f32[16,128]{1,0:T(8,128)S(1)} %constant_dynamic-update-slice_fusion), channel_id=1, source_target_pairs={{0,64},{32,96},{64,0},{96,32},{128,192},{160,224},{192,128},{224,1... | collective-permute-start | bytes 24584 | tf_op jit(solution)/shard_map/ppermute | solution.py:435
  31.1 6.4 %collective-permute-start.9 = (f32[32,128]{1,0:T(8,128)S(1)}, f32[32,128]{1,0:T(8,128)S(1)}, u32[]{:S(2)}, u32[]{:S(2)}) collective-permute-start(f32[32,128]{1,0:T(8,128)S(1)} %constant_dynamic-update-slice_fusion.2), channel_id=1, source_target_pairs={{0,128},{32,160},{64,192},{96,224},{128,0},{160,32},{192,64},{224,... | collective-permute-start | bytes 49160 | tf_op jit(solution)/shard_map/ppermute | solution.py:435
